TPU v7x, 32 devices: a whole 2x2x4 slice. The times are simulated.
32 devices in a mesh: dp: 8 (over z, x), tensor: 4 (over y, core).
Axes of the slice: x: 2, y: 2, z: 4, core: 2. Of those that a mesh axis runs over, the one named last changes fastest.
Arguments:
- tokens: bfloat16 [1024, 4096], P(('dp', 'tensor')), may hold values from -6 to 6
- cotangent: bfloat16 [1024, 4096], P(('dp', 'tensor')), may hold values from -6 to 6
- up_blocks: bfloat16 [8, 4, 32, 128, 128], P('dp', 'tensor'), may hold values from -0.25 to 0.25
- up_place: int32 [8, 4, 32], P('dp', 'tensor'), may hold values from -1 to 1023, as said below
- down_blocks: bfloat16 [8, 4, 32, 128, 128], P('dp', 'tensor'), may hold values from -0.125 to 0.125
- down_place: int32 [8, 4, 32], P('dp', 'tensor'), may hold values from -1 to 1023, as said below
Outputs:
- outputs: bfloat16 [1024, 4096], P(('dp', 'tensor'))
- input_grads: bfloat16 [1024, 4096], P(('dp', 'tensor'))
- up_grads: float32 [8, 4, 16, 128, 128], P('dp', 'tensor')
- down_grads: float32 [8, 4, 16, 128, 128], P('dp', 'tensor')
Inputs may be any that keep to these rules, and one draw needn't show every extreme that they name: `up_place`: A code q = r * 32 + c names the up projection block at block r of the model width and block c of the tensor index's 32 hidden blocks; -1 marks an empty slot. On each device the live slots come first; the live codes of one tensor index are distinct and number exactly 128 over its devices; every tensor index has a device with 32 live slots and one with none. `down_place`: the same for the down projection: q = r * 32 + c names the block from hidden block c of the tensor index to block r of the model width; -1 marks an empty slot. Live slots come first on each device, live codes of one tensor index are distinct and number exactly 128, and every tensor index has a device with 32 live slots and one with none.
All inputs are finite; a program needn't handle non-finite values.
Results may differ from a plain program's by a relative error of at most 0.0095.
Values may be sent and summed in bfloat16 or wider, within the bound.
No kernel may reach another device: no remote copies, remote signals or barrier semaphores. Data moves between devices by JAX's collectives and lax.ppermute only.
A program may use at most 128 MiB of HBM per device.

v0:
```python
import math

import jax
import jax.numpy as jnp
from jax import lax
from jax.sharding import PartitionSpec as P

FF = 16384
BLK = 128


gelu_root = 0.7978845608028654
gelu_cubic = 0.044715


def from_behind(array, axis, by):
    devices = lax.axis_size(axis)
    return lax.ppermute(array, axis, [(i, (i + by) % devices) for i in range(devices)])


def gelu_value(values):
    return (
        0.5
        * values
        * (1.0 + jnp.tanh(gelu_root * (values + gelu_cubic * values * values * values)))
    )


def gelu_slope(values):
    inner_tanh = jnp.tanh(gelu_root * (values + gelu_cubic * values * values * values))
    return 0.5 * (1.0 + inner_tanh) + 0.5 * values * (1.0 - inner_tanh * inner_tanh) * gelu_root * (
        1.0 + 3.0 * gelu_cubic * values * values
    )


def split_codes(block_codes, group_blocks):
    is_live = block_codes >= 0
    safe_codes = jnp.where(is_live, block_codes, 0)
    return (safe_codes // group_blocks, safe_codes % group_blocks, is_live)


def pack_order(block_codes):
    is_live = (block_codes >= 0).astype(jnp.int32)
    live_rank = jnp.cumsum(is_live) - is_live
    live_total = block_codes.shape[0] // 2
    target = jnp.where(is_live > 0, live_rank, live_total)
    return jnp.zeros((live_total,), jnp.int32).at[target].set(block_codes, mode="drop")


def place_sum(products, block_index, is_live, bucket_count):
    target = jnp.where(is_live, block_index, bucket_count)
    start = jnp.zeros((products.shape[0], bucket_count, products.shape[2]), jnp.float32)
    return start.at[:, target].add(products, mode="drop")


def place_add(running, products, block_index, is_live):
    target = jnp.where(is_live, block_index, running.shape[1])
    return running.at[:, target].add(products, mode="drop")


def shards(tokens, cotangent, up_blocks, up_place, down_blocks, down_place):
    token_rows, cotan_rows = (
        lax.all_gather(tokens, "tensor", axis=0, tiled=True),
        lax.all_gather(cotangent, "tensor", axis=0, tiled=True),
    )
    row_count = token_rows.shape[0]
    model_width = token_rows.shape[1]
    model_blocks = model_width // BLK
    group_blocks = FF // BLK // lax.axis_size("tensor")
    devices_dp = lax.axis_size("dp")
    slot_count = up_place.shape[2]
    mean_slots = slot_count // 2
    token_cube = token_rows.reshape(row_count, model_blocks, BLK)
    cotan_cube = cotan_rows.reshape(row_count, model_blocks, BLK)
    up_all, down_all = (
        lax.all_gather(up_place, "dp", axis=0, tiled=True),
        lax.all_gather(down_place, "dp", axis=0, tiled=True),
    )
    up_codes = up_all.reshape(devices_dp * slot_count)
    down_codes = down_all.reshape(devices_dp * slot_count)
    up_list = pack_order(up_codes)
    down_list = pack_order(down_codes)
    my_place = lax.axis_index("dp")
    up_source = up_blocks.reshape(1, slot_count, BLK, BLK)
    down_source = down_blocks.reshape(1, slot_count, BLK, BLK)
    shard_piece = lax.all_gather(up_source, "dp", axis=0, tiled=True)
    pre_total = jnp.zeros((row_count, group_blocks, BLK), jnp.float32)
    piece_slots = shard_piece.shape[0] * shard_piece.shape[1]
    blocks = shard_piece.reshape(piece_slots, BLK, BLK)
    block_codes = up_codes
    block_rows, block_cols, is_live = split_codes(block_codes, group_blocks)
    products = jnp.einsum(
        "rsa,sab->rsb",
        jnp.take(token_cube, block_rows, axis=1),
        blocks,
        preferred_element_type=jnp.float32,
    )
    pre_total = place_add(pre_total, products, block_cols, is_live)
    kept_blocks = blocks
    up_kept = kept_blocks
    hidden = gelu_value(pre_total).astype(jnp.bfloat16)
    shard_piece = lax.all_gather(down_source, "dp", axis=0, tiled=True)
    out_total = jnp.zeros((row_count, model_blocks, BLK), jnp.float32)
    piece_slots = shard_piece.shape[0] * shard_piece.shape[1]
    blocks = shard_piece.reshape(piece_slots, BLK, BLK)
    block_codes = down_codes
    block_rows, block_cols, is_live = split_codes(block_codes, group_blocks)
    products = jnp.einsum(
        "rsa,sab->rsb",
        jnp.take(hidden, block_cols, axis=1),
        blocks,
        preferred_element_type=jnp.float32,
    )
    out_total = place_add(out_total, products, block_rows, is_live)
    kept_blocks = blocks
    outputs = lax.psum_scatter(
        out_total.reshape(row_count, model_width).astype(jnp.bfloat16),
        "tensor",
        scatter_dimension=0,
        tiled=True,
    )
    down_rows, down_cols, down_live = split_codes(down_codes, group_blocks)
    products = jnp.einsum(
        "rsb,sab->rsa",
        jnp.take(cotan_cube, down_rows, axis=1),
        kept_blocks,
        preferred_element_type=jnp.float32,
    )
    grad_hidden = place_sum(products, down_cols, down_live, group_blocks)
    grad_pre = (grad_hidden * gelu_slope(pre_total)).astype(jnp.bfloat16)
    up_rows, up_cols, up_live = split_codes(up_codes, group_blocks)
    products = jnp.einsum(
        "rsb,sab->rsa",
        jnp.take(grad_pre, up_cols, axis=1),
        up_kept,
        preferred_element_type=jnp.float32,
    )
    in_part = place_sum(products, up_rows, up_live, model_blocks)
    input_grads = lax.psum_scatter(
        in_part.reshape(row_count, model_width).astype(jnp.bfloat16),
        "tensor",
        scatter_dimension=0,
        tiled=True,
    )

    def contribution(owner_index):
        up_own = lax.dynamic_slice_in_dim(up_list, owner_index * mean_slots, mean_slots)
        down_own = lax.dynamic_slice_in_dim(down_list, owner_index * mean_slots, mean_slots)
        up_terms = jnp.einsum(
            "rsa,rsb->sab",
            jnp.take(token_cube, up_own // group_blocks, axis=1),
            jnp.take(grad_pre, up_own % group_blocks, axis=1),
            preferred_element_type=jnp.float32,
        )
        down_terms = jnp.einsum(
            "rsa,rsb->sab",
            jnp.take(hidden, down_own % group_blocks, axis=1),
            jnp.take(cotan_cube, down_own // group_blocks, axis=1),
            preferred_element_type=jnp.float32,
        )
        return jnp.stack([up_terms, down_terms])

    def rise_owner(turn_index):
        return (my_place - turn_index - 1) % devices_dp

    def turn_one(turn_index, running):
        return from_behind(running.astype(jnp.bfloat16), "dp", 1).astype(
            running.dtype
        ) + contribution(rise_owner(turn_index))

    block_grads = lax.fori_loop(1, devices_dp, turn_one, contribution(rise_owner(0)))
    grad_scale = 1.0 / math.sqrt(devices_dp * row_count)
    block_grads = block_grads * grad_scale
    up_grads = block_grads[0].reshape(1, 1, mean_slots, BLK, BLK)
    down_grads = block_grads[1].reshape(1, 1, mean_slots, BLK, BLK)
    return (outputs, input_grads, up_grads, down_grads)


def solution(mesh):
    return jax.shard_map(
        shards,
        mesh=mesh,
        in_specs=(
            P(("dp", "tensor"), None),
            P(("dp", "tensor"), None),
            P("dp", "tensor", None, None, None),
            P("dp", "tensor", None),
            P("dp", "tensor", None, None, None),
            P("dp", "tensor", None),
        ),
        out_specs=(
            P(("dp", "tensor"), None),
            P(("dp", "tensor"), None),
            P("dp", "tensor", None, None, None),
            P("dp", "tensor", None, None, None),
        ),
        check_vma=False,
    )
```

profile of v0, /device:TPU:0, one launch (start us, length us, event | category | flops | bytes accessed | tf_op | source)
XLA Modules:
  0.0 726.5 jit_solution(8489693114438113247)
XLA Ops:
  10.0 22.3 %all_gather.18 = s32[8,1,32]{2,1,0:T(1,128)S(1)} all-gather(s32[1,1,32]{2,1,0:T(1,128)} %param.17), channel_id=1, replica_groups=mesh['dp'=8,'tensor'=4] {'dp'}, dimensions={0}, use_global_device_ids=true | all-gather | bytes 1152 | tf_op jit(solution)/shard_map/all_gather | solution.py:77
  32.3 16.4 %all_gather.19 = s32[8,1,32]{2,1,0:T(1,128)S(1)} all-gather(s32[1,1,32]{2,1,0:T(1,128)} %param.15), channel_id=1, replica_groups=mesh['dp'=8,'tensor'=4] {'dp'}, dimensions={0}, use_global_device_ids=true | all-gather | bytes 1152 | tf_op jit(solution)/shard_map/all_gather | solution.py:76
  59.7 8.6 %gather_fusion.4 = bf16[256,128,128]{2,1,0:T(8,128)(2,1)} fusion(bf16[128,32,128]{2,0,1:T(8,128)(2,1)S(1)} %copy.48, s32[1024]{0:T(1024)S(1)} %get-tuple-element.379), kind=kCustom, calls=%fused_computation.clone | custom fusion | bytes 16778240 | tf_op jit(solution)/shard_map/jit(_take)/gather | solution.py:94
  68.3 8.5 %gather_fusion.6 = bf16[256,128,128]{2,1,0:T(8,128)(2,1)} fusion(bf16[128,32,128]{2,0,1:T(8,128)(2,1)S(1)} %copy.51, s32[1024]{0:T(1024)S(1)} %get-tuple-element.376), kind=kCustom, calls=%fused_computation.3.clone | custom fusion | bytes 16778240 | tf_op jit(solution)/shard_map/jit(_take)/gather | solution.py:125
  76.8 97.6 %all-gather.11.cloned.1.call-done = bf16[8,1,32,128,128]{4,3,2,1,0:T(8,128)(2,1)} async-done(((bf16[1,1,32,128,128]{4,3,2,1,0:T(8,128)(2,1)}), bf16[8,1,32,128,128]{4,3,2,1,0:T(8,128)(2,1)}) %all-gather.11.cloned.1.call-update) | async-done | bytes 8388624 | tf_op jit(solution)/shard_map/all_gather | solution.py:86
  174.4 14.2 %fusion.22 = f32[256,128,128]{2,1,0:T(8,128)} fusion(bf16[256,128,128]{2,1,0:T(8,128)(2,1)} %bitcast.82, bf16[256,128,128]{2,1,0:T(8,128)(2,1)} %gather_fusion.4, pred[256]{0:T(512)(128)(4,1)S(1)} %get-tuple-element.370), kind=kOutput, calls=%fused_computation.65 | convolution fusion | flops 1077936128 | bytes 33554688 | tf_op jit(solution)/shard_map/rsa,sab->rsb/dot_general | solution.py:92
  188.9 33.2 %scatter_fusion = f32[128,32,128]{2,0,1:T(8,128)S(1)} fusion(f32[128,32,128]{2,0,1:T(8,128)S(1)} %broadcast.525.clone.2, s32[256]{0:T(256)S(1)} %bitcast.95, f32[256,128,128]{2,1,0:T(8,128)} %fusion.22), kind=kCustom, calls=%fused_computation.12 | custom fusion | flops 4194304 | bytes 50332672 | tf_op jit(solution)/shard_map/scatter-add | solution.py:58
  222.1 77.5 %all-gather.13.cloned.1.call-done = bf16[8,1,32,128,128]{4,3,2,1,0:T(8,128)(2,1)} async-done(((bf16[1,1,32,128,128]{4,3,2,1,0:T(8,128)(2,1)}), bf16[8,1,32,128,128]{4,3,2,1,0:T(8,128)(2,1)}) %all-gather.13.cloned.1.call-update) | async-done | bytes 8388624 | tf_op jit(solution)/shard_map/all_gather | solution.py:102
  299.6 12.7 %fusion.18 = f32[256,128,128]{2,1,0:T(8,128)} fusion(bf16[256,128,128]{2,1,0:T(8,128)(2,1)} %bitcast.84, bf16[256,128,128]{2,1,0:T(8,128)(2,1)} %gather_fusion.6, pred[256]{0:T(512)(128)(4,1)S(1)} %get-tuple-element.350), kind=kOutput, calls=%fused_computation.61 | convolution fusion | flops 1077936128 | bytes 33554688 | tf_op jit(solution)/shard_map/rsb,sab->rsa/dot_general | solution.py:123
  313.8 49.1 %scatter_fusion.2 = f32[128,32,128]{2,0,1:T(8,128)} fusion(f32[128,32,128]{2,0,1:T(8,128)} %broadcast.525.clone.1, s32[256]{0:T(256)S(1)} %bitcast.94, f32[256,128,128]{2,1,0:T(8,128)} %fusion.18), kind=kCustom, calls=%fused_computation.14 | custom fusion | flops 4194304 | bytes 50332672 | tf_op jit(solution)/shard_map/scatter-add | solution.py:53
  362.9 4.4 fusion.42
  367.4 9.7 %gather_fusion.5 = bf16[256,128,128]{2,1,0:T(8,128)(2,1)} fusion(bf16[128,32,128]{2,0,1:T(8,128)(2,1)} %get-tuple-element.462, s32[1024]{0:T(1024)S(1)} %get-tuple-element.377), kind=kCustom, calls=%fused_computation.2.clone | custom fusion | bytes 16778240 | tf_op jit(solution)/shard_map/jit(_take)/gather | solution.py:110
  377.1 13.9 %fusion.20 = f32[256,128,128]{2,1,0:T(8,128)} fusion(bf16[256,128,128]{2,1,0:T(8,128)(2,1)} %bitcast.85, bf16[256,128,128]{2,1,0:T(8,128)(2,1)} %gather_fusion.5, pred[256]{0:T(512)(128)(4,1)S(1)} %get-tuple-element.372), kind=kOutput, calls=%fused_computation.63 | convolution fusion | flops 1077936128 | bytes 33554688 | tf_op jit(solution)/shard_map/rsa,sab->rsb/dot_general | solution.py:108
  391.2 33.1 %scatter_fusion.1 = f32[128,32,128]{2,0,1:T(8,128)S(1)} fusion(f32[128,32,128]{2,0,1:T(8,128)S(1)} %broadcast.525.clone, s32[256]{0:T(256)S(1)} %bitcast.93, f32[256,128,128]{2,1,0:T(8,128)} %fusion.20), kind=kCustom, calls=%fused_computation.13 | custom fusion | flops 4194304 | bytes 50332672 | tf_op jit(solution)/shard_map/scatter-add | solution.py:58
  428.7 2.6 gather_fusion.11
  432.8 2.6 gather_fusion.10
  436.8 8.8 %gather_fusion.7 = bf16[256,128,128]{2,1,0:T(8,128)(2,1)} fusion(bf16[128,32,128]{2,0,1:T(8,128)(2,1)S(1)} %copy-done.2, s32[1024]{0:T(1024)S(1)} %get-tuple-element.378), kind=kCustom, calls=%fused_computation.4.clone | custom fusion | bytes 16778240 | tf_op jit(solution)/shard_map/jit(_take)/gather | solution.py:134
  445.7 12.8 %fusion.16 = f32[256,128,128]{2,1,0:T(8,128)} fusion(bf16[256,128,128]{2,1,0:T(8,128)(2,1)} %bitcast.83, bf16[256,128,128]{2,1,0:T(8,128)(2,1)} %gather_fusion.7, pred[256]{0:T(512)(128)(4,1)S(1)} %get-tuple-element.348), kind=kOutput, calls=%fused_computation.59 | convolution fusion | flops 1077936128 | bytes 33554688 | tf_op jit(solution)/shard_map/rsb,sab->rsa/dot_general | solution.py:132
  458.7 33.1 %scatter_fusion.3 = f32[128,32,128]{2,0,1:T(8,128)S(1)} fusion(f32[128,32,128]{2,0,1:T(8,128)S(1)} %broadcast.525.clone.3, s32[256]{0:T(256)S(1)} %bitcast.92, f32[256,128,128]{2,1,0:T(8,128)} %fusion.16), kind=kCustom, calls=%fused_computation.15 | custom fusion | flops 4194304 | bytes 50332672 | tf_op jit(solution)/shard_map/scatter-add | solution.py:53
  502.5 214.0 %while.16 = (s32[]{:T(128)}, f32[2,16,128,128]{3,2,1,0:T(8,128)}, s32[]{:T(128)}, s32[128]{0:T(128)S(1)}, bf16[128,32,128]{2,0,1:T(8,128)(2,1)S(1)}, /*index=5*/...) while((s32[]{:T(128)}, f32[2,16,128,128]{3,2,1,0:T(8,128)}, ...), condition=%wide.region_13.16_spmd, body=%wide.region_12.15_spmd.sunk | while | flops 137368640 | bytes 20989624 | solution.py:171
  502.5 2.7 convert_element_type.100
  510.4 2.6 gather_fusion.1
  516.3 16.7 %collective-permute-done = bf16[2,16,128,128]{3,2,1,0:T(8,128)(2,1)} collective-permute-done((bf16[2,16,128,128]{3,2,1,0:T(8,128)(2,1)}, bf16[2,16,128,128]{3,2,1,0:T(8,128)(2,1)}, u32[]{:S(2)}, u32[]{:S(2)}) %collective-permute-start) | collective-permute-done | bytes 1048608 | tf_op jit(solution)/shard_map/while/body/eval_jaxpr/ppermute | solution.py:18
  532.9 2.9 maximum_add_fusion.2
  535.8 2.7 convert_element_type.100
  543.0 2.6 gather_fusion.1
  548.9 16.4 %collective-permute-done = bf16[2,16,128,128]{3,2,1,0:T(8,128)(2,1)} collective-permute-done((bf16[2,16,128,128]{3,2,1,0:T(8,128)(2,1)}, bf16[2,16,128,128]{3,2,1,0:T(8,128)(2,1)}, u32[]{:S(2)}, u32[]{:S(2)}) %collective-permute-start) | collective-permute-done | bytes 1048608 | tf_op jit(solution)/shard_map/while/body/eval_jaxpr/ppermute | solution.py:18
  565.3 2.9 maximum_add_fusion.2
  568.2 2.7 convert_element_type.100
  575.4 2.6 gather_fusion.1
  581.3 15.5 %collective-permute-done = bf16[2,16,128,128]{3,2,1,0:T(8,128)(2,1)} collective-permute-done((bf16[2,16,128,128]{3,2,1,0:T(8,128)(2,1)}, bf16[2,16,128,128]{3,2,1,0:T(8,128)(2,1)}, u32[]{:S(2)}, u32[]{:S(2)}) %collective-permute-start) | collective-permute-done | bytes 1048608 | tf_op jit(solution)/shard_map/while/body/eval_jaxpr/ppermute | solution.py:18
  596.8 2.9 maximum_add_fusion.2
  599.7 2.7 convert_element_type.100
  606.9 2.6 gather_fusion.1
  612.8 14.6 %collective-permute-done = bf16[2,16,128,128]{3,2,1,0:T(8,128)(2,1)} collective-permute-done((bf16[2,16,128,128]{3,2,1,0:T(8,128)(2,1)}, bf16[2,16,128,128]{3,2,1,0:T(8,128)(2,1)}, u32[]{:S(2)}, u32[]{:S(2)}) %collective-permute-start) | collective-permute-done | bytes 1048608 | tf_op jit(solution)/shard_map/while/body/eval_jaxpr/ppermute | solution.py:18
  627.4 2.9 maximum_add_fusion.2
  630.3 2.7 convert_element_type.100
  637.5 2.6 gather_fusion.1
  643.4 13.7 %collective-permute-done = bf16[2,16,128,128]{3,2,1,0:T(8,128)(2,1)} collective-permute-done((bf16[2,16,128,128]{3,2,1,0:T(8,128)(2,1)}, bf16[2,16,128,128]{3,2,1,0:T(8,128)(2,1)}, u32[]{:S(2)}, u32[]{:S(2)}) %collective-permute-start) | collective-permute-done | bytes 1048608 | tf_op jit(solution)/shard_map/while/body/eval_jaxpr/ppermute | solution.py:18
  657.1 2.9 maximum_add_fusion.2
  659.9 2.7 convert_element_type.100
  667.1 2.6 gather_fusion.1
  673.0 12.8 %collective-permute-done = bf16[2,16,128,128]{3,2,1,0:T(8,128)(2,1)} collective-permute-done((bf16[2,16,128,128]{3,2,1,0:T(8,128)(2,1)}, bf16[2,16,128,128]{3,2,1,0:T(8,128)(2,1)}, u32[]{:S(2)}, u32[]{:S(2)}) %collective-permute-start) | collective-permute-done | bytes 1048608 | tf_op jit(solution)/shard_map/while/body/eval_jaxpr/ppermute | solution.py:18
  685.8 2.9 maximum_add_fusion.2
  688.7 2.7 convert_element_type.100
  695.9 2.6 gather_fusion.1
  701.8 11.8 %collective-permute-done = bf16[2,16,128,128]{3,2,1,0:T(8,128)(2,1)} collective-permute-done((bf16[2,16,128,128]{3,2,1,0:T(8,128)(2,1)}, bf16[2,16,128,128]{3,2,1,0:T(8,128)(2,1)}, u32[]{:S(2)}, u32[]{:S(2)}) %collective-permute-start) | collective-permute-done | bytes 1048608 | tf_op jit(solution)/shard_map/while/body/eval_jaxpr/ppermute | solution.py:18
  713.6 2.9 maximum_add_fusion.2
  (172 shorter events, 91.4 us)
Async XLA Ops:
  7.2 47.8 %all-gather.7.cloned.1.call-start = ((), (), s32[]{:S(2)}) async-start(), calls=%async_computation.2 | async-start | bytes 1310720 | tf_op jit(solution)/shard_map/all_gather | solution.py:63
  7.9 49.4 %all-gather.9.cloned.1.call-start = ((), (), s32[]{:S(2)}) async-start(), calls=%async_computation.3 | async-start | bytes 1310720 | tf_op jit(solution)/shard_map/all_gather | solution.py:64
  8.6 165.8 %all-gather.11.cloned.1.call-start = ((), (), s32[]{:S(2)}) async-start(), calls=%async_computation.4 | async-start | bytes 9437184 | tf_op jit(solution)/shard_map/all_gather | solution.py:86
  9.4 290.2 %all-gather.13.cloned.1.call-start = ((), (), s32[]{:S(2)}) async-start(), calls=%async_computation.5 | async-start | bytes 9437184 | tf_op jit(solution)/shard_map/all_gather | solution.py:102
  10.0 709.7 %reduce-scatter.7.cloned.1.call-start = ((), (), s32[]{:S(2)}) async-start(), calls=%async_computation.6 | async-start | bytes 1310720
  59.7 8.6 %copy-start = (bf16[128,32,128]{2,0,1:T(8,128)(2,1)}, bf16[128,32,128]{2,0,1:T(8,128)(2,1)S(1)}, u32[]{:S(2)}) copy-start(bf16[128,32,128]{2,0,1:T(8,128)(2,1)S(1)} %copy.51) | copy-start | bytes 3145732
  425.5 9.9 %copy-start.2 = (bf16[128,32,128]{2,0,1:T(8,128)(2,1)S(1)}, bf16[128,32,128]{2,0,1:T(8,128)(2,1)}, u32[]{:S(2)}) copy-start(bf16[128,32,128]{2,0,1:T(8,128)(2,1)} %get-tuple-element.460) | copy-start | bytes 3145732
  428.5 291.1 %reduce-scatter.9.cloned.1.call-start = ((), (), s32[]{:S(2)}) async-start(), calls=%async_computation.7 | async-start | bytes 1310720
  493.0 9.5 %copy-start.1 = (bf16[128,32,128]{2,0,1:T(8,128)(2,1)S(1)}, bf16[128,32,128]{2,0,1:T(8,128)(2,1)}, u32[]{:S(2)}) copy-start(bf16[128,32,128]{2,0,1:T(8,128)(2,1)} %copy-done) | copy-start | bytes 3145732
  493.0 9.5 %copy-start.3 = (bf16[128,32,128]{2,0,1:T(8,128)(2,1)S(1)}, bf16[128,32,128]{2,0,1:T(8,128)(2,1)}, u32[]{:S(2)}) copy-start(bf16[128,32,128]{2,0,1:T(8,128)(2,1)} %get-tuple-element.460) | copy-start | bytes 3145732
  505.2 27.7 %collective-permute-start = (bf16[2,16,128,128]{3,2,1,0:T(8,128)(2,1)}, bf16[2,16,128,128]{3,2,1,0:T(8,128)(2,1)}, u32[]{:S(2)}, u32[]{:S(2)}) collective-permute-start(bf16[2,16,128,128]{3,2,1,0:T(8,128)(2,1)} %convert_element_type.100), channel_id=1, source_target_pairs={{0,4},{4,8},{8,12},{12,16},{16,20},{20,24},{24,28},{28,0},{1,5},{5... | collective-permute-start | bytes 3145736 | tf_op jit(solution)/shard_map/while/body/eval_jaxpr/ppermute | solution.py:18
  538.5 26.8 %collective-permute-start = (bf16[2,16,128,128]{3,2,1,0:T(8,128)(2,1)}, bf16[2,16,128,128]{3,2,1,0:T(8,128)(2,1)}, u32[]{:S(2)}, u32[]{:S(2)}) collective-permute-start(bf16[2,16,128,128]{3,2,1,0:T(8,128)(2,1)} %convert_element_type.100), channel_id=1, source_target_pairs={{0,4},{4,8},{8,12},{12,16},{16,20},{20,24},{24,28},{28,0},{1,5},{5... | collective-permute-start | bytes 3145736 | tf_op jit(solution)/shard_map/while/body/eval_jaxpr/ppermute | solution.py:18
  570.9 25.9 %collective-permute-start = (bf16[2,16,128,128]{3,2,1,0:T(8,128)(2,1)}, bf16[2,16,128,128]{3,2,1,0:T(8,128)(2,1)}, u32[]{:S(2)}, u32[]{:S(2)}) collective-permute-start(bf16[2,16,128,128]{3,2,1,0:T(8,128)(2,1)} %convert_element_type.100), channel_id=1, source_target_pairs={{0,4},{4,8},{8,12},{12,16},{16,20},{20,24},{24,28},{28,0},{1,5},{5... | collective-permute-start | bytes 3145736 | tf_op jit(solution)/shard_map/while/body/eval_jaxpr/ppermute | solution.py:18
  602.4 25.0 %collective-permute-start = (bf16[2,16,128,128]{3,2,1,0:T(8,128)(2,1)}, bf16[2,16,128,128]{3,2,1,0:T(8,128)(2,1)}, u32[]{:S(2)}, u32[]{:S(2)}) collective-permute-start(bf16[2,16,128,128]{3,2,1,0:T(8,128)(2,1)} %convert_element_type.100), channel_id=1, source_target_pairs={{0,4},{4,8},{8,12},{12,16},{16,20},{20,24},{24,28},{28,0},{1,5},{5... | collective-permute-start | bytes 3145736 | tf_op jit(solution)/shard_map/while/body/eval_jaxpr/ppermute | solution.py:18
  633.0 24.1 %collective-permute-start = (bf16[2,16,128,128]{3,2,1,0:T(8,128)(2,1)}, bf16[2,16,128,128]{3,2,1,0:T(8,128)(2,1)}, u32[]{:S(2)}, u32[]{:S(2)}) collective-permute-start(bf16[2,16,128,128]{3,2,1,0:T(8,128)(2,1)} %convert_element_type.100), channel_id=1, source_target_pairs={{0,4},{4,8},{8,12},{12,16},{16,20},{20,24},{24,28},{28,0},{1,5},{5... | collective-permute-start | bytes 3145736 | tf_op jit(solution)/shard_map/while/body/eval_jaxpr/ppermute | solution.py:18
  662.7 23.1 %collective-permute-start = (bf16[2,16,128,128]{3,2,1,0:T(8,128)(2,1)}, bf16[2,16,128,128]{3,2,1,0:T(8,128)(2,1)}, u32[]{:S(2)}, u32[]{:S(2)}) collective-permute-start(bf16[2,16,128,128]{3,2,1,0:T(8,128)(2,1)} %convert_element_type.100), channel_id=1, source_target_pairs={{0,4},{4,8},{8,12},{12,16},{16,20},{20,24},{24,28},{28,0},{1,5},{5... | collective-permute-start | bytes 3145736 | tf_op jit(solution)/shard_map/while/body/eval_jaxpr/ppermute | solution.py:18
  691.4 22.2 %collective-permute-start = (bf16[2,16,128,128]{3,2,1,0:T(8,128)(2,1)}, bf16[2,16,128,128]{3,2,1,0:T(8,128)(2,1)}, u32[]{:S(2)}, u32[]{:S(2)}) collective-permute-start(bf16[2,16,128,128]{3,2,1,0:T(8,128)(2,1)} %convert_element_type.100), channel_id=1, source_target_pairs={{0,4},{4,8},{8,12},{12,16},{16,20},{20,24},{24,28},{28,0},{1,5},{5... | collective-permute-start | bytes 3145736 | tf_op jit(solution)/shard_map/while/body/eval_jaxpr/ppermute | solution.py:18
Sparse Core Ops, SparseCore 0:
  9.6 19.4 all-gather.6
  30.6 16.7 all-gather.8
  49.5 124.9 all-gather.10
  176.4 123.1 all-gather.12
  428.7 23.4 reduce-scatter.6
  502.6 23.5 reduce-scatter.8
where the time goes:
time: 731 us; the launch traced here: 727 us
  waiting for transfers between devices  279 us (38%)
  other arithmetic  201 us (27%)
  local copies, waits for them, and re-layouts  112 us (15%)
  matrix products  79.5 us (11%)
  blocking collectives  38.7 us (5%)
  between operations  14.4 us (2%)
    ppermute x7, waiting for transfers between devices, from_behind(): lax.ppermute(array, axis, [(i, (i + by) % devices) for i in range(devices)])  102 us
    all_gather x1, waiting for transfers between devices, shards(): shard_piece = lax.all_gather(up_source, 'dp', axis=0, tiled=True)  97.6 us
    scatter-add x2, other arithmetic, place_sum(): return start.at[:, target].add(products, mode='drop')  82.2 us
    all_gather x1, waiting for transfers between devices, shards(): shard_piece = lax.all_gather(down_source, 'dp', axis=0, tiled=True)  77.5 us
    scatter-add x2, other arithmetic, place_add(): return running.at[:, target].add(products, mode='drop')  66.3 us
    all_gather x1, blocking collectives, shards(): lax.all_gather(down_place, 'dp', axis=0, tiled=True)  22.3 us
    gather x8, local copies, waits for them, and re-layouts, contribution(): jnp.take(hidden, down_own % group_blocks, axis=1)  21.2 us
    add x7, other arithmetic, turn_one(): from_behind(running.astype(jnp.bfloat16), 'dp', 1).astype(running.dtype)  20.1 us
  transfers between devices with their start and end apart: 13, of which 9 were waited for; matrix products, arithmetic and copies ran while one was open for 36% of the time, Pallas kernels for 0%

commit v1 on v0

v1 whole, which is shorter than its diff:
```python
import functools
import math

import jax
import jax.numpy as jnp
from jax import lax
from jax.experimental import pallas as pl
from jax.experimental.pallas import tpu as pltpu
from jax.sharding import PartitionSpec as P

FF = 16384
BLK = 128
PACK = 16
VMEM_LIMIT = 40 << 20

gelu_root = 0.7978845608028654
gelu_cubic = 0.044715

SMEM_SPEC = pl.BlockSpec(memory_space=pltpu.SMEM)
VMEM_SPEC = pl.BlockSpec(memory_space=pltpu.VMEM)


def ring_order(devices):
    evens = list(range(0, devices, 2))
    odds = list(range(1, devices, 2))
    return evens + odds[::-1]


def ring_pairs(devices):
    order = ring_order(devices)
    ahead = [(order[i], order[(i + 1) % devices]) for i in range(devices)]
    behind = [(b, a) for a, b in ahead]
    return ahead, behind


def call(kernel, out_shape, in_specs, scratch=(), flops=0, nbytes=0, grid=None, out_specs=VMEM_SPEC):
    extra = {} if grid is None else {"grid": grid}
    return pl.pallas_call(
        kernel,
        out_shape=out_shape,
        in_specs=in_specs,
        out_specs=out_specs,
        scratch_shapes=list(scratch),
        compiler_params=pltpu.CompilerParams(vmem_limit_bytes=VMEM_LIMIT),
        cost_estimate=pl.CostEstimate(flops=flops, bytes_accessed=nbytes, transcendentals=0),
        **extra,
    )


def shape(dims, dtype):
    return jax.ShapeDtypeStruct(tuple(dims), dtype)


def dot(a, b, ca, cb):
    return lax.dot_general(a, b, (((ca,), (cb,)), ((), ())), preferred_element_type=jnp.float32)


def unroll_of(count):
    return math.gcd(count, 8)


def split_kernel(me_ref, x_ref, *outs):
    piece = outs[0].shape[1]
    for step, out in enumerate(outs):
        start = pl.multiple_of((me_ref[0] ^ step) * piece, piece)
        out[...] = x_ref[:, pl.ds(start, piece), :]


def split_blocks(me, blocks, devices):
    slots = blocks.shape[0]
    piece = BLK // devices
    out = [shape((slots, piece, BLK), blocks.dtype)] * devices
    return call(
        split_kernel, out, [SMEM_SPEC, VMEM_SPEC], out_specs=[VMEM_SPEC] * devices, nbytes=2 * blocks.size * 2
    )(me, blocks)


def pack_kernel(pick_ref, *refs):
    *ins, out_a, out_b, held = refs
    slots = ins[0].shape[0]
    half = out_a.shape[0]
    for step, part in enumerate(ins):
        held[step * slots : (step + 1) * slots] = part[...]
    unroll = unroll_of(half)

    def body(i, carry):
        for u in range(unroll):
            k = i * unroll + u
            out_a[k] = held[pick_ref[k]]
            out_b[k] = held[pick_ref[half + k]]
        return carry

    lax.fori_loop(0, half // unroll, body, 0)


def pack_pieces(pick, parts, live):
    slots, piece, _ = parts[0].shape
    out = [shape((live // 2, piece, BLK), parts[0].dtype)] * 2
    return call(
        pack_kernel,
        out,
        [SMEM_SPEC] + [VMEM_SPEC] * len(parts),
        out_specs=[VMEM_SPEC] * 2,
        scratch=[pltpu.VMEM((len(parts) * slots, piece, BLK), parts[0].dtype)],
        nbytes=3 * len(parts) * slots * piece * BLK,
    )(pick, *parts)


def join_kernel(ahead_ref, behind_ref, *refs):
    *ins, out = refs
    devices = len(ins) // 2
    half, piece, _ = ins[0].shape
    for j in range(devices):
        start = pl.multiple_of(ahead_ref[j] * piece, piece)
        out[:half, pl.ds(start, piece), :] = ins[j][...]
        start = pl.multiple_of(behind_ref[j] * piece, piece)
        out[half:, pl.ds(start, piece), :] = ins[devices + j][...]


def join_pieces(ahead, behind, first, second):
    half = first[0].shape[0]
    return call(
        join_kernel,
        shape((2 * half, BLK, BLK), first[0].dtype),
        [SMEM_SPEC] * 2 + [VMEM_SPEC] * (2 * len(first)),
        nbytes=8 * half * BLK * BLK,
    )(ahead, behind, *first, *second)


def lanes(ref, block):
    return ref[:, pl.ds(pl.multiple_of(block * BLK, BLK), BLK)]


def sum_blocks(acc, live, target, term):
    acc[...] = jnp.zeros_like(acc)
    unroll = unroll_of(live)

    def body(i, carry):
        products = [term(i * unroll + u) for u in range(unroll)]
        for u in range(unroll):
            acc[target(i * unroll + u)] += products[u]
        return carry

    lax.fori_loop(0, live // unroll, body, 0)


def hidden_kernel(rows_ref, cols_ref, tok_ref, w_ref, hid_ref, turned_ref, slope_ref, acc):
    sum_blocks(
        acc,
        w_ref.shape[0],
        lambda k: cols_ref[k],
        lambda k: dot(lanes(tok_ref, rows_ref[k]), w_ref[k], 1, 0),
    )

    def body(c, carry):
        values = acc[c]
        tanh = jnp.tanh(gelu_root * (values + gelu_cubic * values * values * values))
        hidden = 0.5 * values * (1.0 + tanh)
        hid_ref[c] = hidden.astype(jnp.bfloat16)
        turned_ref[c] = hidden.T.astype(jnp.bfloat16)
        slope_ref[c] = 0.5 * (1.0 + tanh) + 0.5 * values * (1.0 - tanh * tanh) * gelu_root * (
            1.0 + 3.0 * gelu_cubic * values * values
        )
        return carry

    lax.fori_loop(0, acc.shape[0], body, 0)


def grad_pre_kernel(rows_ref, cols_ref, cot_ref, w_ref, slope_ref, out_ref, acc):
    sum_blocks(
        acc,
        w_ref.shape[0],
        lambda k: cols_ref[k],
        lambda k: dot(lanes(cot_ref, rows_ref[k]), w_ref[k], 1, 1),
    )

    def body(c, carry):
        out_ref[c] = (acc[c] * slope_ref[c]).astype(jnp.bfloat16)
        return carry

    lax.fori_loop(0, acc.shape[0], body, 0)


def width_kernel(contract, rows_ref, cols_ref, x_ref, w_ref, out_ref, acc):
    sum_blocks(
        acc,
        w_ref.shape[0],
        lambda k: rows_ref[k],
        lambda k: dot(x_ref[cols_ref[k]], w_ref[k], 1, contract),
    )
    for r in range(acc.shape[0]):
        out_ref[:, r * BLK : (r + 1) * BLK] = acc[r].astype(jnp.bfloat16)


def up_terms_kernel(owner_ref, rows_ref, cols_ref, turned_ref, grad_ref, out_ref):
    mean = out_ref.shape[1]
    base = owner_ref[pl.program_id(0)] * mean
    for j in range(mean):
        start = pl.multiple_of(rows_ref[base + j] * BLK, BLK)
        out_ref[0, j] = dot(turned_ref[pl.ds(start, BLK), :], grad_ref[cols_ref[base + j]], 1, 0)


def down_terms_kernel(owner_ref, rows_ref, cols_ref, turned_ref, cot_ref, out_ref):
    mean = out_ref.shape[1]
    base = owner_ref[pl.program_id(0)] * mean
    for j in range(mean):
        out_ref[0, j] = dot(turned_ref[cols_ref[base + j]], lanes(cot_ref, rows_ref[base + j]), 1, 0)


def terms(kernel, owner, rows, cols, left, right):
    devices = owner.shape[0]
    live = rows.shape[0]
    mean = live // devices
    return call(
        kernel,
        shape((devices, mean, BLK, BLK), jnp.float32),
        [SMEM_SPEC] * 3 + [VMEM_SPEC] * 2,
        grid=(devices,),
        out_specs=pl.BlockSpec((1, mean, BLK, BLK), lambda i: (i, 0, 0, 0)),
        flops=2 * live * BLK**3 * 4,
        nbytes=live * BLK * BLK * 4 + 2 * (left.size + right.size),
    )(owner, rows, cols, left, right)


def ring_sum(parts, ahead, behind):
    devices = parts.shape[0]
    half = BLK // 2

    def low(q):
        return parts[q, :, :half]

    def high(q):
        return parts[q, :, half:]

    run_a = low(0)
    run_b = high((devices - 2) % devices)
    for step in range(1, devices):
        run_a = lax.ppermute(run_a.astype(jnp.bfloat16), "dp", ahead)
        run_b = lax.ppermute(run_b.astype(jnp.bfloat16), "dp", behind)
        last = step == devices - 1
        run_a = run_a.astype(jnp.float32) + low(step)
        run_b = run_b.astype(jnp.float32) + high(step if last else devices - 2 - step)
    return jnp.concatenate([run_a, run_b], axis=1)


def shards(tokens, cotangent, up_blocks, up_place, down_blocks, down_place):
    devices = lax.axis_size("dp")
    me = lax.axis_index("dp")
    slots = up_place.shape[2]
    mean = slots // 2
    live = devices * mean
    group_blocks = FF // BLK // lax.axis_size("tensor")
    model_width = tokens.shape[1]
    model_blocks = model_width // BLK

    order = ring_order(devices)
    place = {d: i for i, d in enumerate(order)}
    ahead, behind = ring_pairs(devices)
    nav = jnp.array(
        [
            [
                [order[(place[d] - j) % devices] for j in range(devices)],
                [order[(place[d] + j) % devices] for j in range(devices)],
                [order[(place[d] - 1 - j) % devices] for j in range(devices)],
            ]
            for d in range(devices)
        ],
        jnp.int32,
    )[me]
    from_ahead, from_behind, owner = nav[0], nav[1], nav[2]

    codes = lax.all_gather(
        jnp.stack([up_place.reshape(slots), down_place.reshape(slots)])[None], "dp", axis=0, tiled=True
    )
    codes = jnp.transpose(codes, (1, 0, 2))
    counts = jnp.sum((codes >= 0).astype(jnp.int32), axis=2)
    index = jnp.arange(devices, dtype=jnp.int32)
    ends = jnp.sum(jnp.where(index[None, None, :] <= index[None, :, None], counts[:, None, :], 0), axis=2)
    listed = jnp.arange(live, dtype=jnp.int32)
    holder = jnp.sum((listed[None, :, None] >= ends[:, None, :]).astype(jnp.int32), axis=2)
    offset = jnp.sum(jnp.where(index[None, None, :] < holder[:, :, None], counts[:, None, :], 0), axis=2)
    slot = listed[None, :] - offset
    source = holder * slots + slot
    every = jnp.arange(devices * slots, dtype=jnp.int32)
    flat = codes.reshape(2, devices * slots)
    code = jnp.sum(jnp.where(every[None, None, :] == source[:, :, None], flat[:, None, :], 0), axis=2)
    rows = code // group_blocks
    cols = code % group_blocks
    pick = (holder ^ me) * slots + slot

    tok = lax.all_gather(tokens, "tensor", axis=0, tiled=True)
    cot = lax.all_gather(cotangent, "tensor", axis=0, tiled=True)
    row_count = tok.shape[0]

    if BLK % (PACK * devices) == 0:
        here = me.reshape(1).astype(jnp.int32)

        def spread(blocks):
            parts = split_blocks(here, blocks.reshape(slots, BLK, BLK), devices)
            return [parts[0]] + [
                lax.ppermute(parts[s], "dp", [(i, i ^ s) for i in range(devices)]) for s in range(1, devices)
            ]

        def gather(parts, which):
            a, b = pack_pieces(pick[which], parts, live)
            first, second = [a], [b]
            for _ in range(1, devices):
                a, b = lax.ppermute(a, "dp", ahead), lax.ppermute(b, "dp", behind)
                first.append(a)
                second.append(b)
            return join_pieces(from_ahead, from_behind, first, second)

        up_parts = spread(up_blocks)
        down_parts = spread(down_blocks)
        up = gather(up_parts, 0)
        down = gather(down_parts, 1)
    else:

        def gather_all(blocks, which):
            every_slot = lax.all_gather(blocks.reshape(slots, BLK, BLK), "dp", axis=0, tiled=True)
            return jnp.take(every_slot, source[which], axis=0)

        up = gather_all(up_blocks, 0)
        down = gather_all(down_blocks, 1)

    flops = 2 * live * row_count * BLK * BLK * 4
    block_bytes = live * BLK * BLK * 2
    side = row_count * BLK
    group_acc = pltpu.VMEM((group_blocks, row_count, BLK), jnp.float32)
    model_acc = pltpu.VMEM((model_blocks, row_count, BLK), jnp.float32)
    tables = [SMEM_SPEC] * 2

    hid, hid_turned, slope = call(
        hidden_kernel,
        [
            shape((group_blocks, row_count, BLK), jnp.bfloat16),
            shape((group_blocks, BLK, row_count), jnp.bfloat16),
            shape((group_blocks, row_count, BLK), jnp.float32),
        ],
        tables + [VMEM_SPEC] * 2,
        out_specs=[VMEM_SPEC] * 3,
        scratch=[group_acc],
        flops=flops,
        nbytes=block_bytes + side * (2 * model_blocks + 8 * group_blocks),
    )(rows[0], cols[0], tok, up)

    down_terms = terms(down_terms_kernel, owner, rows[1], cols[1], hid_turned, cot)

    grad_pre = call(
        grad_pre_kernel,
        shape((group_blocks, row_count, BLK), jnp.bfloat16),
        tables + [VMEM_SPEC] * 3,
        scratch=[group_acc],
        flops=flops,
        nbytes=block_bytes + side * (2 * model_blocks + 6 * group_blocks),
    )(rows[1], cols[1], cot, down, slope)

    up_terms = terms(up_terms_kernel, owner, rows[0], cols[0], tok.T, grad_pre)

    def width(contract, which, x, w):
        return call(
            functools.partial(width_kernel, contract),
            shape((row_count, model_width), jnp.bfloat16),
            tables + [VMEM_SPEC] * 2,
            scratch=[model_acc],
            flops=flops,
            nbytes=block_bytes + side * (2 * model_blocks + 2 * group_blocks),
        )(rows[which], cols[which], x, w)

    out_part = width(0, 1, hid, down)
    in_part = width(1, 0, grad_pre, up)

    outputs = lax.psum_scatter(out_part, "tensor", scatter_dimension=0, tiled=True)
    input_grads = lax.psum_scatter(in_part, "tensor", scatter_dimension=0, tiled=True)

    scale = 1.0 / math.sqrt(devices * row_count)
    down_grads = ring_sum(down_terms, ahead, behind) * scale
    up_grads = ring_sum(up_terms, ahead, behind) * scale
    grads_shape = (1, 1, mean, BLK, BLK)
    return (outputs, input_grads, up_grads.reshape(grads_shape), down_grads.reshape(grads_shape))


def solution(mesh):
    return jax.shard_map(
        shards,
        mesh=mesh,
        in_specs=(
            P(("dp", "tensor"), None),
            P(("dp", "tensor"), None),
            P("dp", "tensor", None, None, None),
            P("dp", "tensor", None),
            P("dp", "tensor", None, None, None),
            P("dp", "tensor", None),
        ),
        out_specs=(
            P(("dp", "tensor"), None),
            P(("dp", "tensor"), None),
            P("dp", "tensor", None, None, None),
            P("dp", "tensor", None, None, None),
        ),
        check_vma=False,
    )
```

time: 731 us -> 291 us (0.40)
  waiting for transfers between devices: 279 us -> 73 us
  other arithmetic: 201 us -> 24.5 us
  starting transfers between devices: 0.94 us -> 96 us
  local copies, waits for them, and re-layouts: 112 us -> 23.4 us
  matrix products: 79.5 us -> 0 us
  Pallas kernels: 0 us -> 38.6 us
  blocking collectives: 38.7 us -> 20.6 us
    all_gather x4 -> x2, waiting for transfers between devices: 175 us -> 0.01 us  [the longest x1 0.01 us: shards(): tok = lax.all_gather(tokens, 'tensor', axis=0, tiled=True)]
    scatter-add x4 -> x0, other arithmetic: 149 us -> none  [the longest x2 82.2 us: place_sum(): return start.at[:, target].add(products, mode='drop')]
    ppermute x7 -> x70, starting transfers between devices: 0.71 us -> 95.8 us  [the longest x28 37.9 us: gather(): a, b = (lax.ppermute(a, 'dp', ahead), lax.ppermute(b, 'dp', behind))]
    gather x36 -> x0, local copies, waits for them, and re-layouts: 92 us -> none  [the longest x8 21.2 us: contribution(): jnp.take(hidden, down_own % group_blocks, axis=1)]
    dot_general x20 -> x0, matrix products: 79.5 us -> none  [the longest x1 14.2 us: shards(): jnp.einsum('rsa,sab->rsb', jnp.take(token_cube, block_rows, axis=1), bloc...]
    pallas_call x0 -> x12, Pallas kernels: none -> 38.6 us  [the longest x2 12.6 us: width(): call(functools.partial(width_kernel, contract), shape((row_count, model_w...]
    ppermute x7 -> x70, waiting for transfers between devices: 102 us -> 72.2 us  [the longest x28 39 us: gather(): a, b = (lax.ppermute(a, 'dp', ahead), lax.ppermute(b, 'dp', behind))]
    add x7 -> x1, other arithmetic: 20.1 us -> 0.01 us  [shards(): pick = (holder ^ me) * slots + slot]
  transfers between devices with their start and end apart: 13 -> 74, of which waited for: 9 -> 38; matrix products, arithmetic and copies ran while one was open for 36% -> 9% of each run, Pallas kernels for 0% -> 9%
where the time goes in v1:
time: 291 us; the launch traced here: 290 us
  starting transfers between devices  96 us (33%)
  waiting for transfers between devices  73 us (25%)
  Pallas kernels  38.6 us (13%)
  other arithmetic  24.5 us (8%)
  local copies, waits for them, and re-layouts  23.4 us (8%)
  blocking collectives  20.6 us (7%)
  between operations  14.3 us (5%)
    ppermute x28, waiting for transfers between devices, gather(): a, b = (lax.ppermute(a, 'dp', ahead), lax.ppermute(b, 'dp', behind))  39 us
    ppermute x28, starting transfers between devices, gather(): a, b = (lax.ppermute(a, 'dp', ahead), lax.ppermute(b, 'dp', behind))  37.9 us
    ppermute x14, starting transfers between devices, spread(): lax.ppermute(parts[s], 'dp', [(i, i ^ s) for i in range(devices)])  27.5 us
    unnamed x36, local copies, waits for them, and re-layouts  21.8 us
    all_gather x1, blocking collectives, shards(): lax.all_gather(jnp.stack([up_place.reshape(slots), down_place.reshape(slo...  20.6 us
    ppermute x14, starting transfers between devices, ring_sum(): run_b = lax.ppermute(run_b.astype(jnp.bfloat16), 'dp', behind)  19.9 us
    convert_element_type x12, other arithmetic, ring_sum(): run_a = lax.ppermute(run_a.astype(jnp.bfloat16), 'dp', ahead)  16.3 us
    ppermute x14, waiting for transfers between devices, ring_sum(): run_a = lax.ppermute(run_a.astype(jnp.bfloat16), 'dp', ahead)  14.4 us
  transfers between devices with their start and end apart: 74, of which 38 were waited for; matrix products, arithmetic and copies ran while one was open for 9% of the time, Pallas kernels for 9%

profile of v1, /device:TPU:0, one launch (start us, length us, event | category | flops | bytes accessed | tf_op | source)
XLA Modules:
  0.0 290.4 jit_solution(8747178801452267763)
XLA Ops:
  9.3 3.0 %collective-permute-start = (bf16[32,16,128]{2,1,0:T(8,128)(2,1)S(1)}, bf16[32,16,128]{2,1,0:T(8,128)(2,1)S(1)}, u32[]{:S(2)}, u32[]{:S(2)}) collective-permute-start(bf16[32,16,128]{2,1,0:T(8,128)(2,1)S(1)} %get-tuple-element.28), channel_id=1, source_target_pairs={{0,4},{4,0},{8,12},{12,8},{16,20},{20,16},{24,28},{28,24},{1,5},{5... | collective-permute-start | bytes 393224 | tf_op jit(solution)/shard_map/ppermute | solution.py:301
  13.9 3.0 %collective-permute-start.3 = (bf16[32,16,128]{2,1,0:T(8,128)(2,1)S(1)}, bf16[32,16,128]{2,1,0:T(8,128)(2,1)S(1)}, u32[]{:S(2)}, u32[]{:S(2)}) collective-permute-start(bf16[32,16,128]{2,1,0:T(8,128)(2,1)S(1)} %get-tuple-element.31), channel_id=1, source_target_pairs={{0,16},{4,20},{8,24},{12,28},{16,0},{20,4},{24,8},{28,12},{1,17},{... | collective-permute-start | bytes 393224 | tf_op jit(solution)/shard_map/ppermute | solution.py:301
  18.9 20.6 %all-gather.1 = s32[8,2,32]{2,1,0:T(2,128)S(1)} all-gather(s32[1,2,32]{2,1,0:T(2,128)S(1)} %add_bitcast_fusion), channel_id=2, replica_groups=mesh['dp'=8,'tensor'=4] {'dp'}, dimensions={0}, use_global_device_ids=true | all-gather | bytes 2304 | tf_op jit(solution)/shard_map/all_gather | solution.py:272
  41.5 3.0 %collective-permute-start.6 = (bf16[32,16,128]{2,1,0:T(8,128)(2,1)S(1)}, bf16[32,16,128]{2,1,0:T(8,128)(2,1)S(1)}, u32[]{:S(2)}, u32[]{:S(2)}) collective-permute-start(bf16[32,16,128]{2,1,0:T(8,128)(2,1)S(1)} %get-tuple-element.34), channel_id=1, source_target_pairs={{0,28},{4,24},{8,20},{12,16},{16,12},{20,8},{24,4},{28,0},{1,29},{... | collective-permute-start | bytes 393224 | tf_op jit(solution)/shard_map/ppermute | solution.py:301
  44.5 2.3 collective-permute-start.21
  51.8 4.9 %collective-permute-start.25 = (bf16[32,16,128]{2,1,0:T(8,128)(2,1)S(1)}, bf16[32,16,128]{2,1,0:T(8,128)(2,1)S(1)}, u32[]{:S(2)}, u32[]{:S(2)}) collective-permute-start(bf16[32,16,128]{2,1,0:T(8,128)(2,1)S(1)} %get-tuple-element.43), channel_id=1, source_target_pairs={{0,20},{4,16},{8,28},{12,24},{16,4},{20,0},{24,12},{28,8},{1,21},{... | collective-permute-start | bytes 393224 | tf_op jit(solution)/shard_map/ppermute | solution.py:301
  56.6 3.8 %collective-permute-start.26 = (bf16[32,16,128]{2,1,0:T(8,128)(2,1)S(1)}, bf16[32,16,128]{2,1,0:T(8,128)(2,1)S(1)}, u32[]{:S(2)}, u32[]{:S(2)}) collective-permute-start(bf16[32,16,128]{2,1,0:T(8,128)(2,1)S(1)} %get-tuple-element.44), channel_id=1, source_target_pairs={{0,24},{4,28},{8,16},{12,20},{16,8},{20,12},{24,0},{28,4},{1,25},{... | collective-permute-start | bytes 393224 | tf_op jit(solution)/shard_map/ppermute | solution.py:301
  60.4 3.1 %collective-permute-start.27 = (bf16[32,16,128]{2,1,0:T(8,128)(2,1)S(1)}, bf16[32,16,128]{2,1,0:T(8,128)(2,1)S(1)}, u32[]{:S(2)}, u32[]{:S(2)}) collective-permute-start(bf16[32,16,128]{2,1,0:T(8,128)(2,1)S(1)} %get-tuple-element.45), channel_id=1, source_target_pairs={{0,28},{4,24},{8,20},{12,16},{16,12},{20,8},{24,4},{28,0},{1,29},{... | collective-permute-start | bytes 393224 | tf_op jit(solution)/shard_map/ppermute | solution.py:301
  66.4 3.3 %collective-permute-done.25.refs_5_ = bf16[32,16,128]{2,1,0:T(8,128)(2,1)S(1)} collective-permute-done((bf16[32,16,128]{2,1,0:T(8,128)(2,1)S(1)}, bf16[32,16,128]{2,1,0:T(8,128)(2,1)S(1)}, u32[]{:S(2)}, u32[]{:S(2)}) %collective-permute-start.25) | collective-permute-done | bytes 131104 | tf_op jit(solution)/shard_map/ppermute | solution.py:301
  70.5 6.2 %collective-permute-start.28 = (bf16[64,16,128]{2,1,0:T(8,128)(2,1)S(1)}, bf16[64,16,128]{2,1,0:T(8,128)(2,1)S(1)}, u32[]{:S(2)}, u32[]{:S(2)}) collective-permute-start(bf16[64,16,128]{2,1,0:T(8,128)(2,1)S(1)} %get-tuple-element.46.refs_0_), channel_id=1, source_target_pairs={{0,8},{8,16},{16,24},{24,28},{28,20},{20,12},{12,4},{4,0},{1,9},{9... | collective-permute-start | bytes 786440 | tf_op jit(solution)/shard_map/ppermute | solution.py:308
  76.7 2.1 collective-permute-start.8
  78.8 4.6 %collective-permute-done.28.refs_1_ = bf16[64,16,128]{2,1,0:T(8,128)(2,1)S(1)} collective-permute-done((bf16[64,16,128]{2,1,0:T(8,128)(2,1)S(1)}, bf16[64,16,128]{2,1,0:T(8,128)(2,1)S(1)}, u32[]{:S(2)}, u32[]{:S(2)}) %collective-permute-start.28) | collective-permute-done | bytes 262176 | tf_op jit(solution)/shard_map/ppermute | solution.py:308
  83.5 2.5 collective-permute-start.29
  85.9 3.1 %collective-permute-done.8.refs_2_ = bf16[64,16,128]{2,1,0:T(8,128)(2,1)S(1)} collective-permute-done((bf16[64,16,128]{2,1,0:T(8,128)(2,1)S(1)}, bf16[64,16,128]{2,1,0:T(8,128)(2,1)S(1)}, u32[]{:S(2)}, u32[]{:S(2)}) %collective-permute-start.8) | collective-permute-done | bytes 262176 | tf_op jit(solution)/shard_map/ppermute | solution.py:308
  89.1 2.5 collective-permute-start.9
  91.6 3.1 %collective-permute-done.29.refs_2_ = bf16[64,16,128]{2,1,0:T(8,128)(2,1)S(1)} collective-permute-done((bf16[64,16,128]{2,1,0:T(8,128)(2,1)S(1)}, bf16[64,16,128]{2,1,0:T(8,128)(2,1)S(1)}, u32[]{:S(2)}, u32[]{:S(2)}) %collective-permute-start.29) | collective-permute-done | bytes 262176 | tf_op jit(solution)/shard_map/ppermute | solution.py:308
  94.7 2.5 collective-permute-start.30
  97.3 2.9 collective-permute-done.9.refs_3_
  100.1 2.6 collective-permute-start.10
  102.7 3.0 %collective-permute-done.30.refs_3_ = bf16[64,16,128]{2,1,0:T(8,128)(2,1)S(1)} collective-permute-done((bf16[64,16,128]{2,1,0:T(8,128)(2,1)S(1)}, bf16[64,16,128]{2,1,0:T(8,128)(2,1)S(1)}, u32[]{:S(2)}, u32[]{:S(2)}) %collective-permute-start.30) | collective-permute-done | bytes 262176 | tf_op jit(solution)/shard_map/ppermute | solution.py:308
  105.7 2.5 collective-permute-start.31
  108.3 3.0 %collective-permute-done.10.refs_4_ = bf16[64,16,128]{2,1,0:T(8,128)(2,1)} collective-permute-done((bf16[64,16,128]{2,1,0:T(8,128)(2,1)}, bf16[64,16,128]{2,1,0:T(8,128)(2,1)}, u32[]{:S(2)}, u32[]{:S(2)}) %collective-permute-start.10) | collective-permute-done | bytes 262176 | tf_op jit(solution)/shard_map/ppermute | solution.py:308
  111.4 2.5 collective-permute-start.11
  113.9 3.0 %collective-permute-done.31.refs_4_ = bf16[64,16,128]{2,1,0:T(8,128)(2,1)} collective-permute-done((bf16[64,16,128]{2,1,0:T(8,128)(2,1)S(1)}, bf16[64,16,128]{2,1,0:T(8,128)(2,1)}, u32[]{:S(2)}, u32[]{:S(2)}) %collective-permute-start.31) | collective-permute-done | bytes 262176 | tf_op jit(solution)/shard_map/ppermute | solution.py:308
  116.9 2.6 collective-permute-start.32
  119.7 2.9 collective-permute-done.11.refs_5_
  122.6 2.5 collective-permute-start.12
  125.1 3.1 %collective-permute-done.32.refs_5_ = bf16[64,16,128]{2,1,0:T(8,128)(2,1)} collective-permute-done((bf16[64,16,128]{2,1,0:T(8,128)(2,1)}, bf16[64,16,128]{2,1,0:T(8,128)(2,1)}, u32[]{:S(2)}, u32[]{:S(2)}) %collective-permute-start.32) | collective-permute-done | bytes 262176 | tf_op jit(solution)/shard_map/ppermute | solution.py:308
  128.2 2.5 collective-permute-start.33
  131.4 2.4 collective-permute-done.12.refs_6_
  133.8 2.4 collective-permute-start.13
  136.2 3.2 %collective-permute-done.33.refs_6_ = bf16[64,16,128]{2,1,0:T(8,128)(2,1)S(1)} collective-permute-done((bf16[64,16,128]{2,1,0:T(8,128)(2,1)}, bf16[64,16,128]{2,1,0:T(8,128)(2,1)S(1)}, u32[]{:S(2)}, u32[]{:S(2)}) %collective-permute-start.33) | collective-permute-done | bytes 262176 | tf_op jit(solution)/shard_map/ppermute | solution.py:308
  139.5 2.4 collective-permute-start.34
  143.8 2.6 collective-permute-done.20.refs_15_
  154.2 2.2 copy-done.6
  157.6 8.1 %shard_map.105 = (bf16[32,128,128]{2,1,0:T(8,128)(2,1)S(1)}, bf16[32,128,128]{2,1,0:T(8,128)(2,1)S(1)}, f32[32,128,128]{2,1,0:T(8,128)S(1)}) custom-call(s32[128]{0:T(128)S(1)} %get-tuple-element.96.rows_ref, s32[128]{0:T(128)S(1)} %get-tuple-element.89.cols_ref, bf16[128,4096]{1,0:T(8,128)(2,1)S(1)} %copy-done.12, bf16[128,128,128]{2,1,0:T(8,128)(2,1)S(1)} %copy-done.6), custom_call_target="tpu_custom_call" | custom-call | flops 2147483648 | bytes 9437184 | tf_op jit(solution)/shard_map/pallas_call | solution.py:333
  167.7 2.2 copy-done.3
  171.1 5.9 %shard_map.110.x_ref.grad_ref = bf16[32,128,128]{2,1,0:T(8,128)(2,1)S(1)} custom-call(s32[128]{0:T(128)S(1)} %get-tuple-element.95.rows_ref, s32[128]{0:T(128)S(1)} %get-tuple-element.90.cols_ref, bf16[128,4096]{1,0:T(8,128)(2,1)S(1)} %copy-done.8, bf16[128,128,128]{2,1,0:T(8,128)(2,1)S(1)} %copy-done.3, f32[32,128,128]{2,1,0:T(8,128)S(1)} %get-tuple-element.48.slope_ref), custom_call_target="tpu_custom_call" | custom-call | flops 2147483648 | bytes 8388608 | tf_op jit(solution)/shard_map/pallas_call | solution.py:349
  177.0 7.0 %shard_map.111 = bf16[128,4096]{1,0:T(8,128)(2,1)} custom-call(s32[128]{0:T(128)S(1)} %get-tuple-element.96.rows_ref, s32[128]{0:T(128)S(1)} %get-tuple-element.89.cols_ref, bf16[32,128,128]{2,1,0:T(8,128)(2,1)S(1)} %shard_map.110.x_ref.grad_ref, bf16[128,128,128]{2,1,0:T(8,128)(2,1)S(1)} %copy-done.7), custom_call_target="tpu_custom_call" | custom-call | flops 2147483648 | bytes 6291456 | tf_op jit(solution)/shard_map/pallas_call | solution.py:361
  184.8 3.1 %shard_map.112 = f32[8,16,128,128]{3,2,1,0:T(8,128)S(1)} custom-call(s32[8]{0:T(128)S(1)} %get-tuple-element.82.owner_ref, s32[128]{0:T(128)S(1)} %get-tuple-element.96.rows_ref, s32[128]{0:T(128)S(1)} %get-tuple-element.89.cols_ref, bf16[4096,128]{1,0:T(8,128)(2,1)S(1)} %bitcast.212, bf16[32,128,128]{2,1,0:T(8,128)(2,1)S(1)} %shard_map.110.x_ref.grad_ref), custom_call_target="tpu_custom_call" | custom-call | flops 2147483648 | bytes 10485760 | tf_op jit(solution)/shard_map/pallas_call | solution.py:214
  187.9 3.3 %copy-done = f32[8,16,128,128]{3,2,1,0:T(8,128)} copy-done((f32[8,16,128,128]{3,2,1,0:T(8,128)}, f32[8,16,128,128]{3,2,1,0:T(8,128)S(1)}, u32[]{:S(2)}) %copy-start) | copy-done | bytes 8388632
  192.3 3.3 %collective-permute-start.42 = (bf16[16,64,128]{2,1,0:T(8,128)(2,1)S(1)}, bf16[16,64,128]{2,1,0:T(8,128)(2,1)S(1)}, u32[]{:S(2)}, u32[]{:S(2)}) collective-permute-start(bf16[16,64,128]{2,1,0:T(8,128)(2,1)S(1)} %get-tuple-element.80), channel_id=1, source_target_pairs={{0,8},{8,16},{16,24},{24,28},{28,20},{20,12},{12,4},{4,0},{1,9},{9... | collective-permute-start | bytes 786440 | tf_op jit(solution)/shard_map/ppermute | solution.py:238
  195.6 3.3 %shard_map.113 = f32[8,16,128,128]{3,2,1,0:T(8,128)S(1)} custom-call(s32[8]{0:T(128)S(1)} %get-tuple-element.82.owner_ref, s32[128]{0:T(128)S(1)} %get-tuple-element.95.rows_ref, s32[128]{0:T(128)S(1)} %get-tuple-element.90.cols_ref, bf16[32,128,128]{2,1,0:T(8,128)(2,1)S(1)} %copy-done.15, bf16[128,4096]{1,0:T(8,128)(2,1)S(1)} %copy-done.9), custom_call_target="tpu_custom_call" | custom-call | flops 2147483648 | bytes 10485760 | tf_op jit(solution)/shard_map/pallas_call | solution.py:214
  198.9 3.3 %copy-done.1 = f32[8,16,128,128]{3,2,1,0:T(8,128)} copy-done((f32[8,16,128,128]{3,2,1,0:T(8,128)}, f32[8,16,128,128]{3,2,1,0:T(8,128)S(1)}, u32[]{:S(2)}) %copy-start.1) | copy-done | bytes 8388632
  205.4 5.6 %shard_map.109 = bf16[128,4096]{1,0:T(8,128)(2,1)} custom-call(s32[128]{0:T(128)S(1)} %get-tuple-element.95.rows_ref, s32[128]{0:T(128)S(1)} %get-tuple-element.90.cols_ref, bf16[32,128,128]{2,1,0:T(8,128)(2,1)S(1)} %copy-done.17, bf16[128,128,128]{2,1,0:T(8,128)(2,1)S(1)} %copy-done.4), custom_call_target="tpu_custom_call" | custom-call | flops 2147483648 | bytes 6291456 | tf_op jit(solution)/shard_map/pallas_call | solution.py:361
  212.4 2.1 collective-permute-start.43
  217.9 2.7 collective-permute-done.43
  220.6 2.3 collective-permute-done.50
  (190 shorter events, 102.0 us)
Async XLA Ops:
  7.2 147.0 %all-gather.5.cloned.1.call-start = ((), (), s32[]{:S(2)}) async-start(), calls=%async_computation.2 | async-start | bytes 1310720 | tf_op jit(solution)/shard_map/all_gather | solution.py:291
  7.9 159.8 %all-gather.7.cloned.1.call-start = ((), (), s32[]{:S(2)}) async-start(), calls=%async_computation.4 | async-start | bytes 1310720 | tf_op jit(solution)/shard_map/all_gather | solution.py:292
  9.3 32.1 %collective-permute-start = (bf16[32,16,128]{2,1,0:T(8,128)(2,1)S(1)}, bf16[32,16,128]{2,1,0:T(8,128)(2,1)S(1)}, u32[]{:S(2)}, u32[]{:S(2)}) collective-permute-start(bf16[32,16,128]{2,1,0:T(8,128)(2,1)S(1)} %get-tuple-element.28), channel_id=1, source_target_pairs={{0,4},{4,0},{8,12},{12,8},{16,20},{20,16},{24,28},{28,24},{1,5},{5... | collective-permute-start | bytes 393224 | tf_op jit(solution)/shard_map/ppermute | solution.py:301
  12.3 29.2 %collective-permute-start.1 = (bf16[32,16,128]{2,1,0:T(8,128)(2,1)S(1)}, bf16[32,16,128]{2,1,0:T(8,128)(2,1)S(1)}, u32[]{:S(2)}, u32[]{:S(2)}) collective-permute-start(bf16[32,16,128]{2,1,0:T(8,128)(2,1)S(1)} %get-tuple-element.29), channel_id=1, source_target_pairs={{0,8},{4,12},{8,0},{12,4},{16,24},{20,28},{24,16},{28,20},{1,9},{5... | collective-permute-start | bytes 393224 | tf_op jit(solution)/shard_map/ppermute | solution.py:301
  13.9 30.6 %collective-permute-start.2 = (bf16[32,16,128]{2,1,0:T(8,128)(2,1)S(1)}, bf16[32,16,128]{2,1,0:T(8,128)(2,1)S(1)}, u32[]{:S(2)}, u32[]{:S(2)}) collective-permute-start(bf16[32,16,128]{2,1,0:T(8,128)(2,1)S(1)} %get-tuple-element.30), channel_id=1, source_target_pairs={{0,12},{4,8},{8,4},{12,0},{16,28},{20,24},{24,20},{28,16},{1,13},{... | collective-permute-start | bytes 393224 | tf_op jit(solution)/shard_map/ppermute | solution.py:301
  13.9 32.9 %collective-permute-start.3 = (bf16[32,16,128]{2,1,0:T(8,128)(2,1)S(1)}, bf16[32,16,128]{2,1,0:T(8,128)(2,1)S(1)}, u32[]{:S(2)}, u32[]{:S(2)}) collective-permute-start(bf16[32,16,128]{2,1,0:T(8,128)(2,1)S(1)} %get-tuple-element.31), channel_id=1, source_target_pairs={{0,16},{4,20},{8,24},{12,28},{16,0},{20,4},{24,8},{28,12},{1,17},{... | collective-permute-start | bytes 393224 | tf_op jit(solution)/shard_map/ppermute | solution.py:301
  16.9 29.9 %collective-permute-start.4 = (bf16[32,16,128]{2,1,0:T(8,128)(2,1)S(1)}, bf16[32,16,128]{2,1,0:T(8,128)(2,1)S(1)}, u32[]{:S(2)}, u32[]{:S(2)}) collective-permute-start(bf16[32,16,128]{2,1,0:T(8,128)(2,1)S(1)} %get-tuple-element.32), channel_id=1, source_target_pairs={{0,20},{4,16},{8,28},{12,24},{16,4},{20,0},{24,12},{28,8},{1,21},{... | collective-permute-start | bytes 393224 | tf_op jit(solution)/shard_map/ppermute | solution.py:301
  41.5 10.2 %collective-permute-start.6 = (bf16[32,16,128]{2,1,0:T(8,128)(2,1)S(1)}, bf16[32,16,128]{2,1,0:T(8,128)(2,1)S(1)}, u32[]{:S(2)}, u32[]{:S(2)}) collective-permute-start(bf16[32,16,128]{2,1,0:T(8,128)(2,1)S(1)} %get-tuple-element.34), channel_id=1, source_target_pairs={{0,28},{4,24},{8,20},{12,16},{16,12},{20,8},{24,4},{28,0},{1,29},{... | collective-permute-start | bytes 393224 | tf_op jit(solution)/shard_map/ppermute | solution.py:301
  44.5 12.1 %collective-permute-start.21 = (bf16[32,16,128]{2,1,0:T(8,128)(2,1)S(1)}, bf16[32,16,128]{2,1,0:T(8,128)(2,1)S(1)}, u32[]{:S(2)}, u32[]{:S(2)}) collective-permute-start(bf16[32,16,128]{2,1,0:T(8,128)(2,1)S(1)} %get-tuple-element.39), channel_id=1, source_target_pairs={{0,4},{4,0},{8,12},{12,8},{16,20},{20,16},{24,28},{28,24},{1,5},{5... | collective-permute-start | bytes 393224 | tf_op jit(solution)/shard_map/ppermute | solution.py:301
  46.8 13.6 %collective-permute-start.22 = (bf16[32,16,128]{2,1,0:T(8,128)(2,1)S(1)}, bf16[32,16,128]{2,1,0:T(8,128)(2,1)S(1)}, u32[]{:S(2)}, u32[]{:S(2)}) collective-permute-start(bf16[32,16,128]{2,1,0:T(8,128)(2,1)S(1)} %get-tuple-element.40), channel_id=1, source_target_pairs={{0,8},{4,12},{8,0},{12,4},{16,24},{20,28},{24,16},{28,20},{1,9},{5... | collective-permute-start | bytes 393224 | tf_op jit(solution)/shard_map/ppermute | solution.py:301
  46.8 17.5 %collective-permute-start.23 = (bf16[32,16,128]{2,1,0:T(8,128)(2,1)S(1)}, bf16[32,16,128]{2,1,0:T(8,128)(2,1)S(1)}, u32[]{:S(2)}, u32[]{:S(2)}) collective-permute-start(bf16[32,16,128]{2,1,0:T(8,128)(2,1)S(1)} %get-tuple-element.41), channel_id=1, source_target_pairs={{0,12},{4,8},{8,4},{12,0},{16,28},{20,24},{24,20},{28,16},{1,13},{... | collective-permute-start | bytes 393224 | tf_op jit(solution)/shard_map/ppermute | solution.py:301
  49.8 14.5 %collective-permute-start.24 = (bf16[32,16,128]{2,1,0:T(8,128)(2,1)S(1)}, bf16[32,16,128]{2,1,0:T(8,128)(2,1)S(1)}, u32[]{:S(2)}, u32[]{:S(2)}) collective-permute-start(bf16[32,16,128]{2,1,0:T(8,128)(2,1)S(1)} %get-tuple-element.42), channel_id=1, source_target_pairs={{0,16},{4,20},{8,24},{12,28},{16,0},{20,4},{24,8},{28,12},{1,17},{... | collective-permute-start | bytes 393224 | tf_op jit(solution)/shard_map/ppermute | solution.py:301
  51.8 17.9 %collective-permute-start.25 = (bf16[32,16,128]{2,1,0:T(8,128)(2,1)S(1)}, bf16[32,16,128]{2,1,0:T(8,128)(2,1)S(1)}, u32[]{:S(2)}, u32[]{:S(2)}) collective-permute-start(bf16[32,16,128]{2,1,0:T(8,128)(2,1)S(1)} %get-tuple-element.43), channel_id=1, source_target_pairs={{0,20},{4,16},{8,28},{12,24},{16,4},{20,0},{24,12},{28,8},{1,21},{... | collective-permute-start | bytes 393224 | tf_op jit(solution)/shard_map/ppermute | solution.py:301
  56.6 13.1 %collective-permute-start.26 = (bf16[32,16,128]{2,1,0:T(8,128)(2,1)S(1)}, bf16[32,16,128]{2,1,0:T(8,128)(2,1)S(1)}, u32[]{:S(2)}, u32[]{:S(2)}) collective-permute-start(bf16[32,16,128]{2,1,0:T(8,128)(2,1)S(1)} %get-tuple-element.44), channel_id=1, source_target_pairs={{0,24},{4,28},{8,16},{12,20},{16,8},{20,12},{24,0},{28,4},{1,25},{... | collective-permute-start | bytes 393224 | tf_op jit(solution)/shard_map/ppermute | solution.py:301
  64.3 12.4 %collective-permute-start.7 = (bf16[64,16,128]{2,1,0:T(8,128)(2,1)S(1)}, bf16[64,16,128]{2,1,0:T(8,128)(2,1)S(1)}, u32[]{:S(2)}, u32[]{:S(2)}) collective-permute-start(bf16[64,16,128]{2,1,0:T(8,128)(2,1)S(1)} %get-tuple-element.35.refs_0_), channel_id=1, source_target_pairs={{0,8},{8,16},{16,24},{24,28},{28,20},{20,12},{12,4},{4,0},{1,9},{9... | collective-permute-start | bytes 786440 | tf_op jit(solution)/shard_map/ppermute | solution.py:308
  64.4 14.4 %collective-permute-start.14 = (bf16[64,16,128]{2,1,0:T(8,128)(2,1)S(1)}, bf16[64,16,128]{2,1,0:T(8,128)(2,1)S(1)}, u32[]{:S(2)}, u32[]{:S(2)}) collective-permute-start(bf16[64,16,128]{2,1,0:T(8,128)(2,1)S(1)} %get-tuple-element.36.refs_8_), channel_id=1, source_target_pairs={{8,0},{16,8},{24,16},{28,24},{20,28},{12,20},{4,12},{0,4},{9,1},{1... | collective-permute-start | bytes 786440 | tf_op jit(solution)/shard_map/ppermute | solution.py:308
  70.5 13.0 %collective-permute-start.28 = (bf16[64,16,128]{2,1,0:T(8,128)(2,1)S(1)}, bf16[64,16,128]{2,1,0:T(8,128)(2,1)S(1)}, u32[]{:S(2)}, u32[]{:S(2)}) collective-permute-start(bf16[64,16,128]{2,1,0:T(8,128)(2,1)S(1)} %get-tuple-element.46.refs_0_), channel_id=1, source_target_pairs={{0,8},{8,16},{16,24},{24,28},{28,20},{20,12},{12,4},{4,0},{1,9},{9... | collective-permute-start | bytes 786440 | tf_op jit(solution)/shard_map/ppermute | solution.py:308
  76.7 12.4 %collective-permute-start.8 = (bf16[64,16,128]{2,1,0:T(8,128)(2,1)S(1)}, bf16[64,16,128]{2,1,0:T(8,128)(2,1)S(1)}, u32[]{:S(2)}, u32[]{:S(2)}) collective-permute-start(bf16[64,16,128]{2,1,0:T(8,128)(2,1)S(1)} %collective-permute-done.7.refs_1_), channel_id=1, source_target_pairs={{0,8},{8,16},{16,24},{24,28},{28,20},{20,12},{12,4},{4,0},{1,9},{9... | collective-permute-start | bytes 786440 | tf_op jit(solution)/shard_map/ppermute | solution.py:308
  78.8 12.7 %collective-permute-start.15 = (bf16[64,16,128]{2,1,0:T(8,128)(2,1)S(1)}, bf16[64,16,128]{2,1,0:T(8,128)(2,1)S(1)}, u32[]{:S(2)}, u32[]{:S(2)}) collective-permute-start(bf16[64,16,128]{2,1,0:T(8,128)(2,1)S(1)} %collective-permute-done.14.refs_9_), channel_id=1, source_target_pairs={{8,0},{16,8},{24,16},{28,24},{20,28},{12,20},{4,12},{0,4},{9,1},{1... | collective-permute-start | bytes 786440 | tf_op jit(solution)/shard_map/ppermute | solution.py:308
  83.5 11.2 %collective-permute-start.29 = (bf16[64,16,128]{2,1,0:T(8,128)(2,1)S(1)}, bf16[64,16,128]{2,1,0:T(8,128)(2,1)S(1)}, u32[]{:S(2)}, u32[]{:S(2)}) collective-permute-start(bf16[64,16,128]{2,1,0:T(8,128)(2,1)S(1)} %collective-permute-done.28.refs_1_), channel_id=1, source_target_pairs={{0,8},{8,16},{16,24},{24,28},{28,20},{20,12},{12,4},{4,0},{1,9},{9... | collective-permute-start | bytes 786440 | tf_op jit(solution)/shard_map/ppermute | solution.py:308
  85.9 11.2 %collective-permute-start.36 = (bf16[64,16,128]{2,1,0:T(8,128)(2,1)S(1)}, bf16[64,16,128]{2,1,0:T(8,128)(2,1)S(1)}, u32[]{:S(2)}, u32[]{:S(2)}) collective-permute-start(bf16[64,16,128]{2,1,0:T(8,128)(2,1)S(1)} %collective-permute-done.35.refs_9_), channel_id=1, source_target_pairs={{8,0},{16,8},{24,16},{28,24},{20,28},{12,20},{4,12},{0,4},{9,1},{1... | collective-permute-start | bytes 786440 | tf_op jit(solution)/shard_map/ppermute | solution.py:308
  89.1 11.0 %collective-permute-start.9 = (bf16[64,16,128]{2,1,0:T(8,128)(2,1)S(1)}, bf16[64,16,128]{2,1,0:T(8,128)(2,1)}, u32[]{:S(2)}, u32[]{:S(2)}) collective-permute-start(bf16[64,16,128]{2,1,0:T(8,128)(2,1)S(1)} %collective-permute-done.8.refs_2_), channel_id=1, source_target_pairs={{0,8},{8,16},{16,24},{24,28},{28,20},{20,12},{12,4},{4,0},{1,9},{9... | collective-permute-start | bytes 786440 | tf_op jit(solution)/shard_map/ppermute | solution.py:308
  91.6 11.2 %collective-permute-start.16 = (bf16[64,16,128]{2,1,0:T(8,128)(2,1)S(1)}, bf16[64,16,128]{2,1,0:T(8,128)(2,1)}, u32[]{:S(2)}, u32[]{:S(2)}) collective-permute-start(bf16[64,16,128]{2,1,0:T(8,128)(2,1)S(1)} %collective-permute-done.15.refs_10_), channel_id=1, source_target_pairs={{8,0},{16,8},{24,16},{28,24},{20,28},{12,20},{4,12},{0,4},{9,1},{1... | collective-permute-start | bytes 786440 | tf_op jit(solution)/shard_map/ppermute | solution.py:308
  94.7 11.0 %collective-permute-start.30 = (bf16[64,16,128]{2,1,0:T(8,128)(2,1)S(1)}, bf16[64,16,128]{2,1,0:T(8,128)(2,1)S(1)}, u32[]{:S(2)}, u32[]{:S(2)}) collective-permute-start(bf16[64,16,128]{2,1,0:T(8,128)(2,1)S(1)} %collective-permute-done.29.refs_2_), channel_id=1, source_target_pairs={{0,8},{8,16},{16,24},{24,28},{28,20},{20,12},{12,4},{4,0},{1,9},{9... | collective-permute-start | bytes 786440 | tf_op jit(solution)/shard_map/ppermute | solution.py:308
  97.2 11.0 %collective-permute-start.37 = (bf16[64,16,128]{2,1,0:T(8,128)(2,1)S(1)}, bf16[64,16,128]{2,1,0:T(8,128)(2,1)}, u32[]{:S(2)}, u32[]{:S(2)}) collective-permute-start(bf16[64,16,128]{2,1,0:T(8,128)(2,1)S(1)} %collective-permute-done.36.refs_10_), channel_id=1, source_target_pairs={{8,0},{16,8},{24,16},{28,24},{20,28},{12,20},{4,12},{0,4},{9,1},{1... | collective-permute-start | bytes 786440 | tf_op jit(solution)/shard_map/ppermute | solution.py:308
  97.2 186.6 %reduce-scatter.5.cloned.1.call-start = ((), (), s32[]{:S(2)}) async-start(), calls=%async_computation.5 | async-start | bytes 1310720 | tf_op jit(solution)/shard_map/reduce_scatter | solution.py:374
  100.1 11.2 %collective-permute-start.10 = (bf16[64,16,128]{2,1,0:T(8,128)(2,1)}, bf16[64,16,128]{2,1,0:T(8,128)(2,1)}, u32[]{:S(2)}, u32[]{:S(2)}) collective-permute-start(bf16[64,16,128]{2,1,0:T(8,128)(2,1)} %collective-permute-done.9.refs_3_), channel_id=1, source_target_pairs={{0,8},{8,16},{16,24},{24,28},{28,20},{20,12},{12,4},{4,0},{1,9},{9... | collective-permute-start | bytes 786440 | tf_op jit(solution)/shard_map/ppermute | solution.py:308
  102.7 11.1 %collective-permute-start.17 = (bf16[64,16,128]{2,1,0:T(8,128)(2,1)}, bf16[64,16,128]{2,1,0:T(8,128)(2,1)}, u32[]{:S(2)}, u32[]{:S(2)}) collective-permute-start(bf16[64,16,128]{2,1,0:T(8,128)(2,1)} %collective-permute-done.16.refs_11_), channel_id=1, source_target_pairs={{8,0},{16,8},{24,16},{28,24},{20,28},{12,20},{4,12},{0,4},{9,1},{1... | collective-permute-start | bytes 786440 | tf_op jit(solution)/shard_map/ppermute | solution.py:308
  105.7 11.1 %collective-permute-start.31 = (bf16[64,16,128]{2,1,0:T(8,128)(2,1)S(1)}, bf16[64,16,128]{2,1,0:T(8,128)(2,1)}, u32[]{:S(2)}, u32[]{:S(2)}) collective-permute-start(bf16[64,16,128]{2,1,0:T(8,128)(2,1)S(1)} %collective-permute-done.30.refs_3_), channel_id=1, source_target_pairs={{0,8},{8,16},{16,24},{24,28},{28,20},{20,12},{12,4},{4,0},{1,9},{9... | collective-permute-start | bytes 786440 | tf_op jit(solution)/shard_map/ppermute | solution.py:308
  108.2 11.2 %collective-permute-start.38 = (bf16[64,16,128]{2,1,0:T(8,128)(2,1)}, bf16[64,16,128]{2,1,0:T(8,128)(2,1)}, u32[]{:S(2)}, u32[]{:S(2)}) collective-permute-start(bf16[64,16,128]{2,1,0:T(8,128)(2,1)} %collective-permute-done.37.refs_11_), channel_id=1, source_target_pairs={{8,0},{16,8},{24,16},{28,24},{20,28},{12,20},{4,12},{0,4},{9,1},{1... | collective-permute-start | bytes 786440 | tf_op jit(solution)/shard_map/ppermute | solution.py:308
  111.4 11.2 %collective-permute-start.11 = (bf16[64,16,128]{2,1,0:T(8,128)(2,1)}, bf16[64,16,128]{2,1,0:T(8,128)(2,1)}, u32[]{:S(2)}, u32[]{:S(2)}) collective-permute-start(bf16[64,16,128]{2,1,0:T(8,128)(2,1)} %collective-permute-done.10.refs_4_), channel_id=1, source_target_pairs={{0,8},{8,16},{16,24},{24,28},{28,20},{20,12},{12,4},{4,0},{1,9},{9... | collective-permute-start | bytes 786440 | tf_op jit(solution)/shard_map/ppermute | solution.py:308
  113.8 11.2 %collective-permute-start.18 = (bf16[64,16,128]{2,1,0:T(8,128)(2,1)}, bf16[64,16,128]{2,1,0:T(8,128)(2,1)}, u32[]{:S(2)}, u32[]{:S(2)}) collective-permute-start(bf16[64,16,128]{2,1,0:T(8,128)(2,1)} %collective-permute-done.17.refs_12_), channel_id=1, source_target_pairs={{8,0},{16,8},{24,16},{28,24},{20,28},{12,20},{4,12},{0,4},{9,1},{1... | collective-permute-start | bytes 786440 | tf_op jit(solution)/shard_map/ppermute | solution.py:308
  116.9 11.3 %collective-permute-start.32 = (bf16[64,16,128]{2,1,0:T(8,128)(2,1)}, bf16[64,16,128]{2,1,0:T(8,128)(2,1)}, u32[]{:S(2)}, u32[]{:S(2)}) collective-permute-start(bf16[64,16,128]{2,1,0:T(8,128)(2,1)} %collective-permute-done.31.refs_4_), channel_id=1, source_target_pairs={{0,8},{8,16},{16,24},{24,28},{28,20},{20,12},{12,4},{4,0},{1,9},{9... | collective-permute-start | bytes 786440 | tf_op jit(solution)/shard_map/ppermute | solution.py:308
  119.5 11.2 %collective-permute-start.39 = (bf16[64,16,128]{2,1,0:T(8,128)(2,1)}, bf16[64,16,128]{2,1,0:T(8,128)(2,1)}, u32[]{:S(2)}, u32[]{:S(2)}) collective-permute-start(bf16[64,16,128]{2,1,0:T(8,128)(2,1)} %collective-permute-done.38.refs_12_), channel_id=1, source_target_pairs={{8,0},{16,8},{24,16},{28,24},{20,28},{12,20},{4,12},{0,4},{9,1},{1... | collective-permute-start | bytes 786440 | tf_op jit(solution)/shard_map/ppermute | solution.py:308
  122.6 11.2 %collective-permute-start.12 = (bf16[64,16,128]{2,1,0:T(8,128)(2,1)}, bf16[64,16,128]{2,1,0:T(8,128)(2,1)S(1)}, u32[]{:S(2)}, u32[]{:S(2)}) collective-permute-start(bf16[64,16,128]{2,1,0:T(8,128)(2,1)} %collective-permute-done.11.refs_5_), channel_id=1, source_target_pairs={{0,8},{8,16},{16,24},{24,28},{28,20},{20,12},{12,4},{4,0},{1,9},{9... | collective-permute-start | bytes 786440 | tf_op jit(solution)/shard_map/ppermute | solution.py:308
  125.1 11.2 %collective-permute-start.19 = (bf16[64,16,128]{2,1,0:T(8,128)(2,1)}, bf16[64,16,128]{2,1,0:T(8,128)(2,1)S(1)}, u32[]{:S(2)}, u32[]{:S(2)}) collective-permute-start(bf16[64,16,128]{2,1,0:T(8,128)(2,1)} %collective-permute-done.18.refs_13_), channel_id=1, source_target_pairs={{8,0},{16,8},{24,16},{28,24},{20,28},{12,20},{4,12},{0,4},{9,1},{1... | collective-permute-start | bytes 786440 | tf_op jit(solution)/shard_map/ppermute | solution.py:308
  128.2 11.2 %collective-permute-start.33 = (bf16[64,16,128]{2,1,0:T(8,128)(2,1)}, bf16[64,16,128]{2,1,0:T(8,128)(2,1)S(1)}, u32[]{:S(2)}, u32[]{:S(2)}) collective-permute-start(bf16[64,16,128]{2,1,0:T(8,128)(2,1)} %collective-permute-done.32.refs_5_), channel_id=1, source_target_pairs={{0,8},{8,16},{16,24},{24,28},{28,20},{20,12},{12,4},{4,0},{1,9},{9... | collective-permute-start | bytes 786440 | tf_op jit(solution)/shard_map/ppermute | solution.py:308
  130.7 11.2 %collective-permute-start.40 = (bf16[64,16,128]{2,1,0:T(8,128)(2,1)}, bf16[64,16,128]{2,1,0:T(8,128)(2,1)S(1)}, u32[]{:S(2)}, u32[]{:S(2)}) collective-permute-start(bf16[64,16,128]{2,1,0:T(8,128)(2,1)} %collective-permute-done.39.refs_13_), channel_id=1, source_target_pairs={{8,0},{16,8},{24,16},{28,24},{20,28},{12,20},{4,12},{0,4},{9,1},{1... | collective-permute-start | bytes 786440 | tf_op jit(solution)/shard_map/ppermute | solution.py:308
  133.8 9.9 %collective-permute-start.13 = (bf16[64,16,128]{2,1,0:T(8,128)(2,1)S(1)}, bf16[64,16,128]{2,1,0:T(8,128)(2,1)S(1)}, u32[]{:S(2)}, u32[]{:S(2)}) collective-permute-start(bf16[64,16,128]{2,1,0:T(8,128)(2,1)S(1)} %collective-permute-done.12.refs_6_), channel_id=1, source_target_pairs={{0,8},{8,16},{16,24},{24,28},{28,20},{20,12},{12,4},{4,0},{1,9},{9... | collective-permute-start | bytes 786440 | tf_op jit(solution)/shard_map/ppermute | solution.py:308
  136.2 10.2 %collective-permute-start.20 = (bf16[64,16,128]{2,1,0:T(8,128)(2,1)S(1)}, bf16[64,16,128]{2,1,0:T(8,128)(2,1)S(1)}, u32[]{:S(2)}, u32[]{:S(2)}) collective-permute-start(bf16[64,16,128]{2,1,0:T(8,128)(2,1)S(1)} %collective-permute-done.19.refs_14_), channel_id=1, source_target_pairs={{8,0},{16,8},{24,16},{28,24},{20,28},{12,20},{4,12},{0,4},{9,1},{1... | collective-permute-start | bytes 786440 | tf_op jit(solution)/shard_map/ppermute | solution.py:308
  139.5 10.9 %collective-permute-start.34 = (bf16[64,16,128]{2,1,0:T(8,128)(2,1)S(1)}, bf16[64,16,128]{2,1,0:T(8,128)(2,1)S(1)}, u32[]{:S(2)}, u32[]{:S(2)}) collective-permute-start(bf16[64,16,128]{2,1,0:T(8,128)(2,1)S(1)} %collective-permute-done.33.refs_6_), channel_id=1, source_target_pairs={{0,8},{8,16},{16,24},{24,28},{28,20},{20,12},{12,4},{4,0},{1,9},{9... | collective-permute-start | bytes 786440 | tf_op jit(solution)/shard_map/ppermute | solution.py:308
  184.1 99.8 %reduce-scatter.3.cloned.1.call-start = ((), (), s32[]{:S(2)}) async-start(), calls=%async_computation.3 | async-start | bytes 1310720 | tf_op jit(solution)/shard_map/reduce_scatter | solution.py:373
  192.3 18.7 %collective-permute-start.42 = (bf16[16,64,128]{2,1,0:T(8,128)(2,1)S(1)}, bf16[16,64,128]{2,1,0:T(8,128)(2,1)S(1)}, u32[]{:S(2)}, u32[]{:S(2)}) collective-permute-start(bf16[16,64,128]{2,1,0:T(8,128)(2,1)S(1)} %get-tuple-element.80), channel_id=1, source_target_pairs={{0,8},{8,16},{16,24},{24,28},{28,20},{20,12},{12,4},{4,0},{1,9},{9... | collective-permute-start | bytes 786440 | tf_op jit(solution)/shard_map/ppermute | solution.py:238
  195.6 15.3 %collective-permute-start.49 = (bf16[16,64,128]{2,1,0:T(8,128)(2,1)S(1)}, bf16[16,64,128]{2,1,0:T(8,128)(2,1)}, u32[]{:S(2)}, u32[]{:S(2)}) collective-permute-start(bf16[16,64,128]{2,1,0:T(8,128)(2,1)S(1)} %get-tuple-element.81), channel_id=1, source_target_pairs={{8,0},{16,8},{24,16},{28,24},{20,28},{12,20},{4,12},{0,4},{9,1},{1... | collective-permute-start | bytes 786440 | tf_op jit(solution)/shard_map/ppermute | solution.py:239
  203.3 11.2 %collective-permute-start.56 = (bf16[16,64,128]{2,1,0:T(8,128)(2,1)S(1)}, bf16[16,64,128]{2,1,0:T(8,128)(2,1)S(1)}, u32[]{:S(2)}, u32[]{:S(2)}) collective-permute-start(bf16[16,64,128]{2,1,0:T(8,128)(2,1)S(1)} %get-tuple-element.78), channel_id=1, source_target_pairs={{0,8},{8,16},{16,24},{24,28},{28,20},{20,12},{12,4},{4,0},{1,9},{9... | collective-permute-start | bytes 786440 | tf_op jit(solution)/shard_map/ppermute | solution.py:238
  215.8 10.7 %collective-permute-start.57 = (bf16[16,64,128]{2,1,0:T(8,128)(2,1)S(1)}, bf16[16,64,128]{2,1,0:T(8,128)(2,1)S(1)}, u32[]{:S(2)}, u32[]{:S(2)}) collective-permute-start(bf16[16,64,128]{2,1,0:T(8,128)(2,1)S(1)} %get-tuple-element.62), channel_id=1, source_target_pairs={{0,8},{8,16},{16,24},{24,28},{28,20},{20,12},{12,4},{4,0},{1,9},{9... | collective-permute-start | bytes 786440 | tf_op jit(solution)/shard_map/ppermute | solution.py:238
  217.9 10.6 %collective-permute-start.64 = (bf16[16,64,128]{2,1,0:T(8,128)(2,1)S(1)}, bf16[16,64,128]{2,1,0:T(8,128)(2,1)S(1)}, u32[]{:S(2)}, u32[]{:S(2)}) collective-permute-start(bf16[16,64,128]{2,1,0:T(8,128)(2,1)S(1)} %get-tuple-element.63), channel_id=1, source_target_pairs={{8,0},{16,8},{24,16},{28,24},{20,28},{12,20},{4,12},{0,4},{9,1},{1... | collective-permute-start | bytes 786440 | tf_op jit(solution)/shard_map/ppermute | solution.py:239
  235.6 9.8 %collective-permute-start.52 = (bf16[16,64,128]{2,1,0:T(8,128)(2,1)S(1)}, bf16[16,64,128]{2,1,0:T(8,128)(2,1)S(1)}, u32[]{:S(2)}, u32[]{:S(2)}) collective-permute-start(bf16[16,64,128]{2,1,0:T(8,128)(2,1)S(1)} %get-tuple-element.73), channel_id=1, source_target_pairs={{8,0},{16,8},{24,16},{28,24},{20,28},{12,20},{4,12},{0,4},{9,1},{1... | collective-permute-start | bytes 786440 | tf_op jit(solution)/shard_map/ppermute | solution.py:239
  (44 other events, 279.1 us)
Sparse Core Ops, SparseCore 0:
  9.6 19.4 all-gather.4
  97.3 17.0 all-gather.6
  184.2 25.6 reduce-scatter.4
  213.0 24.8 reduce-scatter.2

commit v2 on v0

v2 whole, which is shorter than its diff:
```python
import functools
import math

import jax
import jax.numpy as jnp
from jax import lax
from jax.experimental import pallas as pl
from jax.experimental.pallas import tpu as pltpu
from jax.sharding import PartitionSpec as P

FF = 16384
BLK = 128
PACK = 16
VMEM_LIMIT = 56 << 20

gelu_root = 0.7978845608028654
gelu_cubic = 0.044715

SMEM_SPEC = pl.BlockSpec(memory_space=pltpu.SMEM)
ANY_SPEC = pl.BlockSpec(memory_space=pl.ANY)


def ring_order(devices):
    evens = list(range(0, devices, 2))
    odds = list(range(1, devices, 2))
    return evens + odds[::-1]


def ring_pairs(devices):
    order = ring_order(devices)
    ahead = [(order[i], order[(i + 1) % devices]) for i in range(devices)]
    behind = [(b, a) for a, b in ahead]
    return ahead, behind


def shape(dims, dtype):
    return jax.ShapeDtypeStruct(tuple(dims), dtype)


def dot(a, b, ca, cb):
    return lax.dot_general(a, b, (((ca,), (cb,)), ((), ())), preferred_element_type=jnp.float32)


def unroll_of(count):
    return math.gcd(count, 8)


class Whole:
    sides = 1

    def __init__(self, array):
        self.arrays, self.tables = [array], []
        self.held = pltpu.VMEM(array.shape, array.dtype)

    def copies(self, tables, refs, held, sems):
        return [pltpu.make_async_copy(refs[0], held, sems.at[0])]


class Parts:
    def __init__(self, arrays, slots):
        self.arrays, self.tables, self.slots = list(arrays), [], slots
        first = arrays[0]
        self.held = pltpu.VMEM((len(arrays) * slots, *first.shape[1:]), first.dtype)

    def copies(self, tables, refs, held, sems):
        slots = self.slots
        return [
            pltpu.make_async_copy(ref.at[pl.ds(0, slots)], held.at[pl.ds(i * slots, slots)], sems.at[i])
            for i, ref in enumerate(refs)
        ]


class Joined:
    sides = 2

    def __init__(self, first, second, tables):
        self.arrays, self.tables = [*first, *second], list(tables)
        half = first[0].shape[0]
        self.held = pltpu.VMEM((2 * half, BLK, BLK), first[0].dtype)

    def copies(self, tables, refs, held, sems):
        half, piece, _ = refs[0].shape
        out = []
        for i, ref in enumerate(refs):
            side, j = divmod(i, len(refs) // 2)
            start = pl.multiple_of(tables[side][j] * piece, piece)
            to = held.at[pl.ds(side * half, half), pl.ds(start, piece), :]
            out.append(pltpu.make_async_copy(ref, to, sems.at[i]))
        return out


def run(kernel, small, items, outs, scratch=(), flops=0, nbytes=0, chunks=None):
    tables = [t for item in items for t in item.tables]
    arrays = [x for item in items for x in item.arrays]
    chunks = chunks or [0] * len(outs)

    def body(*refs):
        refs = list(refs)

        def take(n):
            taken = refs[:n]
            del refs[:n]
            return taken

        small_refs = take(len(small))
        table_refs = [take(len(item.tables)) for item in items]
        array_refs = [take(len(item.arrays)) for item in items]
        out_refs = take(len(outs))
        held_refs = take(len(items))
        result_refs = take(len(outs))
        scratch_refs = take(len(scratch))
        in_sems, out_sems = refs[: len(items)], refs[len(items) :]
        fetches = [
            item.copies(t, x, held, sems)
            for item, t, x, held, sems in zip(items, table_refs, array_refs, held_refs, in_sems, strict=True)
        ]
        for copies in fetches:
            for copy in copies:
                copy.start()

        def need(*which, part=(0, 1)):
            for i in which:
                size = len(fetches[i]) // part[1]
                for copy in fetches[i][part[0] * size : (part[0] + 1) * size]:
                    copy.wait()

        sent = {}

        def send(i, q=None):
            result, out, sem = result_refs[i], out_refs[i], out_sems[i].at[q or 0]
            if q is not None:
                result, out = result.at[q], out.at[q]
            sent[i, q] = pltpu.make_async_copy(result, out, sem)
            sent[i, q].start()

        kernel(need, send, *small_refs, *held_refs, *result_refs, *scratch_refs)
        for i, count in enumerate(chunks):
            for q in range(count) if count else [None]:
                if (i, q) not in sent:
                    send(i, q)
        for copy in sent.values():
            copy.wait()

    return pl.pallas_call(
        body,
        out_shape=list(outs),
        in_specs=[SMEM_SPEC] * (len(small) + len(tables)) + [ANY_SPEC] * len(arrays),
        out_specs=[ANY_SPEC] * len(outs),
        scratch_shapes=[
            *(item.held for item in items),
            *(pltpu.VMEM(x.shape, x.dtype) for x in outs),
            *scratch,
            *(pltpu.SemaphoreType.DMA((len(item.arrays),)) for item in items),
            *(pltpu.SemaphoreType.DMA((max(1, count),)) for count in chunks),
        ],
        compiler_params=pltpu.CompilerParams(vmem_limit_bytes=VMEM_LIMIT),
        cost_estimate=pl.CostEstimate(flops=flops, bytes_accessed=nbytes, transcendentals=0),
    )(*small, *tables, *arrays)


def split_blocks(me, up, down, note, devices):
    slots = up.shape[0]
    piece = BLK // devices

    def kernel(need, send, me_ref, up_ref, down_ref, note_ref, *outs):
        need(0, 1, 2)
        for step, out in enumerate(outs):
            start = pl.multiple_of((me_ref[0] ^ step) * piece, piece)
            out[:slots] = up_ref[:, pl.ds(start, piece), :]
            out[slots : 2 * slots] = down_ref[:, pl.ds(start, piece), :]
            out[2 * slots] = note_ref[...]
            send(step)

    out = [shape((2 * slots + 1, piece, BLK), up.dtype)] * devices
    return run(kernel, [me], [Whole(up), Whole(down), Whole(note)], out, nbytes=8 * up.size)


def pack_pieces(pick, parts, slots, live):
    piece = parts[0].shape[1]
    half = live // 2
    unroll = unroll_of(half)

    def kernel(need, send, up_pick, down_pick, held, *outs):
        need(0)
        for which, picked in enumerate((up_pick, down_pick)):
            ahead, behind = outs[2 * which : 2 * which + 2]

            def body(i, carry, picked=picked, ahead=ahead, behind=behind):
                for u in range(unroll):
                    k = i * unroll + u
                    ahead[k] = held[picked[k]]
                    behind[k] = held[picked[half + k]]
                return carry

            lax.fori_loop(0, half // unroll, body, 0)
            send(2 * which)
            send(2 * which + 1)

    out = [shape((half, piece, BLK), parts[0].dtype)] * 4
    items = [Parts(parts, 2 * slots)]
    return run(kernel, [pick[0], pick[1]], items, out, nbytes=6 * len(parts) * slots * piece * BLK)


def lanes(ref, block):
    return ref[:, pl.ds(pl.multiple_of(block * BLK, BLK), BLK)]


def sum_blocks(acc, live, sides, target, term, fetch):
    acc[...] = jnp.zeros_like(acc)
    count = live // sides
    unroll = unroll_of(count)
    for side in range(sides):
        fetch(side)

        def body(i, carry, first=side * count):
            products = [term(first + i * unroll + u) for u in range(unroll)]
            for u in range(unroll):
                acc[target(first + i * unroll + u)] += products[u]
            return carry

        lax.fori_loop(0, count // unroll, body, 0)


def fetch_of(need, item, sides):
    return lambda side: need(item, part=(side, sides))


def down_terms(owner_ref, rows_ref, cols_ref, turned_ref, cot_ref, out_ref, send):
    devices, mean = out_ref.shape[:2]
    for q in range(devices):
        base = owner_ref[q] * mean
        for j in range(mean):
            row, col = rows_ref[base + j], cols_ref[base + j]
            out_ref[q, j] = dot(turned_ref[col], lanes(cot_ref, row), 1, 0).astype(jnp.bfloat16)
        send(q)


def up_terms(owner_ref, rows_ref, cols_ref, turned_ref, grad_ref, out_ref, send):
    devices, mean = out_ref.shape[:2]
    for q in range(devices):
        base = owner_ref[q] * mean
        for j in range(mean):
            row, col = rows_ref[base + j], cols_ref[base + j]
            turned = turned_ref[pl.ds(pl.multiple_of(row * BLK, BLK), BLK), :]
            out_ref[q, j] = dot(turned, grad_ref[col], 1, 0).astype(jnp.bfloat16)
        send(q)


def hidden_kernel(sides, need, send, owner, rows, cols, down_rows, down_cols, tok, w, cot, hid, slope, out, acc, turned):
    need(0)
    fetch = fetch_of(need, 1, sides)
    sum_blocks(acc, w.shape[0], sides, lambda k: cols[k], lambda k: dot(lanes(tok, rows[k]), w[k], 1, 0), fetch)

    def body(c, carry):
        values = acc[c]
        tanh = jnp.tanh(gelu_root * (values + gelu_cubic * values * values * values))
        hidden = 0.5 * values * (1.0 + tanh)
        hid[c] = hidden.astype(jnp.bfloat16)
        turned[c] = hidden.T.astype(jnp.bfloat16)
        slope[c] = 0.5 * (1.0 + tanh) + 0.5 * values * (1.0 - tanh * tanh) * gelu_root * (
            1.0 + 3.0 * gelu_cubic * values * values
        )
        return carry

    lax.fori_loop(0, acc.shape[0], body, 0)
    send(0)
    send(1)
    need(2)
    down_terms(owner, down_rows, down_cols, turned, cot, out, lambda q: send(2, q))


def grad_pre_kernel(sides, need, send, owner, rows, cols, up_rows, up_cols, cot, w, slope, tok_turned, grad, out, acc):
    need(0)
    fetch = fetch_of(need, 1, sides)
    sum_blocks(acc, w.shape[0], sides, lambda k: cols[k], lambda k: dot(lanes(cot, rows[k]), w[k], 1, 1), fetch)
    need(2)

    def body(c, carry):
        grad[c] = (acc[c] * slope[c]).astype(jnp.bfloat16)
        return carry

    lax.fori_loop(0, acc.shape[0], body, 0)
    send(0)
    need(3)
    up_terms(owner, up_rows, up_cols, tok_turned, grad, out, lambda q: send(1, q))


def width_kernel(contract, sides, need, send, rows, cols, x, w, out, acc):
    need(0)
    fetch = fetch_of(need, 1, sides)
    sum_blocks(acc, w.shape[0], sides, lambda k: rows[k], lambda k: dot(x[cols[k]], w[k], 1, contract), fetch)
    for r in range(acc.shape[0]):
        out[:, r * BLK : (r + 1) * BLK] = acc[r].astype(jnp.bfloat16)


def tie(value, *others):
    return lax.optimization_barrier((value, others))[0]


class RingSum:
    def __init__(self, parts, ahead, behind):
        self.parts, self.ahead, self.behind = parts, ahead, behind
        self.devices = parts.shape[0]
        self.done = 0
        self.run = (self.low(0), self.high((self.devices - 2) % self.devices))

    def low(self, q):
        return self.parts[q, :, : BLK // 2]

    def high(self, q):
        return self.parts[q, :, BLK // 2 :]

    def step(self, *after):
        self.done += 1
        last = self.done == self.devices - 1
        a, b = (x.astype(jnp.bfloat16) for x in self.run)
        if after:
            a, b = tie((a, b), *after)
        a = lax.ppermute(a, "dp", self.ahead)
        b = lax.ppermute(b, "dp", self.behind)
        a = a.astype(jnp.float32) + self.low(self.done).astype(jnp.float32)
        q = self.done if last else self.devices - 2 - self.done
        b = b.astype(jnp.float32) + self.high(q).astype(jnp.float32)
        if not last:
            a, b = a.astype(jnp.bfloat16), b.astype(jnp.bfloat16)
        self.run = (a, b)
        return self.run

    def steps_left(self):
        return self.devices - 1 - self.done

    def total(self):
        return jnp.concatenate(self.run, axis=1)


def tables(rows, cols, owners):
    _, devices, slots = rows.shape
    live = devices * (slots // 2)
    counts = jnp.sum((cols >= 0).astype(jnp.int32), axis=2)
    earlier = owners[None, :] < owners[:, None]
    offset = jnp.sum(jnp.where(earlier[None], counts[:, None, :], 0), axis=2)
    within = jnp.arange(live, dtype=jnp.int32)[None, :, None] - offset[:, None, :]
    held = (within >= 0) & (within < counts[:, None, :])
    base = jnp.arange(devices, dtype=jnp.int32) * slots
    pick = jnp.sum(jnp.where(held, within + base[None, None, :], 0), axis=2)
    every = jnp.arange(devices * slots, dtype=jnp.int32)
    chosen = every[None, None, :] == pick[:, :, None]
    at = [jnp.sum(jnp.where(chosen, x.reshape(2, 1, devices * slots), 0), axis=2) for x in (rows, cols)]
    return pick, at[0], at[1]


def shards(tokens, cotangent, up_blocks, up_place, down_blocks, down_place):
    devices = lax.axis_size("dp")
    me = lax.axis_index("dp")
    slots = up_place.shape[2]
    mean = slots // 2
    live = devices * mean
    group_blocks = FF // BLK // lax.axis_size("tensor")
    row_count = tokens.shape[0] * lax.axis_size("tensor")
    model_width = tokens.shape[1]
    model_blocks = model_width // BLK

    order = ring_order(devices)
    place = {d: i for i, d in enumerate(order)}
    ahead, behind = ring_pairs(devices)
    nav = jnp.array(
        [
            [
                [order[(place[d] - j) % devices] for j in range(devices)],
                [order[(place[d] + j) % devices] for j in range(devices)],
                [order[(place[d] - 1 - j) % devices] for j in range(devices)],
            ]
            for d in range(devices)
        ],
        jnp.int32,
    )[me]
    from_ahead, from_behind, owner = nav[0], nav[1], nav[2]
    index = jnp.arange(devices, dtype=jnp.int32)
    up_slots = up_blocks.reshape(slots, BLK, BLK)
    down_slots = down_blocks.reshape(slots, BLK, BLK)
    codes = jnp.stack([up_place.reshape(1, slots), down_place.reshape(1, slots)])

    flops = 2 * live * row_count * BLK * BLK * 4
    block_bytes = live * BLK * BLK * 2
    side = row_count * BLK
    group_acc = pltpu.VMEM((group_blocks, row_count, BLK), jnp.float32)
    model_acc = pltpu.VMEM((model_blocks, row_count, BLK), jnp.float32)

    group_cube = (group_blocks, row_count, BLK)
    terms_shape = shape((devices, mean, BLK, BLK), jnp.bfloat16)

    def hidden_of(rows, cols, tok, cot, up):
        outs = [shape(group_cube, jnp.bfloat16), shape(group_cube, jnp.float32), terms_shape]
        return run(
            functools.partial(hidden_kernel, up.sides),
            [owner, rows[0], cols[0], rows[1], cols[1]],
            [Whole(tok), up, Whole(cot)],
            outs,
            [group_acc, pltpu.VMEM((group_blocks, BLK, row_count), jnp.bfloat16)],
            2 * flops,
            2 * block_bytes + side * (4 * model_blocks + 6 * group_blocks),
            [0, 0, devices],
        )

    def grad_pre_of(rows, cols, cot, down, slope, tok_turned):
        return run(
            functools.partial(grad_pre_kernel, down.sides),
            [owner, rows[1], cols[1], rows[0], cols[0]],
            [Whole(cot), down, Whole(slope), Whole(tok_turned)],
            [shape(group_cube, jnp.bfloat16), terms_shape],
            [group_acc],
            2 * flops,
            2 * block_bytes + side * (4 * model_blocks + 6 * group_blocks),
            [0, devices],
        )

    def width(contract, rows, cols, x, weights):
        outs = [shape((row_count, model_width), jnp.bfloat16)]
        nbytes = block_bytes + side * (2 * model_blocks + 2 * group_blocks)
        kernel = functools.partial(width_kernel, contract, weights.sides)
        return run(kernel, [rows, cols], [Whole(x), weights], outs, [model_acc], flops, nbytes)[0]

    is_live = codes >= 0
    row_codes = jnp.where(is_live, codes // group_blocks, 0)
    col_codes = jnp.where(is_live, codes % group_blocks, -1)

    if BLK % (PACK * devices) == 0 and slots <= BLK:
        here = me.reshape(1).astype(jnp.int32)
        piece = BLK // devices

        note = jnp.concatenate([row_codes, col_codes]).reshape(4, slots).astype(jnp.bfloat16)
        note = jnp.pad(note, ((0, piece - 4), (0, BLK - slots)))
        messages = split_blocks(here, up_slots, down_slots, note, devices)
        parts = [messages[0]] + [
            lax.ppermute(messages[s], "dp", [(i, i ^ s) for i in range(devices)]) for s in range(1, devices)
        ]
        notes = jnp.stack([part[2 * slots, :4, :slots] for part in parts], axis=1).astype(jnp.int32)
        pick, rows, cols = tables(notes[:2], notes[2:], index ^ me)
        place_of = (pick // slots) * (2 * slots) + pick % slots
        pick = place_of + jnp.array([[0], [slots]], jnp.int32)

        tokens, cotangent = tie((tokens, cotangent), parts[1])
        tok = lax.all_gather(tokens, "tensor", axis=0, tiled=True)
        cot = lax.all_gather(cotangent, "tensor", axis=0, tiled=True)

        def onward(pair):
            return lax.ppermute(pair[0], "dp", ahead), lax.ppermute(pair[1], "dp", behind)

        def ring(pair):
            pairs = [pair]
            for _ in range(1, devices):
                pairs.append(onward(pairs[-1]))
            return Joined(*zip(*pairs, strict=True), (from_ahead, from_behind))

        packed = pack_pieces(pick, parts, slots, live)
        up, down = ring(packed[:2]), ring(packed[2:])
    else:

        def everywhere(x, axis):
            return lax.all_gather(x, "dp", axis=axis, tiled=True)

        pick, rows, cols = tables(everywhere(row_codes, 1), everywhere(col_codes, 1), index)
        tok = lax.all_gather(tokens, "tensor", axis=0, tiled=True)
        cot = lax.all_gather(cotangent, "tensor", axis=0, tiled=True)
        up = Whole(jnp.take(everywhere(up_slots, 0), pick[0], axis=0))
        down = Whole(jnp.take(everywhere(down_slots, 0), pick[1], axis=0))

    hid, slope, terms = hidden_of(rows, cols, tok, cot, up)
    down_sum = RingSum(terms, ahead, behind)
    down_sum.step()
    grad_pre, terms = grad_pre_of(rows, cols, tie(cot, down_sum.run), down, slope, tok.T)
    up_sum = RingSum(terms, ahead, behind)
    up_sum.step()
    out_part = width(0, rows[1], cols[1], tie(hid, up_sum.run), down)
    up_sum.step()
    in_part = width(1, rows[0], cols[0], tie(grad_pre, out_part, up_sum.run), up)
    outputs = lax.psum_scatter(out_part, "tensor", scatter_dimension=0, tiled=True)
    input_grads = lax.psum_scatter(in_part, "tensor", scatter_dimension=0, tiled=True)
    while down_sum.steps_left():
        down_sum.step()
    while up_sum.steps_left():
        up_sum.step()

    scale = 1.0 / math.sqrt(devices * row_count)
    grads_shape = (1, 1, mean, BLK, BLK)
    up_grads = (up_sum.total() * scale).reshape(grads_shape)
    down_grads = (down_sum.total() * scale).reshape(grads_shape)
    return (outputs, input_grads, up_grads, down_grads)


def solution(mesh):
    return jax.shard_map(
        shards,
        mesh=mesh,
        in_specs=(
            P(("dp", "tensor"), None),
            P(("dp", "tensor"), None),
            P("dp", "tensor", None, None, None),
            P("dp", "tensor", None),
            P("dp", "tensor", None, None, None),
            P("dp", "tensor", None),
        ),
        out_specs=(
            P(("dp", "tensor"), None),
            P(("dp", "tensor"), None),
            P("dp", "tensor", None, None, None),
            P("dp", "tensor", None, None, None),
        ),
        check_vma=False,
    )
```

time: 731 us -> 281 us (0.38)
  other arithmetic: 201 us -> 20 us
  waiting for transfers between devices: 279 us -> 102 us
  local copies, waits for them, and re-layouts: 112 us -> 9.6 us
  starting transfers between devices: 0.94 us -> 85.4 us
  matrix products: 79.5 us -> 0 us
  Pallas kernels: 0 us -> 49.7 us
  blocking collectives: 38.7 us -> 0 us
    all_gather x4 -> x2, waiting for transfers between devices: 175 us -> 0.01 us  [the longest x1 0.01 us: shards(): tok = lax.all_gather(tokens, 'tensor', axis=0, tiled=True)]
    scatter-add x4 -> x0, other arithmetic: 149 us -> none  [the longest x2 82.2 us: place_sum(): return start.at[:, target].add(products, mode='drop')]
    gather x36 -> x0, local copies, waits for them, and re-layouts: 92 us -> none  [the longest x8 21.2 us: contribution(): jnp.take(hidden, down_own % group_blocks, axis=1)]
    ppermute x7 -> x63, starting transfers between devices: 0.71 us -> 85.2 us  [the longest x14 42.2 us: onward(): lax.ppermute(pair[0], 'dp', ahead)]
    dot_general x20 -> x0, matrix products: 79.5 us -> none  [the longest x1 14.2 us: shards(): jnp.einsum('rsa,sab->rsb', jnp.take(token_cube, block_rows, axis=1), bloc...]
    pallas_call x0 -> x6, Pallas kernels: none -> 49.7 us  [run(): pl.pallas_call(body, out_shape=list(outs), in_specs=[SMEM_SPEC] * (len(sm...]
    all_gather x2 -> x0, blocking collectives: 38.7 us -> none  [the longest x1 22.3 us: shards(): lax.all_gather(down_place, 'dp', axis=0, tiled=True)]
    add x7 -> x2, other arithmetic: 20.1 us -> 0.07 us  [shards(): pick = place_of + jnp.array([[0], [slots]], jnp.int32)]
  transfers between devices with their start and end apart: 13 -> 67, of which waited for: 9 -> 49; matrix products, arithmetic and copies ran while one was open for 36% -> 9% of each run, Pallas kernels for 0% -> 10%
where the time goes in v2:
time: 281 us
  waiting for transfers between devices  102 us (36%)
  starting transfers between devices  85.4 us (30%)
  Pallas kernels  49.7 us (18%)
  other arithmetic  20 us (7%)
  between operations  14.2 us (5%)
  local copies, waits for them, and re-layouts  9.6 us (3%)
    pallas_call x6, Pallas kernels, run(): pl.pallas_call(body, out_shape=list(outs), in_specs=[SMEM_SPEC] * (len(sm...  49.7 us
    ppermute x14, starting transfers between devices, onward(): lax.ppermute(pair[0], 'dp', ahead)  42.2 us
    ppermute x14, waiting for transfers between devices, onward(): lax.ppermute(pair[0], 'dp', ahead)  34.1 us
    ppermute x7, waiting for transfers between devices, shards(): lax.ppermute(messages[s], 'dp', [(i, i ^ s) for i in range(devices)])  30.3 us
    ppermute x14, waiting for transfers between devices, step(): b = lax.ppermute(b, 'dp', self.behind)  18.8 us
    ppermute x14, starting transfers between devices, step(): a = lax.ppermute(a, 'dp', self.ahead)  16.2 us
    convert_element_type x12, other arithmetic, step(): a, b = (a.astype(jnp.bfloat16), b.astype(jnp.bfloat16))  14.6 us
    ppermute x7, starting transfers between devices, shards(): lax.ppermute(messages[s], 'dp', [(i, i ^ s) for i in range(devices)])  13.7 us
  transfers between devices with their start and end apart: 67, of which 49 were waited for; matrix products, arithmetic and copies ran while one was open for 9% of the time, Pallas kernels for 10%

profile of v2, /device:TPU:0, one launch (start us, length us, event | category | flops | bytes accessed | tf_op | source)
XLA Modules:
  0.0 280.7 jit_solution(6760981141922861458)
XLA Ops:
  9.2 3.0 %shard_map.111 = (bf16[65,16,128]{2,1,0:T(8,128)(2,1)}, bf16[65,16,128]{2,1,0:T(8,128)(2,1)}, bf16[65,16,128]{2,1,0:T(8,128)(2,1)}, bf16[65,16,128]{2,1,0:T(8,12...) custom-call(s32[1]{0:T(128)} %bitcast.refs_0_, ...), custom_call_target="tpu_custom_call" | custom-call | bytes 4194304 | tf_op jit(solution)/shard_map/pallas_call | solution.py:144
  12.2 3.0 %collective-permute-start = (bf16[65,16,128]{2,1,0:T(8,128)(2,1)}, bf16[65,16,128]{2,1,0:T(8,128)(2,1)S(1)}, u32[]{:S(2)}, u32[]{:S(2)}) collective-permute-start(bf16[65,16,128]{2,1,0:T(8,128)(2,1)} %get-tuple-element.27), channel_id=1, source_target_pairs={{0,4},{4,0},{8,12},{12,8},{16,20},{20,16},{24,28},{28,24},{1,5},{5... | collective-permute-start | bytes 798728 | tf_op jit(solution)/shard_map/ppermute | solution.py:435
  16.8 3.0 %collective-permute-start.3 = (bf16[65,16,128]{2,1,0:T(8,128)(2,1)}, bf16[65,16,128]{2,1,0:T(8,128)(2,1)S(1)}, u32[]{:S(2)}, u32[]{:S(2)}) collective-permute-start(bf16[65,16,128]{2,1,0:T(8,128)(2,1)} %get-tuple-element.30), channel_id=1, source_target_pairs={{0,16},{4,20},{8,24},{12,28},{16,0},{20,4},{24,8},{28,12},{1,17},{... | collective-permute-start | bytes 798728 | tf_op jit(solution)/shard_map/ppermute | solution.py:435
  21.8 3.8 %collective-permute-start.5 = (bf16[65,16,128]{2,1,0:T(8,128)(2,1)}, bf16[65,16,128]{2,1,0:T(8,128)(2,1)S(1)}, u32[]{:S(2)}, u32[]{:S(2)}) collective-permute-start(bf16[65,16,128]{2,1,0:T(8,128)(2,1)} %get-tuple-element.32), channel_id=1, source_target_pairs={{0,24},{4,28},{8,16},{12,20},{16,8},{20,12},{24,0},{28,4},{1,25},{... | collective-permute-start | bytes 798728 | tf_op jit(solution)/shard_map/ppermute | solution.py:435
  25.7 9.4 %collective-permute-done.1.refs_4_ = bf16[65,16,128]{2,1,0:T(8,128)(2,1)S(1)} collective-permute-done((bf16[65,16,128]{2,1,0:T(8,128)(2,1)}, bf16[65,16,128]{2,1,0:T(8,128)(2,1)S(1)}, u32[]{:S(2)}, u32[]{:S(2)}) %collective-permute-start.1) | collective-permute-done | bytes 266272 | tf_op jit(solution)/shard_map/ppermute | solution.py:435
  36.2 2.3 collective-permute-done.2.refs_5_
  38.6 18.5 %collective-permute-done.4.refs_7_ = bf16[65,16,128]{2,1,0:T(8,128)(2,1)S(1)} collective-permute-done((bf16[65,16,128]{2,1,0:T(8,128)(2,1)}, bf16[65,16,128]{2,1,0:T(8,128)(2,1)S(1)}, u32[]{:S(2)}, u32[]{:S(2)}) %collective-permute-start.4) | collective-permute-done | bytes 266272 | tf_op jit(solution)/shard_map/ppermute | solution.py:435
  58.4 3.4 %shard_map.112 = (bf16[64,16,128]{2,1,0:T(8,128)(2,1)}, bf16[64,16,128]{2,1,0:T(8,128)(2,1)}, bf16[64,16,128]{2,1,0:T(8,128)(2,1)}, bf16[64,16,128]{2,1,0:T(8,128)(2,1)}) custom-call(s32[128]{0:T(128)} %get-tuple-element.89.refs_0_, s32[128]{0:T(128)} %get-tuple-element.88.refs_1_, bf16[65,16,128]{2,1,0:T(8,128)(2,1)} %get-tuple-element.26.refs_2_, ...), custom_call_target="tpu_custom_call" | custom-call | bytes 3145728 | tf_op jit(solution)/shard_map/pallas_call | solution.py:144
  61.9 10.0 %collective-permute-start.7 = (bf16[64,16,128]{2,1,0:T(8,128)(2,1)}, bf16[64,16,128]{2,1,0:T(8,128)(2,1)S(1)}, u32[]{:S(2)}, u32[]{:S(2)}) collective-permute-start(bf16[64,16,128]{2,1,0:T(8,128)(2,1)} %get-tuple-element.35.refs_8_.refs_5_), channel_id=1, source_target_pairs={{0,8},{8,16},{16,24},{24,28},{28,20},{20,12},{12,4},{4,0},{1,9},{9... | collective-permute-start | bytes 786440 | tf_op jit(solution)/shard_map/ppermute | solution.py:447
  71.8 4.2 %collective-permute-done.7.refs_9_.refs_6_ = bf16[64,16,128]{2,1,0:T(8,128)(2,1)S(1)} collective-permute-done((bf16[64,16,128]{2,1,0:T(8,128)(2,1)}, bf16[64,16,128]{2,1,0:T(8,128)(2,1)S(1)}, u32[]{:S(2)}, u32[]{:S(2)}) %collective-permute-start.7) | collective-permute-done | bytes 262176 | tf_op jit(solution)/shard_map/ppermute | solution.py:447
  76.0 3.1 %collective-permute-start.8 = (bf16[64,16,128]{2,1,0:T(8,128)(2,1)S(1)}, bf16[64,16,128]{2,1,0:T(8,128)(2,1)S(1)}, u32[]{:S(2)}, u32[]{:S(2)}) collective-permute-start(bf16[64,16,128]{2,1,0:T(8,128)(2,1)S(1)} %collective-permute-done.7.refs_9_.refs_6_), channel_id=1, source_target_pairs={{0,8},{8,16},{16,24},{24,28},{28,20},{20,12},{12,4},{4,0},{1,9},{9... | collective-permute-start | bytes 786440 | tf_op jit(solution)/shard_map/ppermute | solution.py:447
  79.2 2.4 collective-permute-start.23
  81.6 4.2 %collective-permute-done.8.refs_10_.refs_7_ = bf16[64,16,128]{2,1,0:T(8,128)(2,1)S(1)} collective-permute-done((bf16[64,16,128]{2,1,0:T(8,128)(2,1)S(1)}, bf16[64,16,128]{2,1,0:T(8,128)(2,1)S(1)}, u32[]{:S(2)}, u32[]{:S(2)}) %collective-permute-start.8) | collective-permute-done | bytes 262176 | tf_op jit(solution)/shard_map/ppermute | solution.py:447
  85.9 2.5 collective-permute-start.9
  88.7 2.9 %collective-permute-done.23.refs_9_.refs_6_ = bf16[64,16,128]{2,1,0:T(8,128)(2,1)S(1)} collective-permute-done((bf16[64,16,128]{2,1,0:T(8,128)(2,1)}, bf16[64,16,128]{2,1,0:T(8,128)(2,1)S(1)}, u32[]{:S(2)}, u32[]{:S(2)}) %collective-permute-start.23) | collective-permute-done | bytes 262176 | tf_op jit(solution)/shard_map/ppermute | solution.py:447
  91.6 2.4 collective-permute-start.24
  94.3 2.8 collective-permute-done.9.refs_11_.refs_8_
  97.1 2.5 collective-permute-start.10
  100.0 2.8 collective-permute-done.24.refs_10_.refs_7_
  102.7 2.5 collective-permute-start.25
  105.7 2.7 collective-permute-done.10.refs_12_.refs_9_
  108.3 2.5 collective-permute-start.11
  111.3 2.7 collective-permute-done.25.refs_11_.refs_8_
  114.0 2.6 collective-permute-start.26
  116.9 2.7 collective-permute-done.11.refs_13_.refs_10_
  119.6 2.5 collective-permute-start.12
  125.3 2.5 collective-permute-start.27
  128.1 2.7 collective-permute-done.12.refs_14_.refs_11_
  130.8 2.5 collective-permute-start.13
  134.6 2.0 collective-permute-done.27.refs_13_.refs_10_
  136.5 2.5 collective-permute-start.28
  140.9 2.9 %collective-permute-done.20.refs_23_.refs_20_ = bf16[64,16,128]{2,1,0:T(8,128)(2,1)} collective-permute-done((bf16[64,16,128]{2,1,0:T(8,128)(2,1)}, bf16[64,16,128]{2,1,0:T(8,128)(2,1)}, u32[]{:S(2)}, u32[]{:S(2)}) %collective-permute-start.20) | collective-permute-done | bytes 262176 | tf_op jit(solution)/shard_map/ppermute | solution.py:447
  143.9 14.3 %shard_map.113 = (bf16[32,128,128]{2,1,0:T(8,128)(2,1)}, f32[32,128,128]{2,1,0:T(8,128)}, bf16[8,16,128,128]{3,2,1,0:T(8,128)(2,1)}) custom-call(s32[8]{0:T(128)} %get-tuple-element.85.refs_0_, s32[128]{0:T(128)} %get-tuple-element.97.refs_1_.refs_3_.refs_0_, s32[128]{0:T(128)} %get-tuple-element.90.refs_2_.refs_4_.refs_1_, ...), custom_call_target="tpu_custom_call" | custom-call | flops 4294967296 | bytes 13631488 | tf_op jit(solution)/shard_map/pallas_call | solution.py:144
  159.3 2.1 collective-permute-start.21
  161.4 2.0 collective-permute-start.29
  167.0 1.6 collective-permute-done.29.refs_15_.refs_12_
  170.7 11.1 %shard_map.114 = (bf16[32,128,128]{2,1,0:T(8,128)(2,1)}, bf16[8,16,128,128]{3,2,1,0:T(8,128)(2,1)}) custom-call(s32[8]{0:T(128)} %get-tuple-element.85.refs_0_, s32[128]{0:T(128)} %get-tuple-element.96.refs_3_.refs_1_.refs_0_, s32[128]{0:T(128)} %get-tuple-element.91.refs_4_.refs_2_.refs_1_, s32[128]{0:T(128)} %get-tuple-element.97.refs_1_.refs_3_.refs_0_, ...), custom_call_target="tpu_custom_call" | custom-call | flops 4294967296 | bytes 13631488 | tf_op jit(solution)/shard_map/pallas_call | solution.py:144
  183.0 2.0 collective-permute-start.37
  185.0 4.3 %collective-permute-done.38 = bf16[16,64,128]{2,1,0:T(8,128)(2,1)S(1)} collective-permute-done((bf16[16,64,128]{2,1,0:T(8,128)(2,1)S(1)}, bf16[16,64,128]{2,1,0:T(8,128)(2,1)S(1)}, u32[]{:S(2)}, u32[]{:S(2)}) %collective-permute-start.38) | collective-permute-done | bytes 262176 | tf_op jit(solution)/shard_map/ppermute | solution.py:320
  190.6 8.4 %shard_map.115 = bf16[128,4096]{1,0:T(8,128)(2,1)} custom-call(s32[128]{0:T(128)} %get-tuple-element.96.refs_3_.refs_1_.refs_0_, s32[128]{0:T(128)} %get-tuple-element.91.refs_4_.refs_2_.refs_1_, s32[8]{0:T(128)} %get-tuple-element.87.refs_5_.refs_2_, s32[8]{0:T(128)} %get-tuple-element.86.refs_6_.refs_3_, bf16[32,128,128]{2,1,0:T(8,128)(2,1)} %get-tuple-element.45.refs_4_, ...), custom_call_target="tpu_custom_call" | custom-call | flops 2147483648 | bytes 6291456 | tf_op jit(solution)/shard_map/pallas_call | solution.py:144
  203.1 5.2 %collective-permute-done.57 = bf16[16,64,128]{2,1,0:T(8,128)(2,1)S(1)} collective-permute-done((bf16[16,64,128]{2,1,0:T(8,128)(2,1)S(1)}, bf16[16,64,128]{2,1,0:T(8,128)(2,1)S(1)}, u32[]{:S(2)}, u32[]{:S(2)}) %collective-permute-start.57) | collective-permute-done | bytes 262176 | tf_op jit(solution)/shard_map/ppermute | solution.py:320
  216.3 1.7 collective-permute-start.46
  218.4 2.3 collective-permute-done.52
  232.8 9.6 %shard_map.116 = bf16[128,4096]{1,0:T(8,128)(2,1)} custom-call(s32[128]{0:T(128)} %get-tuple-element.97.refs_1_.refs_3_.refs_0_, s32[128]{0:T(128)} %get-tuple-element.90.refs_2_.refs_4_.refs_1_, s32[8]{0:T(128)} %get-tuple-element.87.refs_5_.refs_2_, s32[8]{0:T(128)} %get-tuple-element.86.refs_6_.refs_3_, bf16[32,128,128]{2,1,0:T(8,128)(2,1)} %get-tuple-element.47.refs_4_, ...), custom_call_target="tpu_custom_call" | custom-call | flops 2147483648 | bytes 6291456 | tf_op jit(solution)/shard_map/pallas_call | solution.py:144
  249.1 3.8 %collective-permute-done.43 = bf16[16,64,128]{2,1,0:T(8,128)(2,1)S(1)} collective-permute-done((bf16[16,64,128]{2,1,0:T(8,128)(2,1)S(1)}, bf16[16,64,128]{2,1,0:T(8,128)(2,1)S(1)}, u32[]{:S(2)}, u32[]{:S(2)}) %collective-permute-start.43) | collective-permute-done | bytes 262176 | tf_op jit(solution)/shard_map/ppermute | solution.py:319
  255.2 1.9 collective-permute-start.44
  260.6 1.7 collective-permute-start.56
  267.0 1.6 collective-permute-done.62
  (196 shorter events, 74.0 us)
Async XLA Ops:
  7.2 132.2 %all-gather.3.cloned.1.call-start = ((), (), s32[]{:S(2)}) async-start(), calls=%async_computation.2 | async-start | bytes 1310720 | tf_op jit(solution)/shard_map/all_gather | solution.py:443
  12.2 9.6 %collective-permute-start = (bf16[65,16,128]{2,1,0:T(8,128)(2,1)}, bf16[65,16,128]{2,1,0:T(8,128)(2,1)S(1)}, u32[]{:S(2)}, u32[]{:S(2)}) collective-permute-start(bf16[65,16,128]{2,1,0:T(8,128)(2,1)} %get-tuple-element.27), channel_id=1, source_target_pairs={{0,4},{4,0},{8,12},{12,8},{16,20},{20,16},{24,28},{28,24},{1,5},{5... | collective-permute-start | bytes 798728 | tf_op jit(solution)/shard_map/ppermute | solution.py:435
  15.2 20.0 %collective-permute-start.1 = (bf16[65,16,128]{2,1,0:T(8,128)(2,1)}, bf16[65,16,128]{2,1,0:T(8,128)(2,1)S(1)}, u32[]{:S(2)}, u32[]{:S(2)}) collective-permute-start(bf16[65,16,128]{2,1,0:T(8,128)(2,1)} %get-tuple-element.28), channel_id=1, source_target_pairs={{0,8},{4,12},{8,0},{12,4},{16,24},{20,28},{24,16},{28,20},{1,9},{5... | collective-permute-start | bytes 798728 | tf_op jit(solution)/shard_map/ppermute | solution.py:435
  16.8 21.8 %collective-permute-start.2 = (bf16[65,16,128]{2,1,0:T(8,128)(2,1)}, bf16[65,16,128]{2,1,0:T(8,128)(2,1)S(1)}, u32[]{:S(2)}, u32[]{:S(2)}) collective-permute-start(bf16[65,16,128]{2,1,0:T(8,128)(2,1)} %get-tuple-element.29), channel_id=1, source_target_pairs={{0,12},{4,8},{8,4},{12,0},{16,28},{20,24},{24,20},{28,16},{1,13},{... | collective-permute-start | bytes 798728 | tf_op jit(solution)/shard_map/ppermute | solution.py:435
  16.8 21.8 %collective-permute-start.3 = (bf16[65,16,128]{2,1,0:T(8,128)(2,1)}, bf16[65,16,128]{2,1,0:T(8,128)(2,1)S(1)}, u32[]{:S(2)}, u32[]{:S(2)}) collective-permute-start(bf16[65,16,128]{2,1,0:T(8,128)(2,1)} %get-tuple-element.30), channel_id=1, source_target_pairs={{0,16},{4,20},{8,24},{12,28},{16,0},{20,4},{24,8},{28,12},{1,17},{... | collective-permute-start | bytes 798728 | tf_op jit(solution)/shard_map/ppermute | solution.py:435
  19.8 37.3 %collective-permute-start.4 = (bf16[65,16,128]{2,1,0:T(8,128)(2,1)}, bf16[65,16,128]{2,1,0:T(8,128)(2,1)S(1)}, u32[]{:S(2)}, u32[]{:S(2)}) collective-permute-start(bf16[65,16,128]{2,1,0:T(8,128)(2,1)} %get-tuple-element.31), channel_id=1, source_target_pairs={{0,20},{4,16},{8,28},{12,24},{16,4},{20,0},{24,12},{28,8},{1,21},{... | collective-permute-start | bytes 798728 | tf_op jit(solution)/shard_map/ppermute | solution.py:435
  21.8 35.3 %collective-permute-start.5 = (bf16[65,16,128]{2,1,0:T(8,128)(2,1)}, bf16[65,16,128]{2,1,0:T(8,128)(2,1)S(1)}, u32[]{:S(2)}, u32[]{:S(2)}) collective-permute-start(bf16[65,16,128]{2,1,0:T(8,128)(2,1)} %get-tuple-element.32), channel_id=1, source_target_pairs={{0,24},{4,28},{8,16},{12,20},{16,8},{20,12},{24,0},{28,4},{1,25},{... | collective-permute-start | bytes 798728 | tf_op jit(solution)/shard_map/ppermute | solution.py:435
  25.7 113.7 %all-gather.5.cloned.1.call-start = ((), (), s32[]{:S(2)}) async-start(), calls=%async_computation.3 | async-start | bytes 1310720 | tf_op jit(solution)/shard_map/all_gather | solution.py:444
  35.2 21.9 %collective-permute-start.6 = (bf16[65,16,128]{2,1,0:T(8,128)(2,1)}, bf16[65,16,128]{2,1,0:T(8,128)(2,1)S(1)}, u32[]{:S(2)}, u32[]{:S(2)}) collective-permute-start(bf16[65,16,128]{2,1,0:T(8,128)(2,1)} %get-tuple-element.33), channel_id=1, source_target_pairs={{0,28},{4,24},{8,20},{12,16},{16,12},{20,8},{24,4},{28,0},{1,29},{... | collective-permute-start | bytes 798728 | tf_op jit(solution)/shard_map/ppermute | solution.py:435
  61.9 14.2 %collective-permute-start.7 = (bf16[64,16,128]{2,1,0:T(8,128)(2,1)}, bf16[64,16,128]{2,1,0:T(8,128)(2,1)S(1)}, u32[]{:S(2)}, u32[]{:S(2)}) collective-permute-start(bf16[64,16,128]{2,1,0:T(8,128)(2,1)} %get-tuple-element.35.refs_8_.refs_5_), channel_id=1, source_target_pairs={{0,8},{8,16},{16,24},{24,28},{28,20},{20,12},{12,4},{4,0},{1,9},{9... | collective-permute-start | bytes 786440 | tf_op jit(solution)/shard_map/ppermute | solution.py:447
  76.0 9.8 %collective-permute-start.8 = (bf16[64,16,128]{2,1,0:T(8,128)(2,1)S(1)}, bf16[64,16,128]{2,1,0:T(8,128)(2,1)S(1)}, u32[]{:S(2)}, u32[]{:S(2)}) collective-permute-start(bf16[64,16,128]{2,1,0:T(8,128)(2,1)S(1)} %collective-permute-done.7.refs_9_.refs_6_), channel_id=1, source_target_pairs={{0,8},{8,16},{16,24},{24,28},{28,20},{20,12},{12,4},{4,0},{1,9},{9... | collective-permute-start | bytes 786440 | tf_op jit(solution)/shard_map/ppermute | solution.py:447
  79.2 9.5 %collective-permute-start.15 = (bf16[64,16,128]{2,1,0:T(8,128)(2,1)S(1)}, bf16[64,16,128]{2,1,0:T(8,128)(2,1)S(1)}, u32[]{:S(2)}, u32[]{:S(2)}) collective-permute-start(bf16[64,16,128]{2,1,0:T(8,128)(2,1)S(1)} %collective-permute-done.14.refs_17_.refs_14_), channel_id=1, source_target_pairs={{8,0},{16,8},{24,16},{28,24},{20,28},{12,20},{4,12},{0,4},{9,1},{1... | collective-permute-start | bytes 786440 | tf_op jit(solution)/shard_map/ppermute | solution.py:447
  79.2 195.0 %reduce-scatter.3.cloned.1.call-start = ((), (), s32[]{:S(2)}) async-start(), calls=%async_computation.4 | async-start | bytes 1310720 | tf_op jit(solution)/shard_map/reduce_scatter | solution.py:477
  79.2 12.4 %collective-permute-start.23 = (bf16[64,16,128]{2,1,0:T(8,128)(2,1)}, bf16[64,16,128]{2,1,0:T(8,128)(2,1)S(1)}, u32[]{:S(2)}, u32[]{:S(2)}) collective-permute-start(bf16[64,16,128]{2,1,0:T(8,128)(2,1)} %get-tuple-element.41.refs_8_.refs_5_), channel_id=1, source_target_pairs={{0,8},{8,16},{16,24},{24,28},{28,20},{20,12},{12,4},{4,0},{1,9},{9... | collective-permute-start | bytes 786440 | tf_op jit(solution)/shard_map/ppermute | solution.py:447
  81.6 12.7 %collective-permute-start.30 = (bf16[64,16,128]{2,1,0:T(8,128)(2,1)}, bf16[64,16,128]{2,1,0:T(8,128)(2,1)S(1)}, u32[]{:S(2)}, u32[]{:S(2)}) collective-permute-start(bf16[64,16,128]{2,1,0:T(8,128)(2,1)} %get-tuple-element.42.refs_16_.refs_13_), channel_id=1, source_target_pairs={{8,0},{16,8},{24,16},{28,24},{20,28},{12,20},{4,12},{0,4},{9,1},{1... | collective-permute-start | bytes 786440 | tf_op jit(solution)/shard_map/ppermute | solution.py:447
  85.9 11.2 %collective-permute-start.9 = (bf16[64,16,128]{2,1,0:T(8,128)(2,1)S(1)}, bf16[64,16,128]{2,1,0:T(8,128)(2,1)S(1)}, u32[]{:S(2)}, u32[]{:S(2)}) collective-permute-start(bf16[64,16,128]{2,1,0:T(8,128)(2,1)S(1)} %collective-permute-done.8.refs_10_.refs_7_), channel_id=1, source_target_pairs={{0,8},{8,16},{16,24},{24,28},{28,20},{20,12},{12,4},{4,0},{1,9},{9... | collective-permute-start | bytes 786440 | tf_op jit(solution)/shard_map/ppermute | solution.py:447
  88.7 11.2 %collective-permute-start.16 = (bf16[64,16,128]{2,1,0:T(8,128)(2,1)S(1)}, bf16[64,16,128]{2,1,0:T(8,128)(2,1)S(1)}, u32[]{:S(2)}, u32[]{:S(2)}) collective-permute-start(bf16[64,16,128]{2,1,0:T(8,128)(2,1)S(1)} %collective-permute-done.15.refs_18_.refs_15_), channel_id=1, source_target_pairs={{8,0},{16,8},{24,16},{28,24},{20,28},{12,20},{4,12},{0,4},{9,1},{1... | collective-permute-start | bytes 786440 | tf_op jit(solution)/shard_map/ppermute | solution.py:447
  91.6 11.1 %collective-permute-start.24 = (bf16[64,16,128]{2,1,0:T(8,128)(2,1)S(1)}, bf16[64,16,128]{2,1,0:T(8,128)(2,1)S(1)}, u32[]{:S(2)}, u32[]{:S(2)}) collective-permute-start(bf16[64,16,128]{2,1,0:T(8,128)(2,1)S(1)} %collective-permute-done.23.refs_9_.refs_6_), channel_id=1, source_target_pairs={{0,8},{8,16},{16,24},{24,28},{28,20},{20,12},{12,4},{4,0},{1,9},{9... | collective-permute-start | bytes 786440 | tf_op jit(solution)/shard_map/ppermute | solution.py:447
  94.3 11.3 %collective-permute-start.31 = (bf16[64,16,128]{2,1,0:T(8,128)(2,1)S(1)}, bf16[64,16,128]{2,1,0:T(8,128)(2,1)}, u32[]{:S(2)}, u32[]{:S(2)}) collective-permute-start(bf16[64,16,128]{2,1,0:T(8,128)(2,1)S(1)} %collective-permute-done.30.refs_17_.refs_14_), channel_id=1, source_target_pairs={{8,0},{16,8},{24,16},{28,24},{20,28},{12,20},{4,12},{0,4},{9,1},{1... | collective-permute-start | bytes 786440 | tf_op jit(solution)/shard_map/ppermute | solution.py:447
  97.1 11.2 %collective-permute-start.10 = (bf16[64,16,128]{2,1,0:T(8,128)(2,1)S(1)}, bf16[64,16,128]{2,1,0:T(8,128)(2,1)S(1)}, u32[]{:S(2)}, u32[]{:S(2)}) collective-permute-start(bf16[64,16,128]{2,1,0:T(8,128)(2,1)S(1)} %collective-permute-done.9.refs_11_.refs_8_), channel_id=1, source_target_pairs={{0,8},{8,16},{16,24},{24,28},{28,20},{20,12},{12,4},{4,0},{1,9},{9... | collective-permute-start | bytes 786440 | tf_op jit(solution)/shard_map/ppermute | solution.py:447
  100.0 11.2 %collective-permute-start.17 = (bf16[64,16,128]{2,1,0:T(8,128)(2,1)S(1)}, bf16[64,16,128]{2,1,0:T(8,128)(2,1)S(1)}, u32[]{:S(2)}, u32[]{:S(2)}) collective-permute-start(bf16[64,16,128]{2,1,0:T(8,128)(2,1)S(1)} %collective-permute-done.16.refs_19_.refs_16_), channel_id=1, source_target_pairs={{8,0},{16,8},{24,16},{28,24},{20,28},{12,20},{4,12},{0,4},{9,1},{1... | collective-permute-start | bytes 786440 | tf_op jit(solution)/shard_map/ppermute | solution.py:447
  102.7 11.2 %collective-permute-start.25 = (bf16[64,16,128]{2,1,0:T(8,128)(2,1)S(1)}, bf16[64,16,128]{2,1,0:T(8,128)(2,1)}, u32[]{:S(2)}, u32[]{:S(2)}) collective-permute-start(bf16[64,16,128]{2,1,0:T(8,128)(2,1)S(1)} %collective-permute-done.24.refs_10_.refs_7_), channel_id=1, source_target_pairs={{0,8},{8,16},{16,24},{24,28},{28,20},{20,12},{12,4},{4,0},{1,9},{9... | collective-permute-start | bytes 786440 | tf_op jit(solution)/shard_map/ppermute | solution.py:447
  105.7 11.2 %collective-permute-start.32 = (bf16[64,16,128]{2,1,0:T(8,128)(2,1)}, bf16[64,16,128]{2,1,0:T(8,128)(2,1)}, u32[]{:S(2)}, u32[]{:S(2)}) collective-permute-start(bf16[64,16,128]{2,1,0:T(8,128)(2,1)} %collective-permute-done.31.refs_18_.refs_15_), channel_id=1, source_target_pairs={{8,0},{16,8},{24,16},{28,24},{20,28},{12,20},{4,12},{0,4},{9,1},{1... | collective-permute-start | bytes 786440 | tf_op jit(solution)/shard_map/ppermute | solution.py:447
  108.3 11.2 %collective-permute-start.11 = (bf16[64,16,128]{2,1,0:T(8,128)(2,1)S(1)}, bf16[64,16,128]{2,1,0:T(8,128)(2,1)S(1)}, u32[]{:S(2)}, u32[]{:S(2)}) collective-permute-start(bf16[64,16,128]{2,1,0:T(8,128)(2,1)S(1)} %collective-permute-done.10.refs_12_.refs_9_), channel_id=1, source_target_pairs={{0,8},{8,16},{16,24},{24,28},{28,20},{20,12},{12,4},{4,0},{1,9},{9... | collective-permute-start | bytes 786440 | tf_op jit(solution)/shard_map/ppermute | solution.py:447
  111.2 11.2 %collective-permute-start.18 = (bf16[64,16,128]{2,1,0:T(8,128)(2,1)S(1)}, bf16[64,16,128]{2,1,0:T(8,128)(2,1)S(1)}, u32[]{:S(2)}, u32[]{:S(2)}) collective-permute-start(bf16[64,16,128]{2,1,0:T(8,128)(2,1)S(1)} %collective-permute-done.17.refs_20_.refs_17_), channel_id=1, source_target_pairs={{8,0},{16,8},{24,16},{28,24},{20,28},{12,20},{4,12},{0,4},{9,1},{1... | collective-permute-start | bytes 786440 | tf_op jit(solution)/shard_map/ppermute | solution.py:447
  114.0 11.3 %collective-permute-start.26 = (bf16[64,16,128]{2,1,0:T(8,128)(2,1)}, bf16[64,16,128]{2,1,0:T(8,128)(2,1)}, u32[]{:S(2)}, u32[]{:S(2)}) collective-permute-start(bf16[64,16,128]{2,1,0:T(8,128)(2,1)} %collective-permute-done.25.refs_11_.refs_8_), channel_id=1, source_target_pairs={{0,8},{8,16},{16,24},{24,28},{28,20},{20,12},{12,4},{4,0},{1,9},{9... | collective-permute-start | bytes 786440 | tf_op jit(solution)/shard_map/ppermute | solution.py:447
  116.9 11.2 %collective-permute-start.33 = (bf16[64,16,128]{2,1,0:T(8,128)(2,1)}, bf16[64,16,128]{2,1,0:T(8,128)(2,1)}, u32[]{:S(2)}, u32[]{:S(2)}) collective-permute-start(bf16[64,16,128]{2,1,0:T(8,128)(2,1)} %collective-permute-done.32.refs_19_.refs_16_), channel_id=1, source_target_pairs={{8,0},{16,8},{24,16},{28,24},{20,28},{12,20},{4,12},{0,4},{9,1},{1... | collective-permute-start | bytes 786440 | tf_op jit(solution)/shard_map/ppermute | solution.py:447
  119.6 11.2 %collective-permute-start.12 = (bf16[64,16,128]{2,1,0:T(8,128)(2,1)S(1)}, bf16[64,16,128]{2,1,0:T(8,128)(2,1)S(1)}, u32[]{:S(2)}, u32[]{:S(2)}) collective-permute-start(bf16[64,16,128]{2,1,0:T(8,128)(2,1)S(1)} %collective-permute-done.11.refs_13_.refs_10_), channel_id=1, source_target_pairs={{0,8},{8,16},{16,24},{24,28},{28,20},{20,12},{12,4},{4,0},{1,9},{9... | collective-permute-start | bytes 786440 | tf_op jit(solution)/shard_map/ppermute | solution.py:447
  122.4 11.3 %collective-permute-start.19 = (bf16[64,16,128]{2,1,0:T(8,128)(2,1)S(1)}, bf16[64,16,128]{2,1,0:T(8,128)(2,1)}, u32[]{:S(2)}, u32[]{:S(2)}) collective-permute-start(bf16[64,16,128]{2,1,0:T(8,128)(2,1)S(1)} %collective-permute-done.18.refs_21_.refs_18_), channel_id=1, source_target_pairs={{8,0},{16,8},{24,16},{28,24},{20,28},{12,20},{4,12},{0,4},{9,1},{1... | collective-permute-start | bytes 786440 | tf_op jit(solution)/shard_map/ppermute | solution.py:447
  125.3 11.2 %collective-permute-start.27 = (bf16[64,16,128]{2,1,0:T(8,128)(2,1)}, bf16[64,16,128]{2,1,0:T(8,128)(2,1)}, u32[]{:S(2)}, u32[]{:S(2)}) collective-permute-start(bf16[64,16,128]{2,1,0:T(8,128)(2,1)} %collective-permute-done.26.refs_12_.refs_9_), channel_id=1, source_target_pairs={{0,8},{8,16},{16,24},{24,28},{28,20},{20,12},{12,4},{4,0},{1,9},{9... | collective-permute-start | bytes 786440 | tf_op jit(solution)/shard_map/ppermute | solution.py:447
  128.1 11.2 %collective-permute-start.34 = (bf16[64,16,128]{2,1,0:T(8,128)(2,1)}, bf16[64,16,128]{2,1,0:T(8,128)(2,1)}, u32[]{:S(2)}, u32[]{:S(2)}) collective-permute-start(bf16[64,16,128]{2,1,0:T(8,128)(2,1)} %collective-permute-done.33.refs_20_.refs_17_), channel_id=1, source_target_pairs={{8,0},{16,8},{24,16},{28,24},{20,28},{12,20},{4,12},{0,4},{9,1},{1... | collective-permute-start | bytes 786440 | tf_op jit(solution)/shard_map/ppermute | solution.py:447
  130.8 10.1 %collective-permute-start.13 = (bf16[64,16,128]{2,1,0:T(8,128)(2,1)S(1)}, bf16[64,16,128]{2,1,0:T(8,128)(2,1)}, u32[]{:S(2)}, u32[]{:S(2)}) collective-permute-start(bf16[64,16,128]{2,1,0:T(8,128)(2,1)S(1)} %collective-permute-done.12.refs_14_.refs_11_), channel_id=1, source_target_pairs={{0,8},{8,16},{16,24},{24,28},{28,20},{20,12},{12,4},{4,0},{1,9},{9... | collective-permute-start | bytes 786440 | tf_op jit(solution)/shard_map/ppermute | solution.py:447
  133.8 10.0 %collective-permute-start.20 = (bf16[64,16,128]{2,1,0:T(8,128)(2,1)}, bf16[64,16,128]{2,1,0:T(8,128)(2,1)}, u32[]{:S(2)}, u32[]{:S(2)}) collective-permute-start(bf16[64,16,128]{2,1,0:T(8,128)(2,1)} %collective-permute-done.19.refs_22_.refs_19_), channel_id=1, source_target_pairs={{8,0},{16,8},{24,16},{28,24},{20,28},{12,20},{4,12},{0,4},{9,1},{1... | collective-permute-start | bytes 786440 | tf_op jit(solution)/shard_map/ppermute | solution.py:447
  136.5 24.9 %collective-permute-start.28 = (bf16[64,16,128]{2,1,0:T(8,128)(2,1)}, bf16[64,16,128]{2,1,0:T(8,128)(2,1)}, u32[]{:S(2)}, u32[]{:S(2)}) collective-permute-start(bf16[64,16,128]{2,1,0:T(8,128)(2,1)} %collective-permute-done.27.refs_13_.refs_10_), channel_id=1, source_target_pairs={{0,8},{8,16},{16,24},{24,28},{28,20},{20,12},{12,4},{4,0},{1,9},{9... | collective-permute-start | bytes 786440 | tf_op jit(solution)/shard_map/ppermute | solution.py:447
  139.4 24.0 %collective-permute-start.35 = (bf16[64,16,128]{2,1,0:T(8,128)(2,1)}, bf16[64,16,128]{2,1,0:T(8,128)(2,1)}, u32[]{:S(2)}, u32[]{:S(2)}) collective-permute-start(bf16[64,16,128]{2,1,0:T(8,128)(2,1)} %collective-permute-done.34.refs_21_.refs_18_), channel_id=1, source_target_pairs={{8,0},{16,8},{24,16},{28,24},{20,28},{12,20},{4,12},{0,4},{9,1},{1... | collective-permute-start | bytes 786440 | tf_op jit(solution)/shard_map/ppermute | solution.py:447
  199.0 75.2 %reduce-scatter.5.cloned.1.call-start = ((), (), s32[]{:S(2)}) async-start(), calls=%async_computation.5 | async-start | bytes 1310720 | tf_op jit(solution)/shard_map/reduce_scatter | solution.py:478
  199.0 9.3 %collective-permute-start.57 = (bf16[16,64,128]{2,1,0:T(8,128)(2,1)S(1)}, bf16[16,64,128]{2,1,0:T(8,128)(2,1)S(1)}, u32[]{:S(2)}, u32[]{:S(2)}) collective-permute-start(bf16[16,64,128]{2,1,0:T(8,128)(2,1)S(1)} %get-tuple-element.78), channel_id=1, source_target_pairs={{8,0},{16,8},{24,16},{28,24},{20,28},{12,20},{4,12},{0,4},{9,1},{1... | collective-permute-start | bytes 786440 | tf_op jit(solution)/shard_map/ppermute | solution.py:320
  201.1 12.8 %collective-permute-start.40 = (bf16[16,64,128]{2,1,0:T(8,128)(2,1)S(1)}, bf16[16,64,128]{2,1,0:T(8,128)(2,1)S(1)}, u32[]{:S(2)}, u32[]{:S(2)}) collective-permute-start(bf16[16,64,128]{2,1,0:T(8,128)(2,1)S(1)} %get-tuple-element.74), channel_id=1, source_target_pairs={{8,0},{16,8},{24,16},{28,24},{20,28},{12,20},{4,12},{0,4},{9,1},{1... | collective-permute-start | bytes 786440 | tf_op jit(solution)/shard_map/ppermute | solution.py:320
  202.3 12.8 %collective-permute-start.39 = (bf16[16,64,128]{2,1,0:T(8,128)(2,1)S(1)}, bf16[16,64,128]{2,1,0:T(8,128)(2,1)S(1)}, u32[]{:S(2)}, u32[]{:S(2)}) collective-permute-start(bf16[16,64,128]{2,1,0:T(8,128)(2,1)S(1)} %get-tuple-element.75), channel_id=1, source_target_pairs={{0,8},{8,16},{16,24},{24,28},{28,20},{20,12},{12,4},{4,0},{1,9},{9... | collective-permute-start | bytes 786440 | tf_op jit(solution)/shard_map/ppermute | solution.py:319
  210.7 10.0 %collective-permute-start.52 = (bf16[16,64,128]{2,1,0:T(8,128)(2,1)S(1)}, bf16[16,64,128]{2,1,0:T(8,128)(2,1)S(1)}, u32[]{:S(2)}, u32[]{:S(2)}) collective-permute-start(bf16[16,64,128]{2,1,0:T(8,128)(2,1)S(1)} %get-tuple-element.60), channel_id=1, source_target_pairs={{0,8},{8,16},{16,24},{24,28},{28,20},{20,12},{12,4},{4,0},{1,9},{9... | collective-permute-start | bytes 786440 | tf_op jit(solution)/shard_map/ppermute | solution.py:319
  211.5 9.2 %collective-permute-start.58 = (bf16[16,64,128]{2,1,0:T(8,128)(2,1)S(1)}, bf16[16,64,128]{2,1,0:T(8,128)(2,1)S(1)}, u32[]{:S(2)}, u32[]{:S(2)}) collective-permute-start(bf16[16,64,128]{2,1,0:T(8,128)(2,1)S(1)} %get-tuple-element.61), channel_id=1, source_target_pairs={{8,0},{16,8},{24,16},{28,24},{20,28},{12,20},{4,12},{0,4},{9,1},{1... | collective-permute-start | bytes 786440 | tf_op jit(solution)/shard_map/ppermute | solution.py:320
  227.4 15.0 %collective-permute-start.42 = (bf16[16,64,128]{2,1,0:T(8,128)(2,1)S(1)}, bf16[16,64,128]{2,1,0:T(8,128)(2,1)S(1)}, u32[]{:S(2)}, u32[]{:S(2)}) collective-permute-start(bf16[16,64,128]{2,1,0:T(8,128)(2,1)S(1)} %get-tuple-element.70), channel_id=1, source_target_pairs={{0,8},{8,16},{16,24},{24,28},{28,20},{20,12},{12,4},{4,0},{1,9},{9... | collective-permute-start | bytes 786440 | tf_op jit(solution)/shard_map/ppermute | solution.py:319
  228.2 14.3 %collective-permute-start.47 = (bf16[16,64,128]{2,1,0:T(8,128)(2,1)S(1)}, bf16[16,64,128]{2,1,0:T(8,128)(2,1)S(1)}, u32[]{:S(2)}, u32[]{:S(2)}) collective-permute-start(bf16[16,64,128]{2,1,0:T(8,128)(2,1)S(1)} %get-tuple-element.71), channel_id=1, source_target_pairs={{8,0},{16,8},{24,16},{28,24},{20,28},{12,20},{4,12},{0,4},{9,1},{1... | collective-permute-start | bytes 786440 | tf_op jit(solution)/shard_map/ppermute | solution.py:320
  230.8 15.0 %collective-permute-start.54 = (bf16[16,64,128]{2,1,0:T(8,128)(2,1)S(1)}, bf16[16,64,128]{2,1,0:T(8,128)(2,1)S(1)}, u32[]{:S(2)}, u32[]{:S(2)}) collective-permute-start(bf16[16,64,128]{2,1,0:T(8,128)(2,1)S(1)} %get-tuple-element.56), channel_id=1, source_target_pairs={{0,8},{8,16},{16,24},{24,28},{28,20},{20,12},{12,4},{4,0},{1,9},{9... | collective-permute-start | bytes 786440 | tf_op jit(solution)/shard_map/ppermute | solution.py:319
  231.8 13.9 %collective-permute-start.60 = (bf16[16,64,128]{2,1,0:T(8,128)(2,1)S(1)}, bf16[16,64,128]{2,1,0:T(8,128)(2,1)S(1)}, u32[]{:S(2)}, u32[]{:S(2)}) collective-permute-start(bf16[16,64,128]{2,1,0:T(8,128)(2,1)S(1)} %get-tuple-element.57), channel_id=1, source_target_pairs={{8,0},{16,8},{24,16},{28,24},{20,28},{12,20},{4,12},{0,4},{9,1},{1... | collective-permute-start | bytes 786440 | tf_op jit(solution)/shard_map/ppermute | solution.py:320
  243.7 9.2 %collective-permute-start.43 = (bf16[16,64,128]{2,1,0:T(8,128)(2,1)S(1)}, bf16[16,64,128]{2,1,0:T(8,128)(2,1)S(1)}, u32[]{:S(2)}, u32[]{:S(2)}) collective-permute-start(bf16[16,64,128]{2,1,0:T(8,128)(2,1)S(1)} %get-tuple-element.68), channel_id=1, source_target_pairs={{0,8},{8,16},{16,24},{24,28},{28,20},{20,12},{12,4},{4,0},{1,9},{9... | collective-permute-start | bytes 786440 | tf_op jit(solution)/shard_map/ppermute | solution.py:319
  247.0 10.8 %collective-permute-start.55 = (bf16[16,64,128]{2,1,0:T(8,128)(2,1)S(1)}, bf16[16,64,128]{2,1,0:T(8,128)(2,1)S(1)}, u32[]{:S(2)}, u32[]{:S(2)}) collective-permute-start(bf16[16,64,128]{2,1,0:T(8,128)(2,1)S(1)} %get-tuple-element.54), channel_id=1, source_target_pairs={{0,8},{8,16},{16,24},{24,28},{28,20},{20,12},{12,4},{4,0},{1,9},{9... | collective-permute-start | bytes 786440 | tf_op jit(solution)/shard_map/ppermute | solution.py:319
  248.1 11.3 %collective-permute-start.61 = (bf16[16,64,128]{2,1,0:T(8,128)(2,1)S(1)}, bf16[16,64,128]{2,1,0:T(8,128)(2,1)S(1)}, u32[]{:S(2)}, u32[]{:S(2)}) collective-permute-start(bf16[16,64,128]{2,1,0:T(8,128)(2,1)S(1)} %get-tuple-element.55), channel_id=1, source_target_pairs={{8,0},{16,8},{24,16},{28,24},{20,28},{12,20},{4,12},{0,4},{9,1},{1... | collective-permute-start | bytes 786440 | tf_op jit(solution)/shard_map/ppermute | solution.py:320
  (43 other events, 774.7 us)
Sparse Core Ops, SparseCore 0:
  25.8 14.9 all-gather.2
  79.3 17.4 all-gather.4
  199.1 25.1 reduce-scatter.2
  242.6 24.2 reduce-scatter.4

commit v3 on v2

--- a/solution.py
+++ b/solution.py
@@ -11,6 +11,7 @@
 FF = 16384
 BLK = 128
 PACK = 16
+WEIGHT = 16
 VMEM_LIMIT = 56 << 20
 
 gelu_root = 0.7978845608028654
@@ -208,17 +209,10 @@
 def sum_blocks(acc, live, sides, target, term, fetch):
     acc[...] = jnp.zeros_like(acc)
     count = live // sides
-    unroll = unroll_of(count)
     for side in range(sides):
         fetch(side)
-
-        def body(i, carry, first=side * count):
-            products = [term(first + i * unroll + u) for u in range(unroll)]
-            for u in range(unroll):
-                acc[target(first + i * unroll + u)] += products[u]
-            return carry
-
-        lax.fori_loop(0, count // unroll, body, 0)
+        for k in range(side * count, (side + 1) * count):
+            acc[target(k)] += term(k)
 
 
 def fetch_of(need, item, sides):
@@ -380,7 +374,7 @@
     down_slots = down_blocks.reshape(slots, BLK, BLK)
     codes = jnp.stack([up_place.reshape(1, slots), down_place.reshape(1, slots)])
 
-    flops = 2 * live * row_count * BLK * BLK * 4
+    flops = 2 * live * row_count * BLK * BLK * WEIGHT
     block_bytes = live * BLK * BLK * 2
     side = row_count * BLK
     group_acc = pltpu.VMEM((group_blocks, row_count, BLK), jnp.float32)
@@ -446,14 +440,14 @@
         def onward(pair):
             return lax.ppermute(pair[0], "dp", ahead), lax.ppermute(pair[1], "dp", behind)
 
-        def ring(pair):
-            pairs = [pair]
-            for _ in range(1, devices):
-                pairs.append(onward(pairs[-1]))
-            return Joined(*zip(*pairs, strict=True), (from_ahead, from_behind))
-
         packed = pack_pieces(pick, parts, slots, live)
-        up, down = ring(packed[:2]), ring(packed[2:])
+        tok_turned = tok.T
+
+        up_ring, down_ring = [tuple(packed[:2])], [tuple(packed[2:])]
+        for s in range(1, devices):
+            up_ring.append(onward(tie(up_ring[-1], tok_turned) if s == devices // 2 else up_ring[-1]))
+            down_ring.append(onward(down_ring[-1]))
+        up, down = (Joined(*zip(*pairs, strict=True), (from_ahead, from_behind)) for pairs in (up_ring, down_ring))
     else:
 
         def everywhere(x, axis):
@@ -462,13 +456,14 @@
         pick, rows, cols = tables(everywhere(row_codes, 1), everywhere(col_codes, 1), index)
         tok = lax.all_gather(tokens, "tensor", axis=0, tiled=True)
         cot = lax.all_gather(cotangent, "tensor", axis=0, tiled=True)
+        tok_turned = tok.T
         up = Whole(jnp.take(everywhere(up_slots, 0), pick[0], axis=0))
         down = Whole(jnp.take(everywhere(down_slots, 0), pick[1], axis=0))
 
     hid, slope, terms = hidden_of(rows, cols, tok, cot, up)
     down_sum = RingSum(terms, ahead, behind)
     down_sum.step()
-    grad_pre, terms = grad_pre_of(rows, cols, tie(cot, down_sum.run), down, slope, tok.T)
+    grad_pre, terms = grad_pre_of(rows, cols, cot, down, slope, tok_turned)
     up_sum = RingSum(terms, ahead, behind)
     up_sum.step()
     out_part = width(0, rows[1], cols[1], tie(hid, up_sum.run), down)

time: 281 us -> 264 us (0.940)
  waiting for transfers between devices: 102 us -> 90.9 us
  Pallas kernels: 49.7 us -> 42 us
    ppermute x14, waiting for transfers between devices: 18.8 us -> 9.35 us  [step(): b = lax.ppermute(b, 'dp', self.behind)]
    pallas_call x6, Pallas kernels: 49.7 us -> 42 us  [run(): pl.pallas_call(body, out_shape=list(outs), in_specs=[SMEM_SPEC] * (len(sm...]
    ppermute x14, waiting for transfers between devices: 34.1 us -> 30.8 us  [onward(): lax.ppermute(pair[0], 'dp', ahead)]
  transfers between devices with their start and end apart: 67 -> 67, of which waited for: 49 -> 38; matrix products, arithmetic and copies ran while one was open for 9% -> 11% of each run, Pallas kernels for 10% -> 15%
where the time goes in v3:
time: 264 us; the launch traced here: 263 us
  waiting for transfers between devices  90.9 us (34%)
  starting transfers between devices  86.4 us (33%)
  Pallas kernels  42 us (16%)
  other arithmetic  20 us (8%)
  between operations  14.3 us (5%)
  local copies, waits for them, and re-layouts  9.96 us (4%)
    ppermute x14, starting transfers between devices, onward(): lax.ppermute(pair[0], 'dp', ahead)  43.3 us
    pallas_call x6, Pallas kernels, run(): pl.pallas_call(body, out_shape=list(outs), in_specs=[SMEM_SPEC] * (len(sm...  42 us
    ppermute x14, waiting for transfers between devices, onward(): lax.ppermute(pair[0], 'dp', ahead)  30.8 us
    ppermute x7, waiting for transfers between devices, shards(): lax.ppermute(messages[s], 'dp', [(i, i ^ s) for i in range(devices)])  30.3 us
    ppermute x14, starting transfers between devices, step(): a = lax.ppermute(a, 'dp', self.ahead)  15.2 us
    convert_element_type x12, other arithmetic, step(): a, b = (a.astype(jnp.bfloat16), b.astype(jnp.bfloat16))  14.6 us
    ppermute x14, starting transfers between devices, step(): b = lax.ppermute(b, 'dp', self.behind)  13.9 us
    ppermute x7, starting transfers between devices, shards(): lax.ppermute(messages[s], 'dp', [(i, i ^ s) for i in range(devices)])  13.7 us
  transfers between devices with their start and end apart: 67, of which 38 were waited for; matrix products, arithmetic and copies ran while one was open for 11% of the time, Pallas kernels for 15%

profile of v3, /device:TPU:0, one launch (start us, length us, event | category | flops | bytes accessed | tf_op | source)
XLA Modules:
  0.0 263.5 jit_solution(6805439001235924367)
XLA Ops:
  9.2 3.0 %shard_map.111 = (bf16[65,16,128]{2,1,0:T(8,128)(2,1)}, bf16[65,16,128]{2,1,0:T(8,128)(2,1)}, bf16[65,16,128]{2,1,0:T(8,128)(2,1)}, bf16[65,16,128]{2,1,0:T(8,12...) custom-call(s32[1]{0:T(128)} %bitcast.refs_0_, ...), custom_call_target="tpu_custom_call" | custom-call | bytes 4194304 | tf_op jit(solution)/shard_map/pallas_call | solution.py:145
  12.2 3.0 %collective-permute-start = (bf16[65,16,128]{2,1,0:T(8,128)(2,1)}, bf16[65,16,128]{2,1,0:T(8,128)(2,1)S(1)}, u32[]{:S(2)}, u32[]{:S(2)}) collective-permute-start(bf16[65,16,128]{2,1,0:T(8,128)(2,1)} %get-tuple-element.28), channel_id=1, source_target_pairs={{0,4},{4,0},{8,12},{12,8},{16,20},{20,16},{24,28},{28,24},{1,5},{5... | collective-permute-start | bytes 798728 | tf_op jit(solution)/shard_map/ppermute | solution.py:429
  16.8 3.0 %collective-permute-start.3 = (bf16[65,16,128]{2,1,0:T(8,128)(2,1)}, bf16[65,16,128]{2,1,0:T(8,128)(2,1)S(1)}, u32[]{:S(2)}, u32[]{:S(2)}) collective-permute-start(bf16[65,16,128]{2,1,0:T(8,128)(2,1)} %get-tuple-element.31), channel_id=1, source_target_pairs={{0,16},{4,20},{8,24},{12,28},{16,0},{20,4},{24,8},{28,12},{1,17},{... | collective-permute-start | bytes 798728 | tf_op jit(solution)/shard_map/ppermute | solution.py:429
  21.8 3.8 %collective-permute-start.5 = (bf16[65,16,128]{2,1,0:T(8,128)(2,1)}, bf16[65,16,128]{2,1,0:T(8,128)(2,1)S(1)}, u32[]{:S(2)}, u32[]{:S(2)}) collective-permute-start(bf16[65,16,128]{2,1,0:T(8,128)(2,1)} %get-tuple-element.33), channel_id=1, source_target_pairs={{0,24},{4,28},{8,16},{12,20},{16,8},{20,12},{24,0},{28,4},{1,25},{... | collective-permute-start | bytes 798728 | tf_op jit(solution)/shard_map/ppermute | solution.py:429
  25.7 9.4 %collective-permute-done.1.refs_4_ = bf16[65,16,128]{2,1,0:T(8,128)(2,1)S(1)} collective-permute-done((bf16[65,16,128]{2,1,0:T(8,128)(2,1)}, bf16[65,16,128]{2,1,0:T(8,128)(2,1)S(1)}, u32[]{:S(2)}, u32[]{:S(2)}) %collective-permute-start.1) | collective-permute-done | bytes 266272 | tf_op jit(solution)/shard_map/ppermute | solution.py:429
  36.2 2.3 collective-permute-done.2.refs_5_
  38.6 18.5 %collective-permute-done.4.refs_7_ = bf16[65,16,128]{2,1,0:T(8,128)(2,1)S(1)} collective-permute-done((bf16[65,16,128]{2,1,0:T(8,128)(2,1)}, bf16[65,16,128]{2,1,0:T(8,128)(2,1)S(1)}, u32[]{:S(2)}, u32[]{:S(2)}) %collective-permute-start.4) | collective-permute-done | bytes 266272 | tf_op jit(solution)/shard_map/ppermute | solution.py:429
  58.4 3.4 %shard_map.112 = (bf16[64,16,128]{2,1,0:T(8,128)(2,1)}, bf16[64,16,128]{2,1,0:T(8,128)(2,1)}, bf16[64,16,128]{2,1,0:T(8,128)(2,1)}, bf16[64,16,128]{2,1,0:T(8,128)(2,1)}) custom-call(s32[128]{0:T(128)} %get-tuple-element.91.refs_0_, s32[128]{0:T(128)} %get-tuple-element.90.refs_1_, bf16[65,16,128]{2,1,0:T(8,128)(2,1)} %get-tuple-element.27.refs_2_, ...), custom_call_target="tpu_custom_call" | custom-call | bytes 3145728 | tf_op jit(solution)/shard_map/pallas_call | solution.py:145
  61.8 10.0 %collective-permute-start.7 = (bf16[64,16,128]{2,1,0:T(8,128)(2,1)}, bf16[64,16,128]{2,1,0:T(8,128)(2,1)S(1)}, u32[]{:S(2)}, u32[]{:S(2)}) collective-permute-start(bf16[64,16,128]{2,1,0:T(8,128)(2,1)} %get-tuple-element.36.refs_8_.refs_5_), channel_id=1, source_target_pairs={{0,8},{8,16},{16,24},{24,28},{28,20},{20,12},{12,4},{4,0},{1,9},{9... | collective-permute-start | bytes 786440 | tf_op jit(solution)/shard_map/ppermute | solution.py:441
  71.8 2.7 %collective-permute-start.21 = (bf16[64,16,128]{2,1,0:T(8,128)(2,1)}, bf16[64,16,128]{2,1,0:T(8,128)(2,1)S(1)}, u32[]{:S(2)}, u32[]{:S(2)}) collective-permute-start(bf16[64,16,128]{2,1,0:T(8,128)(2,1)} %get-tuple-element.42.refs_8_.refs_5_), channel_id=1, source_target_pairs={{0,8},{8,16},{16,24},{24,28},{28,20},{20,12},{12,4},{4,0},{1,9},{9... | collective-permute-start | bytes 786440 | tf_op jit(solution)/shard_map/ppermute | solution.py:441
  74.5 4.4 %collective-permute-done.7.refs_9_.refs_6_ = bf16[64,16,128]{2,1,0:T(8,128)(2,1)S(1)} collective-permute-done((bf16[64,16,128]{2,1,0:T(8,128)(2,1)}, bf16[64,16,128]{2,1,0:T(8,128)(2,1)S(1)}, u32[]{:S(2)}, u32[]{:S(2)}) %collective-permute-start.7) | collective-permute-done | bytes 262176 | tf_op jit(solution)/shard_map/ppermute | solution.py:441
  78.8 2.7 %collective-permute-start.8 = (bf16[64,16,128]{2,1,0:T(8,128)(2,1)S(1)}, bf16[64,16,128]{2,1,0:T(8,128)(2,1)S(1)}, u32[]{:S(2)}, u32[]{:S(2)}) collective-permute-start(bf16[64,16,128]{2,1,0:T(8,128)(2,1)S(1)} %collective-permute-done.7.refs_9_.refs_6_), channel_id=1, source_target_pairs={{0,8},{8,16},{16,24},{24,28},{28,20},{20,12},{12,4},{4,0},{1,9},{9... | collective-permute-start | bytes 786440 | tf_op jit(solution)/shard_map/ppermute | solution.py:441
  82.0 2.5 collective-permute-done.21.refs_9_.refs_6_
  84.5 2.7 %collective-permute-start.22 = (bf16[64,16,128]{2,1,0:T(8,128)(2,1)S(1)}, bf16[64,16,128]{2,1,0:T(8,128)(2,1)S(1)}, u32[]{:S(2)}, u32[]{:S(2)}) collective-permute-start(bf16[64,16,128]{2,1,0:T(8,128)(2,1)S(1)} %collective-permute-done.21.refs_9_.refs_6_), channel_id=1, source_target_pairs={{0,8},{8,16},{16,24},{24,28},{28,20},{20,12},{12,4},{4,0},{1,9},{9... | collective-permute-start | bytes 786440 | tf_op jit(solution)/shard_map/ppermute | solution.py:441
  87.5 2.4 collective-permute-done.8.refs_10_.refs_7_
  90.0 2.7 %collective-permute-start.9 = (bf16[64,16,128]{2,1,0:T(8,128)(2,1)S(1)}, bf16[64,16,128]{2,1,0:T(8,128)(2,1)S(1)}, u32[]{:S(2)}, u32[]{:S(2)}) collective-permute-start(bf16[64,16,128]{2,1,0:T(8,128)(2,1)S(1)} %collective-permute-done.8.refs_10_.refs_7_), channel_id=1, source_target_pairs={{0,8},{8,16},{16,24},{24,28},{28,20},{20,12},{12,4},{4,0},{1,9},{9... | collective-permute-start | bytes 786440 | tf_op jit(solution)/shard_map/ppermute | solution.py:441
  93.1 2.4 collective-permute-done.22.refs_10_.refs_7_
  95.6 2.7 %collective-permute-start.23 = (bf16[64,16,128]{2,1,0:T(8,128)(2,1)S(1)}, bf16[64,16,128]{2,1,0:T(8,128)(2,1)S(1)}, u32[]{:S(2)}, u32[]{:S(2)}) collective-permute-start(bf16[64,16,128]{2,1,0:T(8,128)(2,1)S(1)} %collective-permute-done.22.refs_10_.refs_7_), channel_id=1, source_target_pairs={{0,8},{8,16},{16,24},{24,28},{28,20},{20,12},{12,4},{4,0},{1,9},{9... | collective-permute-start | bytes 786440 | tf_op jit(solution)/shard_map/ppermute | solution.py:441
  98.8 2.4 copy.27
  101.2 3.2 %collective-permute-done.12.refs_19_.refs_16_ = bf16[64,16,128]{2,1,0:T(8,128)(2,1)S(1)} collective-permute-done((bf16[64,16,128]{2,1,0:T(8,128)(2,1)S(1)}, bf16[64,16,128]{2,1,0:T(8,128)(2,1)S(1)}, u32[]{:S(2)}, u32[]{:S(2)}) %collective-permute-start.12) | collective-permute-done | bytes 262176 | tf_op jit(solution)/shard_map/ppermute | solution.py:441
  104.4 2.1 collective-permute-start.13
  106.8 2.7 %collective-permute-start.24 = (bf16[64,16,128]{2,1,0:T(8,128)(2,1)S(1)}, bf16[64,16,128]{2,1,0:T(8,128)(2,1)}, u32[]{:S(2)}, u32[]{:S(2)}) collective-permute-start(bf16[64,16,128]{2,1,0:T(8,128)(2,1)S(1)} %collective-permute-done.23.refs_11_.refs_8_), channel_id=1, source_target_pairs={{0,8},{8,16},{16,24},{24,28},{28,20},{20,12},{12,4},{4,0},{1,9},{9... | collective-permute-start | bytes 786440 | tf_op jit(solution)/shard_map/ppermute | solution.py:441
  110.0 3.2 %collective-permute-done.13.refs_12_.refs_9_ = bf16[64,16,128]{2,1,0:T(8,128)(2,1)S(1)} collective-permute-done((bf16[64,16,128]{2,1,0:T(8,128)(2,1)S(1)}, bf16[64,16,128]{2,1,0:T(8,128)(2,1)S(1)}, u32[]{:S(2)}, u32[]{:S(2)}) %collective-permute-start.13) | collective-permute-done | bytes 262176 | tf_op jit(solution)/shard_map/ppermute | solution.py:441
  113.2 2.5 collective-permute-start.14
  115.8 3.1 %collective-permute-done.24.refs_12_.refs_9_ = bf16[64,16,128]{2,1,0:T(8,128)(2,1)} collective-permute-done((bf16[64,16,128]{2,1,0:T(8,128)(2,1)S(1)}, bf16[64,16,128]{2,1,0:T(8,128)(2,1)}, u32[]{:S(2)}, u32[]{:S(2)}) %collective-permute-start.24) | collective-permute-done | bytes 262176 | tf_op jit(solution)/shard_map/ppermute | solution.py:441
  118.8 2.6 collective-permute-start.25
  121.4 3.0 %collective-permute-done.14.refs_13_.refs_10_ = bf16[64,16,128]{2,1,0:T(8,128)(2,1)S(1)} collective-permute-done((bf16[64,16,128]{2,1,0:T(8,128)(2,1)S(1)}, bf16[64,16,128]{2,1,0:T(8,128)(2,1)S(1)}, u32[]{:S(2)}, u32[]{:S(2)}) %collective-permute-start.14) | collective-permute-done | bytes 262176 | tf_op jit(solution)/shard_map/ppermute | solution.py:441
  124.4 2.5 collective-permute-start.15
  130.2 2.5 collective-permute-start.26
  132.7 3.0 %collective-permute-done.15.refs_14_.refs_11_ = bf16[64,16,128]{2,1,0:T(8,128)(2,1)S(1)} collective-permute-done((bf16[64,16,128]{2,1,0:T(8,128)(2,1)S(1)}, bf16[64,16,128]{2,1,0:T(8,128)(2,1)S(1)}, u32[]{:S(2)}, u32[]{:S(2)}) %collective-permute-start.15) | collective-permute-done | bytes 262176 | tf_op jit(solution)/shard_map/ppermute | solution.py:441
  135.7 2.5 collective-permute-start.16
  139.0 2.4 collective-permute-done.26.refs_14_.refs_11_
  141.4 2.5 collective-permute-start.27
  143.9 2.1 collective-permute-done.16.refs_15_.refs_12_
  146.0 3.3 %collective-permute-done.20.refs_23_.refs_20_ = bf16[64,16,128]{2,1,0:T(8,128)(2,1)} collective-permute-done((bf16[64,16,128]{2,1,0:T(8,128)(2,1)S(1)}, bf16[64,16,128]{2,1,0:T(8,128)(2,1)}, u32[]{:S(2)}, u32[]{:S(2)}) %collective-permute-start.20) | collective-permute-done | bytes 262176 | tf_op jit(solution)/shard_map/ppermute | solution.py:441
  149.4 12.1 %shard_map.113 = (bf16[32,128,128]{2,1,0:T(8,128)(2,1)}, f32[32,128,128]{2,1,0:T(8,128)}, bf16[8,16,128,128]{3,2,1,0:T(8,128)(2,1)}) custom-call(s32[8]{0:T(128)} %get-tuple-element.87.refs_0_, s32[128]{0:T(128)} %get-tuple-element.99.refs_1_.refs_3_.refs_0_, s32[128]{0:T(128)} %get-tuple-element.92.refs_2_.refs_4_.refs_1_, ...), custom_call_target="tpu_custom_call" | custom-call | flops 17179869184 | bytes 13631488 | tf_op jit(solution)/shard_map/pallas_call | solution.py:145
  164.7 9.4 %shard_map.114 = (bf16[32,128,128]{2,1,0:T(8,128)(2,1)}, bf16[8,16,128,128]{3,2,1,0:T(8,128)(2,1)}) custom-call(s32[8]{0:T(128)} %get-tuple-element.87.refs_0_, s32[128]{0:T(128)} %get-tuple-element.98.refs_3_.refs_1_.refs_0_, s32[128]{0:T(128)} %get-tuple-element.93.refs_4_.refs_2_.refs_1_, s32[128]{0:T(128)} %get-tuple-element.99.refs_1_.refs_3_.refs_0_, ...), custom_call_target="tpu_custom_call" | custom-call | flops 17179869184 | bytes 13631488 | tf_op jit(solution)/shard_map/pallas_call | solution.py:145
  175.2 2.0 collective-permute-start.35
  180.6 3.5 %collective-permute-done.36 = bf16[16,64,128]{2,1,0:T(8,128)(2,1)S(1)} collective-permute-done((bf16[16,64,128]{2,1,0:T(8,128)(2,1)S(1)}, bf16[16,64,128]{2,1,0:T(8,128)(2,1)S(1)}, u32[]{:S(2)}, u32[]{:S(2)}) %collective-permute-start.36) | collective-permute-done | bytes 262176 | tf_op jit(solution)/shard_map/ppermute | solution.py:314
  187.6 6.3 %shard_map.115 = bf16[128,4096]{1,0:T(8,128)(2,1)} custom-call(s32[128]{0:T(128)} %get-tuple-element.98.refs_3_.refs_1_.refs_0_, s32[128]{0:T(128)} %get-tuple-element.93.refs_4_.refs_2_.refs_1_, s32[8]{0:T(128)} %get-tuple-element.89.refs_5_.refs_2_, s32[8]{0:T(128)} %get-tuple-element.88.refs_6_.refs_3_, bf16[32,128,128]{2,1,0:T(8,128)(2,1)} %get-tuple-element.46.refs_4_, ...), custom_call_target="tpu_custom_call" | custom-call | flops 8589934592 | bytes 6291456 | tf_op jit(solution)/shard_map/pallas_call | solution.py:145
  200.6 3.8 %collective-permute-done.51 = bf16[16,64,128]{2,1,0:T(8,128)(2,1)S(1)} collective-permute-done((bf16[16,64,128]{2,1,0:T(8,128)(2,1)S(1)}, bf16[16,64,128]{2,1,0:T(8,128)(2,1)S(1)}, u32[]{:S(2)}, u32[]{:S(2)}) %collective-permute-start.51) | collective-permute-done | bytes 262176 | tf_op jit(solution)/shard_map/ppermute | solution.py:313
  206.8 1.9 collective-permute-start.52
  208.9 2.3 collective-permute-done.44
  219.6 7.8 %shard_map.116 = bf16[128,4096]{1,0:T(8,128)(2,1)} custom-call(s32[128]{0:T(128)} %get-tuple-element.99.refs_1_.refs_3_.refs_0_, s32[128]{0:T(128)} %get-tuple-element.92.refs_2_.refs_4_.refs_1_, s32[8]{0:T(128)} %get-tuple-element.89.refs_5_.refs_2_, s32[8]{0:T(128)} %get-tuple-element.88.refs_6_.refs_3_, bf16[32,128,128]{2,1,0:T(8,128)(2,1)} %get-tuple-element.48.refs_4_, ...), custom_call_target="tpu_custom_call" | custom-call | flops 8589934592 | bytes 6291456 | tf_op jit(solution)/shard_map/pallas_call | solution.py:145
  234.0 3.5 %collective-permute-done.41 = bf16[16,64,128]{2,1,0:T(8,128)(2,1)S(1)} collective-permute-done((bf16[16,64,128]{2,1,0:T(8,128)(2,1)S(1)}, bf16[16,64,128]{2,1,0:T(8,128)(2,1)S(1)}, u32[]{:S(2)}, u32[]{:S(2)}) %collective-permute-start.41) | collective-permute-done | bytes 262176 | tf_op jit(solution)/shard_map/ppermute | solution.py:313
  239.1 2.0 collective-permute-start.47
  241.1 2.1 collective-permute-done.54
  244.7 2.0 collective-permute-start.62
  (198 shorter events, 63.4 us)
Async XLA Ops:
  7.2 91.6 %all-gather.3.cloned.1.call-start = ((), (), s32[]{:S(2)}) async-start(), calls=%async_computation.2 | async-start | bytes 1310720 | tf_op jit(solution)/shard_map/all_gather | solution.py:437
  15.2 20.0 %collective-permute-start.1 = (bf16[65,16,128]{2,1,0:T(8,128)(2,1)}, bf16[65,16,128]{2,1,0:T(8,128)(2,1)S(1)}, u32[]{:S(2)}, u32[]{:S(2)}) collective-permute-start(bf16[65,16,128]{2,1,0:T(8,128)(2,1)} %get-tuple-element.29), channel_id=1, source_target_pairs={{0,8},{4,12},{8,0},{12,4},{16,24},{20,28},{24,16},{28,20},{1,9},{5... | collective-permute-start | bytes 798728 | tf_op jit(solution)/shard_map/ppermute | solution.py:429
  16.8 21.8 %collective-permute-start.2 = (bf16[65,16,128]{2,1,0:T(8,128)(2,1)}, bf16[65,16,128]{2,1,0:T(8,128)(2,1)S(1)}, u32[]{:S(2)}, u32[]{:S(2)}) collective-permute-start(bf16[65,16,128]{2,1,0:T(8,128)(2,1)} %get-tuple-element.30), channel_id=1, source_target_pairs={{0,12},{4,8},{8,4},{12,0},{16,28},{20,24},{24,20},{28,16},{1,13},{... | collective-permute-start | bytes 798728 | tf_op jit(solution)/shard_map/ppermute | solution.py:429
  16.8 21.8 %collective-permute-start.3 = (bf16[65,16,128]{2,1,0:T(8,128)(2,1)}, bf16[65,16,128]{2,1,0:T(8,128)(2,1)S(1)}, u32[]{:S(2)}, u32[]{:S(2)}) collective-permute-start(bf16[65,16,128]{2,1,0:T(8,128)(2,1)} %get-tuple-element.31), channel_id=1, source_target_pairs={{0,16},{4,20},{8,24},{12,28},{16,0},{20,4},{24,8},{28,12},{1,17},{... | collective-permute-start | bytes 798728 | tf_op jit(solution)/shard_map/ppermute | solution.py:429
  19.8 37.3 %collective-permute-start.4 = (bf16[65,16,128]{2,1,0:T(8,128)(2,1)}, bf16[65,16,128]{2,1,0:T(8,128)(2,1)S(1)}, u32[]{:S(2)}, u32[]{:S(2)}) collective-permute-start(bf16[65,16,128]{2,1,0:T(8,128)(2,1)} %get-tuple-element.32), channel_id=1, source_target_pairs={{0,20},{4,16},{8,28},{12,24},{16,4},{20,0},{24,12},{28,8},{1,21},{... | collective-permute-start | bytes 798728 | tf_op jit(solution)/shard_map/ppermute | solution.py:429
  21.8 35.3 %collective-permute-start.5 = (bf16[65,16,128]{2,1,0:T(8,128)(2,1)}, bf16[65,16,128]{2,1,0:T(8,128)(2,1)S(1)}, u32[]{:S(2)}, u32[]{:S(2)}) collective-permute-start(bf16[65,16,128]{2,1,0:T(8,128)(2,1)} %get-tuple-element.33), channel_id=1, source_target_pairs={{0,24},{4,28},{8,16},{12,20},{16,8},{20,12},{24,0},{28,4},{1,25},{... | collective-permute-start | bytes 798728 | tf_op jit(solution)/shard_map/ppermute | solution.py:429
  25.7 118.2 %all-gather.5.cloned.1.call-start = ((), (), s32[]{:S(2)}) async-start(), calls=%async_computation.3 | async-start | bytes 1310720 | tf_op jit(solution)/shard_map/all_gather | solution.py:438
  35.2 21.9 %collective-permute-start.6 = (bf16[65,16,128]{2,1,0:T(8,128)(2,1)}, bf16[65,16,128]{2,1,0:T(8,128)(2,1)S(1)}, u32[]{:S(2)}, u32[]{:S(2)}) collective-permute-start(bf16[65,16,128]{2,1,0:T(8,128)(2,1)} %get-tuple-element.34), channel_id=1, source_target_pairs={{0,28},{4,24},{8,20},{12,16},{16,12},{20,8},{24,4},{28,0},{1,29},{... | collective-permute-start | bytes 798728 | tf_op jit(solution)/shard_map/ppermute | solution.py:429
  61.8 17.1 %collective-permute-start.7 = (bf16[64,16,128]{2,1,0:T(8,128)(2,1)}, bf16[64,16,128]{2,1,0:T(8,128)(2,1)S(1)}, u32[]{:S(2)}, u32[]{:S(2)}) collective-permute-start(bf16[64,16,128]{2,1,0:T(8,128)(2,1)} %get-tuple-element.36.refs_8_.refs_5_), channel_id=1, source_target_pairs={{0,8},{8,16},{16,24},{24,28},{28,20},{20,12},{12,4},{4,0},{1,9},{9... | collective-permute-start | bytes 786440 | tf_op jit(solution)/shard_map/ppermute | solution.py:441
  71.8 12.7 %collective-permute-start.21 = (bf16[64,16,128]{2,1,0:T(8,128)(2,1)}, bf16[64,16,128]{2,1,0:T(8,128)(2,1)S(1)}, u32[]{:S(2)}, u32[]{:S(2)}) collective-permute-start(bf16[64,16,128]{2,1,0:T(8,128)(2,1)} %get-tuple-element.42.refs_8_.refs_5_), channel_id=1, source_target_pairs={{0,8},{8,16},{16,24},{24,28},{28,20},{20,12},{12,4},{4,0},{1,9},{9... | collective-permute-start | bytes 786440 | tf_op jit(solution)/shard_map/ppermute | solution.py:441
  74.5 13.0 %collective-permute-start.28 = (bf16[64,16,128]{2,1,0:T(8,128)(2,1)}, bf16[64,16,128]{2,1,0:T(8,128)(2,1)S(1)}, u32[]{:S(2)}, u32[]{:S(2)}) collective-permute-start(bf16[64,16,128]{2,1,0:T(8,128)(2,1)} %get-tuple-element.43.refs_16_.refs_13_), channel_id=1, source_target_pairs={{8,0},{16,8},{24,16},{28,24},{20,28},{12,20},{4,12},{0,4},{9,1},{1... | collective-permute-start | bytes 786440 | tf_op jit(solution)/shard_map/ppermute | solution.py:441
  78.8 11.1 %collective-permute-start.8 = (bf16[64,16,128]{2,1,0:T(8,128)(2,1)S(1)}, bf16[64,16,128]{2,1,0:T(8,128)(2,1)S(1)}, u32[]{:S(2)}, u32[]{:S(2)}) collective-permute-start(bf16[64,16,128]{2,1,0:T(8,128)(2,1)S(1)} %collective-permute-done.7.refs_9_.refs_6_), channel_id=1, source_target_pairs={{0,8},{8,16},{16,24},{24,28},{28,20},{20,12},{12,4},{4,0},{1,9},{9... | collective-permute-start | bytes 786440 | tf_op jit(solution)/shard_map/ppermute | solution.py:441
  81.9 11.2 %collective-permute-start.11 = (bf16[64,16,128]{2,1,0:T(8,128)(2,1)S(1)}, bf16[64,16,128]{2,1,0:T(8,128)(2,1)S(1)}, u32[]{:S(2)}, u32[]{:S(2)}) collective-permute-start(bf16[64,16,128]{2,1,0:T(8,128)(2,1)S(1)} %collective-permute-done.10.refs_17_.refs_14_), channel_id=1, source_target_pairs={{8,0},{16,8},{24,16},{28,24},{20,28},{12,20},{4,12},{0,4},{9,1},{1... | collective-permute-start | bytes 786440 | tf_op jit(solution)/shard_map/ppermute | solution.py:441
  81.9 175.0 %reduce-scatter.3.cloned.1.call-start = ((), (), s32[]{:S(2)}) async-start(), calls=%async_computation.4 | async-start | bytes 1310720 | tf_op jit(solution)/shard_map/reduce_scatter | solution.py:472
  84.5 11.1 %collective-permute-start.22 = (bf16[64,16,128]{2,1,0:T(8,128)(2,1)S(1)}, bf16[64,16,128]{2,1,0:T(8,128)(2,1)S(1)}, u32[]{:S(2)}, u32[]{:S(2)}) collective-permute-start(bf16[64,16,128]{2,1,0:T(8,128)(2,1)S(1)} %collective-permute-done.21.refs_9_.refs_6_), channel_id=1, source_target_pairs={{0,8},{8,16},{16,24},{24,28},{28,20},{20,12},{12,4},{4,0},{1,9},{9... | collective-permute-start | bytes 786440 | tf_op jit(solution)/shard_map/ppermute | solution.py:441
  87.5 11.2 %collective-permute-start.29 = (bf16[64,16,128]{2,1,0:T(8,128)(2,1)S(1)}, bf16[64,16,128]{2,1,0:T(8,128)(2,1)S(1)}, u32[]{:S(2)}, u32[]{:S(2)}) collective-permute-start(bf16[64,16,128]{2,1,0:T(8,128)(2,1)S(1)} %collective-permute-done.28.refs_17_.refs_14_), channel_id=1, source_target_pairs={{8,0},{16,8},{24,16},{28,24},{20,28},{12,20},{4,12},{0,4},{9,1},{1... | collective-permute-start | bytes 786440 | tf_op jit(solution)/shard_map/ppermute | solution.py:441
  90.0 11.2 %collective-permute-start.9 = (bf16[64,16,128]{2,1,0:T(8,128)(2,1)S(1)}, bf16[64,16,128]{2,1,0:T(8,128)(2,1)S(1)}, u32[]{:S(2)}, u32[]{:S(2)}) collective-permute-start(bf16[64,16,128]{2,1,0:T(8,128)(2,1)S(1)} %collective-permute-done.8.refs_10_.refs_7_), channel_id=1, source_target_pairs={{0,8},{8,16},{16,24},{24,28},{28,20},{20,12},{12,4},{4,0},{1,9},{9... | collective-permute-start | bytes 786440 | tf_op jit(solution)/shard_map/ppermute | solution.py:441
  93.1 11.2 %collective-permute-start.12 = (bf16[64,16,128]{2,1,0:T(8,128)(2,1)S(1)}, bf16[64,16,128]{2,1,0:T(8,128)(2,1)S(1)}, u32[]{:S(2)}, u32[]{:S(2)}) collective-permute-start(bf16[64,16,128]{2,1,0:T(8,128)(2,1)S(1)} %collective-permute-done.11.refs_18_.refs_15_), channel_id=1, source_target_pairs={{8,0},{16,8},{24,16},{28,24},{20,28},{12,20},{4,12},{0,4},{9,1},{1... | collective-permute-start | bytes 786440 | tf_op jit(solution)/shard_map/ppermute | solution.py:441
  95.6 11.2 %collective-permute-start.23 = (bf16[64,16,128]{2,1,0:T(8,128)(2,1)S(1)}, bf16[64,16,128]{2,1,0:T(8,128)(2,1)S(1)}, u32[]{:S(2)}, u32[]{:S(2)}) collective-permute-start(bf16[64,16,128]{2,1,0:T(8,128)(2,1)S(1)} %collective-permute-done.22.refs_10_.refs_7_), channel_id=1, source_target_pairs={{0,8},{8,16},{16,24},{24,28},{28,20},{20,12},{12,4},{4,0},{1,9},{9... | collective-permute-start | bytes 786440 | tf_op jit(solution)/shard_map/ppermute | solution.py:441
  98.8 11.2 %collective-permute-start.30 = (bf16[64,16,128]{2,1,0:T(8,128)(2,1)S(1)}, bf16[64,16,128]{2,1,0:T(8,128)(2,1)S(1)}, u32[]{:S(2)}, u32[]{:S(2)}) collective-permute-start(bf16[64,16,128]{2,1,0:T(8,128)(2,1)S(1)} %collective-permute-done.29.refs_18_.refs_15_), channel_id=1, source_target_pairs={{8,0},{16,8},{24,16},{28,24},{20,28},{12,20},{4,12},{0,4},{9,1},{1... | collective-permute-start | bytes 786440 | tf_op jit(solution)/shard_map/ppermute | solution.py:441
  106.8 12.0 %collective-permute-start.24 = (bf16[64,16,128]{2,1,0:T(8,128)(2,1)S(1)}, bf16[64,16,128]{2,1,0:T(8,128)(2,1)}, u32[]{:S(2)}, u32[]{:S(2)}) collective-permute-start(bf16[64,16,128]{2,1,0:T(8,128)(2,1)S(1)} %collective-permute-done.23.refs_11_.refs_8_), channel_id=1, source_target_pairs={{0,8},{8,16},{16,24},{24,28},{28,20},{20,12},{12,4},{4,0},{1,9},{9... | collective-permute-start | bytes 786440 | tf_op jit(solution)/shard_map/ppermute | solution.py:441
  110.0 11.4 %collective-permute-start.31 = (bf16[64,16,128]{2,1,0:T(8,128)(2,1)S(1)}, bf16[64,16,128]{2,1,0:T(8,128)(2,1)}, u32[]{:S(2)}, u32[]{:S(2)}) collective-permute-start(bf16[64,16,128]{2,1,0:T(8,128)(2,1)S(1)} %collective-permute-done.30.refs_19_.refs_16_), channel_id=1, source_target_pairs={{8,0},{16,8},{24,16},{28,24},{20,28},{12,20},{4,12},{0,4},{9,1},{1... | collective-permute-start | bytes 786440 | tf_op jit(solution)/shard_map/ppermute | solution.py:441
  113.2 11.2 %collective-permute-start.14 = (bf16[64,16,128]{2,1,0:T(8,128)(2,1)S(1)}, bf16[64,16,128]{2,1,0:T(8,128)(2,1)S(1)}, u32[]{:S(2)}, u32[]{:S(2)}) collective-permute-start(bf16[64,16,128]{2,1,0:T(8,128)(2,1)S(1)} %collective-permute-done.13.refs_12_.refs_9_), channel_id=1, source_target_pairs={{0,8},{8,16},{16,24},{24,28},{28,20},{20,12},{12,4},{4,0},{1,9},{9... | collective-permute-start | bytes 786440 | tf_op jit(solution)/shard_map/ppermute | solution.py:441
  115.7 11.2 %collective-permute-start.18 = (bf16[64,16,128]{2,1,0:T(8,128)(2,1)S(1)}, bf16[64,16,128]{2,1,0:T(8,128)(2,1)S(1)}, u32[]{:S(2)}, u32[]{:S(2)}) collective-permute-start(bf16[64,16,128]{2,1,0:T(8,128)(2,1)S(1)} %collective-permute-done.17.refs_20_.refs_17_), channel_id=1, source_target_pairs={{8,0},{16,8},{24,16},{28,24},{20,28},{12,20},{4,12},{0,4},{9,1},{1... | collective-permute-start | bytes 786440 | tf_op jit(solution)/shard_map/ppermute | solution.py:441
  118.8 11.3 %collective-permute-start.25 = (bf16[64,16,128]{2,1,0:T(8,128)(2,1)}, bf16[64,16,128]{2,1,0:T(8,128)(2,1)}, u32[]{:S(2)}, u32[]{:S(2)}) collective-permute-start(bf16[64,16,128]{2,1,0:T(8,128)(2,1)} %collective-permute-done.24.refs_12_.refs_9_), channel_id=1, source_target_pairs={{0,8},{8,16},{16,24},{24,28},{28,20},{20,12},{12,4},{4,0},{1,9},{9... | collective-permute-start | bytes 786440 | tf_op jit(solution)/shard_map/ppermute | solution.py:441
  121.4 11.2 %collective-permute-start.32 = (bf16[64,16,128]{2,1,0:T(8,128)(2,1)}, bf16[64,16,128]{2,1,0:T(8,128)(2,1)}, u32[]{:S(2)}, u32[]{:S(2)}) collective-permute-start(bf16[64,16,128]{2,1,0:T(8,128)(2,1)} %collective-permute-done.31.refs_20_.refs_17_), channel_id=1, source_target_pairs={{8,0},{16,8},{24,16},{28,24},{20,28},{12,20},{4,12},{0,4},{9,1},{1... | collective-permute-start | bytes 786440 | tf_op jit(solution)/shard_map/ppermute | solution.py:441
  124.4 11.2 %collective-permute-start.15 = (bf16[64,16,128]{2,1,0:T(8,128)(2,1)S(1)}, bf16[64,16,128]{2,1,0:T(8,128)(2,1)S(1)}, u32[]{:S(2)}, u32[]{:S(2)}) collective-permute-start(bf16[64,16,128]{2,1,0:T(8,128)(2,1)S(1)} %collective-permute-done.14.refs_13_.refs_10_), channel_id=1, source_target_pairs={{0,8},{8,16},{16,24},{24,28},{28,20},{20,12},{12,4},{4,0},{1,9},{9... | collective-permute-start | bytes 786440 | tf_op jit(solution)/shard_map/ppermute | solution.py:441
  126.9 11.2 %collective-permute-start.19 = (bf16[64,16,128]{2,1,0:T(8,128)(2,1)S(1)}, bf16[64,16,128]{2,1,0:T(8,128)(2,1)S(1)}, u32[]{:S(2)}, u32[]{:S(2)}) collective-permute-start(bf16[64,16,128]{2,1,0:T(8,128)(2,1)S(1)} %collective-permute-done.18.refs_21_.refs_18_), channel_id=1, source_target_pairs={{8,0},{16,8},{24,16},{28,24},{20,28},{12,20},{4,12},{0,4},{9,1},{1... | collective-permute-start | bytes 786440 | tf_op jit(solution)/shard_map/ppermute | solution.py:441
  130.2 11.2 %collective-permute-start.26 = (bf16[64,16,128]{2,1,0:T(8,128)(2,1)}, bf16[64,16,128]{2,1,0:T(8,128)(2,1)}, u32[]{:S(2)}, u32[]{:S(2)}) collective-permute-start(bf16[64,16,128]{2,1,0:T(8,128)(2,1)} %collective-permute-done.25.refs_13_.refs_10_), channel_id=1, source_target_pairs={{0,8},{8,16},{16,24},{24,28},{28,20},{20,12},{12,4},{4,0},{1,9},{9... | collective-permute-start | bytes 786440 | tf_op jit(solution)/shard_map/ppermute | solution.py:441
  132.7 11.2 %collective-permute-start.33 = (bf16[64,16,128]{2,1,0:T(8,128)(2,1)}, bf16[64,16,128]{2,1,0:T(8,128)(2,1)}, u32[]{:S(2)}, u32[]{:S(2)}) collective-permute-start(bf16[64,16,128]{2,1,0:T(8,128)(2,1)} %collective-permute-done.32.refs_21_.refs_18_), channel_id=1, source_target_pairs={{8,0},{16,8},{24,16},{28,24},{20,28},{12,20},{4,12},{0,4},{9,1},{1... | collective-permute-start | bytes 786440 | tf_op jit(solution)/shard_map/ppermute | solution.py:441
  138.2 11.1 %collective-permute-start.20 = (bf16[64,16,128]{2,1,0:T(8,128)(2,1)S(1)}, bf16[64,16,128]{2,1,0:T(8,128)(2,1)}, u32[]{:S(2)}, u32[]{:S(2)}) collective-permute-start(bf16[64,16,128]{2,1,0:T(8,128)(2,1)S(1)} %collective-permute-done.19.refs_22_.refs_19_), channel_id=1, source_target_pairs={{8,0},{16,8},{24,16},{28,24},{20,28},{12,20},{4,12},{0,4},{9,1},{1... | collective-permute-start | bytes 786440 | tf_op jit(solution)/shard_map/ppermute | solution.py:441
  141.4 23.2 %collective-permute-start.27 = (bf16[64,16,128]{2,1,0:T(8,128)(2,1)}, bf16[64,16,128]{2,1,0:T(8,128)(2,1)}, u32[]{:S(2)}, u32[]{:S(2)}) collective-permute-start(bf16[64,16,128]{2,1,0:T(8,128)(2,1)} %collective-permute-done.26.refs_14_.refs_11_), channel_id=1, source_target_pairs={{0,8},{8,16},{16,24},{24,28},{28,20},{20,12},{12,4},{4,0},{1,9},{9... | collective-permute-start | bytes 786440 | tf_op jit(solution)/shard_map/ppermute | solution.py:441
  143.9 20.8 %collective-permute-start.34 = (bf16[64,16,128]{2,1,0:T(8,128)(2,1)}, bf16[64,16,128]{2,1,0:T(8,128)(2,1)}, u32[]{:S(2)}, u32[]{:S(2)}) collective-permute-start(bf16[64,16,128]{2,1,0:T(8,128)(2,1)} %collective-permute-done.33.refs_22_.refs_19_), channel_id=1, source_target_pairs={{8,0},{16,8},{24,16},{28,24},{20,28},{12,20},{4,12},{0,4},{9,1},{1... | collective-permute-start | bytes 786440 | tf_op jit(solution)/shard_map/ppermute | solution.py:441
  162.6 14.7 %collective-permute-start.49 = (bf16[16,64,128]{2,1,0:T(8,128)(2,1)S(1)}, bf16[16,64,128]{2,1,0:T(8,128)(2,1)S(1)}, u32[]{:S(2)}, u32[]{:S(2)}) collective-permute-start(bf16[16,64,128]{2,1,0:T(8,128)(2,1)S(1)} %get-tuple-element.66), channel_id=1, source_target_pairs={{0,8},{8,16},{16,24},{24,28},{28,20},{20,12},{12,4},{4,0},{1,9},{9... | collective-permute-start | bytes 786440 | tf_op jit(solution)/shard_map/ppermute | solution.py:313
  164.4 12.9 %collective-permute-start.56 = (bf16[16,64,128]{2,1,0:T(8,128)(2,1)S(1)}, bf16[16,64,128]{2,1,0:T(8,128)(2,1)S(1)}, u32[]{:S(2)}, u32[]{:S(2)}) collective-permute-start(bf16[16,64,128]{2,1,0:T(8,128)(2,1)S(1)} %get-tuple-element.67), channel_id=1, source_target_pairs={{8,0},{16,8},{24,16},{28,24},{20,28},{12,20},{4,12},{0,4},{9,1},{1... | collective-permute-start | bytes 786440 | tf_op jit(solution)/shard_map/ppermute | solution.py:314
  178.5 15.5 %collective-permute-start.50 = (bf16[16,64,128]{2,1,0:T(8,128)(2,1)S(1)}, bf16[16,64,128]{2,1,0:T(8,128)(2,1)S(1)}, u32[]{:S(2)}, u32[]{:S(2)}) collective-permute-start(bf16[16,64,128]{2,1,0:T(8,128)(2,1)S(1)} %get-tuple-element.64), channel_id=1, source_target_pairs={{0,8},{8,16},{16,24},{24,28},{28,20},{20,12},{12,4},{4,0},{1,9},{9... | collective-permute-start | bytes 786440 | tf_op jit(solution)/shard_map/ppermute | solution.py:313
  180.3 13.7 %collective-permute-start.57 = (bf16[16,64,128]{2,1,0:T(8,128)(2,1)S(1)}, bf16[16,64,128]{2,1,0:T(8,128)(2,1)S(1)}, u32[]{:S(2)}, u32[]{:S(2)}) collective-permute-start(bf16[16,64,128]{2,1,0:T(8,128)(2,1)S(1)} %get-tuple-element.65), channel_id=1, source_target_pairs={{8,0},{16,8},{24,16},{28,24},{20,28},{12,20},{4,12},{0,4},{9,1},{1... | collective-permute-start | bytes 786440 | tf_op jit(solution)/shard_map/ppermute | solution.py:314
  185.6 11.8 %collective-permute-start.38 = (bf16[16,64,128]{2,1,0:T(8,128)(2,1)S(1)}, bf16[16,64,128]{2,1,0:T(8,128)(2,1)S(1)}, u32[]{:S(2)}, u32[]{:S(2)}) collective-permute-start(bf16[16,64,128]{2,1,0:T(8,128)(2,1)S(1)} %get-tuple-element.80), channel_id=1, source_target_pairs={{8,0},{16,8},{24,16},{28,24},{20,28},{12,20},{4,12},{0,4},{9,1},{1... | collective-permute-start | bytes 786440 | tf_op jit(solution)/shard_map/ppermute | solution.py:314
  186.0 11.4 %collective-permute-start.37 = (bf16[16,64,128]{2,1,0:T(8,128)(2,1)S(1)}, bf16[16,64,128]{2,1,0:T(8,128)(2,1)S(1)}, u32[]{:S(2)}, u32[]{:S(2)}) collective-permute-start(bf16[16,64,128]{2,1,0:T(8,128)(2,1)S(1)} %get-tuple-element.81), channel_id=1, source_target_pairs={{0,8},{8,16},{16,24},{24,28},{28,20},{20,12},{12,4},{4,0},{1,9},{9... | collective-permute-start | bytes 786440 | tf_op jit(solution)/shard_map/ppermute | solution.py:313
  193.9 63.0 %reduce-scatter.5.cloned.1.call-start = ((), (), s32[]{:S(2)}) async-start(), calls=%async_computation.5 | async-start | bytes 1310720 | tf_op jit(solution)/shard_map/reduce_scatter | solution.py:473
  198.6 12.7 %collective-permute-start.44 = (bf16[16,64,128]{2,1,0:T(8,128)(2,1)S(1)}, bf16[16,64,128]{2,1,0:T(8,128)(2,1)S(1)}, u32[]{:S(2)}, u32[]{:S(2)}) collective-permute-start(bf16[16,64,128]{2,1,0:T(8,128)(2,1)S(1)} %get-tuple-element.78), channel_id=1, source_target_pairs={{8,0},{16,8},{24,16},{28,24},{20,28},{12,20},{4,12},{0,4},{9,1},{1... | collective-permute-start | bytes 786440 | tf_op jit(solution)/shard_map/ppermute | solution.py:314
  199.1 12.1 %collective-permute-start.39 = (bf16[16,64,128]{2,1,0:T(8,128)(2,1)S(1)}, bf16[16,64,128]{2,1,0:T(8,128)(2,1)S(1)}, u32[]{:S(2)}, u32[]{:S(2)}) collective-permute-start(bf16[16,64,128]{2,1,0:T(8,128)(2,1)S(1)} %get-tuple-element.79), channel_id=1, source_target_pairs={{0,8},{8,16},{16,24},{24,28},{28,20},{20,12},{12,4},{4,0},{1,9},{9... | collective-permute-start | bytes 786440 | tf_op jit(solution)/shard_map/ppermute | solution.py:313
  212.5 14.9 %collective-permute-start.40 = (bf16[16,64,128]{2,1,0:T(8,128)(2,1)S(1)}, bf16[16,64,128]{2,1,0:T(8,128)(2,1)S(1)}, u32[]{:S(2)}, u32[]{:S(2)}) collective-permute-start(bf16[16,64,128]{2,1,0:T(8,128)(2,1)S(1)} %get-tuple-element.76), channel_id=1, source_target_pairs={{0,8},{8,16},{16,24},{24,28},{28,20},{20,12},{12,4},{4,0},{1,9},{9... | collective-permute-start | bytes 786440 | tf_op jit(solution)/shard_map/ppermute | solution.py:313
  214.2 13.2 %collective-permute-start.45 = (bf16[16,64,128]{2,1,0:T(8,128)(2,1)S(1)}, bf16[16,64,128]{2,1,0:T(8,128)(2,1)S(1)}, u32[]{:S(2)}, u32[]{:S(2)}) collective-permute-start(bf16[16,64,128]{2,1,0:T(8,128)(2,1)S(1)} %get-tuple-element.77), channel_id=1, source_target_pairs={{8,0},{16,8},{24,16},{28,24},{20,28},{12,20},{4,12},{0,4},{9,1},{1... | collective-permute-start | bytes 786440 | tf_op jit(solution)/shard_map/ppermute | solution.py:314
  217.5 13.2 %collective-permute-start.53 = (bf16[16,64,128]{2,1,0:T(8,128)(2,1)S(1)}, bf16[16,64,128]{2,1,0:T(8,128)(2,1)S(1)}, u32[]{:S(2)}, u32[]{:S(2)}) collective-permute-start(bf16[16,64,128]{2,1,0:T(8,128)(2,1)S(1)} %get-tuple-element.58), channel_id=1, source_target_pairs={{0,8},{8,16},{16,24},{24,28},{28,20},{20,12},{12,4},{4,0},{1,9},{9... | collective-permute-start | bytes 786440 | tf_op jit(solution)/shard_map/ppermute | solution.py:313
  217.9 12.8 %collective-permute-start.60 = (bf16[16,64,128]{2,1,0:T(8,128)(2,1)S(1)}, bf16[16,64,128]{2,1,0:T(8,128)(2,1)S(1)}, u32[]{:S(2)}, u32[]{:S(2)}) collective-permute-start(bf16[16,64,128]{2,1,0:T(8,128)(2,1)S(1)} %get-tuple-element.59), channel_id=1, source_target_pairs={{8,0},{16,8},{24,16},{28,24},{20,28},{12,20},{4,12},{0,4},{9,1},{1... | collective-permute-start | bytes 786440 | tf_op jit(solution)/shard_map/ppermute | solution.py:314
  231.9 11.2 %collective-permute-start.54 = (bf16[16,64,128]{2,1,0:T(8,128)(2,1)S(1)}, bf16[16,64,128]{2,1,0:T(8,128)(2,1)S(1)}, u32[]{:S(2)}, u32[]{:S(2)}) collective-permute-start(bf16[16,64,128]{2,1,0:T(8,128)(2,1)S(1)} %get-tuple-element.56), channel_id=1, source_target_pairs={{0,8},{8,16},{16,24},{24,28},{28,20},{20,12},{12,4},{4,0},{1,9},{9... | collective-permute-start | bytes 786440 | tf_op jit(solution)/shard_map/ppermute | solution.py:313
  232.3 11.1 %collective-permute-start.61 = (bf16[16,64,128]{2,1,0:T(8,128)(2,1)S(1)}, bf16[16,64,128]{2,1,0:T(8,128)(2,1)S(1)}, u32[]{:S(2)}, u32[]{:S(2)}) collective-permute-start(bf16[16,64,128]{2,1,0:T(8,128)(2,1)S(1)} %get-tuple-element.57), channel_id=1, source_target_pairs={{8,0},{16,8},{24,16},{28,24},{20,28},{12,20},{4,12},{0,4},{9,1},{1... | collective-permute-start | bytes 786440 | tf_op jit(solution)/shard_map/ppermute | solution.py:314
  (44 other events, 849.9 us)
Sparse Core Ops, SparseCore 0:
  25.8 14.9 all-gather.2
  82.0 16.9 all-gather.4
  194.1 24.4 reduce-scatter.2
  227.5 22.4 reduce-scatter.4

commit v4 on v3

--- a/solution.py
+++ b/solution.py
@@ -291,6 +291,34 @@
     return lax.optimization_barrier((value, others))[0]
 
 
+def tensor_masks():
+    masks = []
+    mask = 1
+    while mask < lax.axis_size("tensor"):
+        masks.append(mask)
+        mask *= 2
+    return masks
+
+
+def swap(value, mask):
+    devices = lax.axis_size("tensor")
+    return lax.ppermute(value, "tensor", [(i, i ^ mask) for i in range(devices)])
+
+
+def gather_rows(value):
+    for mask in reversed(tensor_masks()):
+        value = jnp.concatenate([value, swap(value, mask)], axis=1)
+    return value
+
+
+def spread_sum(value):
+    for mask in tensor_masks():
+        half = value.shape[1] // 2
+        other = swap(value[:, half:], mask)
+        value = (value[:, :half].astype(jnp.float32) + other.astype(jnp.float32)).astype(jnp.bfloat16)
+    return value
+
+
 class RingSum:
     def __init__(self, parts, ahead, behind):
         self.parts, self.ahead, self.behind = parts, ahead, behind
@@ -304,21 +332,24 @@
     def high(self, q):
         return self.parts[q, :, BLK // 2 :]
 
-    def step(self, *after):
+    def step(self):
+        self.send()
+        self.add()
+
+    def send(self):
+        a, b = (x.astype(jnp.bfloat16) for x in self.run)
+        self.run = lax.ppermute(a, "dp", self.ahead), lax.ppermute(b, "dp", self.behind)
+
+    def add(self, *after):
         self.done += 1
         last = self.done == self.devices - 1
-        a, b = (x.astype(jnp.bfloat16) for x in self.run)
-        if after:
-            a, b = tie((a, b), *after)
-        a = lax.ppermute(a, "dp", self.ahead)
-        b = lax.ppermute(b, "dp", self.behind)
+        a, b = tie(self.run, *after) if after else self.run
         a = a.astype(jnp.float32) + self.low(self.done).astype(jnp.float32)
         q = self.done if last else self.devices - 2 - self.done
         b = b.astype(jnp.float32) + self.high(q).astype(jnp.float32)
         if not last:
             a, b = a.astype(jnp.bfloat16), b.astype(jnp.bfloat16)
         self.run = (a, b)
-        return self.run
 
     def steps_left(self):
         return self.devices - 1 - self.done
@@ -425,17 +456,15 @@
         note = jnp.concatenate([row_codes, col_codes]).reshape(4, slots).astype(jnp.bfloat16)
         note = jnp.pad(note, ((0, piece - 4), (0, BLK - slots)))
         messages = split_blocks(here, up_slots, down_slots, note, devices)
-        parts = [messages[0]] + [
-            lax.ppermute(messages[s], "dp", [(i, i ^ s) for i in range(devices)]) for s in range(1, devices)
-        ]
+        parts = [messages[0]] * devices
+        for step in range(1, devices):
+            parts[step] = lax.ppermute(messages[step], "dp", [(i, i ^ step) for i in range(devices)])
         notes = jnp.stack([part[2 * slots, :4, :slots] for part in parts], axis=1).astype(jnp.int32)
         pick, rows, cols = tables(notes[:2], notes[2:], index ^ me)
         place_of = (pick // slots) * (2 * slots) + pick % slots
         pick = place_of + jnp.array([[0], [slots]], jnp.int32)
 
-        tokens, cotangent = tie((tokens, cotangent), parts[1])
-        tok = lax.all_gather(tokens, "tensor", axis=0, tiled=True)
-        cot = lax.all_gather(cotangent, "tensor", axis=0, tiled=True)
+        tok, cot = gather_rows(tie(jnp.stack([tokens, cotangent]), parts[1]))
 
         def onward(pair):
             return lax.ppermute(pair[0], "dp", ahead), lax.ppermute(pair[1], "dp", behind)
@@ -454,23 +483,22 @@
             return lax.all_gather(x, "dp", axis=axis, tiled=True)
 
         pick, rows, cols = tables(everywhere(row_codes, 1), everywhere(col_codes, 1), index)
-        tok = lax.all_gather(tokens, "tensor", axis=0, tiled=True)
-        cot = lax.all_gather(cotangent, "tensor", axis=0, tiled=True)
+        tok, cot = gather_rows(jnp.stack([tokens, cotangent]))
         tok_turned = tok.T
         up = Whole(jnp.take(everywhere(up_slots, 0), pick[0], axis=0))
         down = Whole(jnp.take(everywhere(down_slots, 0), pick[1], axis=0))
 
     hid, slope, terms = hidden_of(rows, cols, tok, cot, up)
     down_sum = RingSum(terms, ahead, behind)
-    down_sum.step()
+    down_sum.send()
     grad_pre, terms = grad_pre_of(rows, cols, cot, down, slope, tok_turned)
+    down_sum.add(grad_pre)
     up_sum = RingSum(terms, ahead, behind)
     up_sum.step()
     out_part = width(0, rows[1], cols[1], tie(hid, up_sum.run), down)
     up_sum.step()
     in_part = width(1, rows[0], cols[0], tie(grad_pre, out_part, up_sum.run), up)
-    outputs = lax.psum_scatter(out_part, "tensor", scatter_dimension=0, tiled=True)
-    input_grads = lax.psum_scatter(in_part, "tensor", scatter_dimension=0, tiled=True)
+    outputs, input_grads = spread_sum(jnp.stack([out_part, in_part]))
     while down_sum.steps_left():
         down_sum.step()
     while up_sum.steps_left():

time: 264 us -> 257 us (0.973)
  between operations: 14.3 us -> 1.18 us
  local copies, waits for them, and re-layouts: 9.96 us -> 18.8 us
  other arithmetic: 20 us -> 14.2 us
  waiting for transfers between devices: 90.9 us -> 93.8 us
    convert_element_type x12 -> x14, other arithmetic: 14.6 us -> 4.6 us  [the longest x12 4.21 us: add(): a, b = (a.astype(jnp.bfloat16), b.astype(jnp.bfloat16))]
    ppermute x35 -> x39, waiting for transfers between devices: 51.5 us -> 59.1 us  [the longest x7 28.7 us: shards(): lax.ppermute(messages[step], 'dp', [(i, i ^ step) for i in range(devices)])]
    concatenate x0 -> x2, other arithmetic: none -> 5.17 us  [gather_rows(): value = jnp.concatenate([value, swap(value, mask)], axis=1)]
    ppermute x0 -> x2, local copies, waits for them, and re-layouts: none -> 4.52 us  [swap(): lax.ppermute(value, 'tensor', [(i, i ^ mask) for i in range(devices)])]
    ppermute x14, waiting for transfers between devices: 8.51 us -> 4.02 us  [onward(): lax.ppermute(pair[1], 'dp', behind)]
    ppermute x14, starting transfers between devices: 43.3 us -> 39.6 us  [onward(): lax.ppermute(pair[0], 'dp', ahead)]
    another operation x0 -> x3, local copies, waits for them, and re-layouts: none -> 3.48 us  [the longest x2 2.66 us: shards(): tok, cot = gather_rows(tie(jnp.stack([tokens, cotangent]), parts[1]))]
    ppermute x35 -> x39, starting transfers between devices: 42.8 us -> 46.1 us  [the longest x14 16.5 us: send(): lax.ppermute(b, 'dp', self.behind)]
  transfers between devices with their start and end apart: 67 -> 67, of which waited for: 38 -> 35; matrix products, arithmetic and copies ran while one was open for 11% -> 11% of each run, Pallas kernels for 15% -> 15%
where the time goes in v4:
time: 257 us; the launch traced here: 256 us
  waiting for transfers between devices  93.8 us (36%)
  starting transfers between devices  85.7 us (33%)
  Pallas kernels  42.6 us (17%)
  local copies, waits for them, and re-layouts  18.8 us (7%)
  other arithmetic  14.2 us (6%)
    pallas_call x6, Pallas kernels, run(): pl.pallas_call(body, out_shape=list(outs), in_specs=[SMEM_SPEC] * (len(sm...  42.6 us
    ppermute x14, starting transfers between devices, onward(): lax.ppermute(pair[0], 'dp', ahead)  39.6 us
    ppermute x14, waiting for transfers between devices, onward(): lax.ppermute(pair[0], 'dp', ahead)  30.7 us
    ppermute x7, waiting for transfers between devices, shards(): lax.ppermute(messages[step], 'dp', [(i, i ^ step) for i in range(devices)])  28.7 us
    ppermute x14, waiting for transfers between devices, send(): lax.ppermute(a, 'dp', self.ahead)  25.5 us
    ppermute x14, starting transfers between devices, send(): lax.ppermute(b, 'dp', self.behind)  16.5 us
    ppermute x7, starting transfers between devices, shards(): lax.ppermute(messages[step], 'dp', [(i, i ^ step) for i in range(devices)])  13.7 us
    ppermute x14, starting transfers between devices, send(): lax.ppermute(a, 'dp', self.ahead)  12.6 us
  transfers between devices with their start and end apart: 67, of which 35 were waited for; matrix products, arithmetic and copies ran while one was open for 11% of the time, Pallas kernels for 15%

profile of v4, /device:TPU:0, one launch (start us, length us, event | category | flops | bytes accessed | tf_op | source)
XLA Modules:
  0.0 256.4 jit_solution(8109458820072757559)
XLA Ops:
  2.7 3.0 %shard_map.111 = (bf16[65,16,128]{2,1,0:T(8,128)(2,1)}, bf16[65,16,128]{2,1,0:T(8,128)(2,1)}, bf16[65,16,128]{2,1,0:T(8,128)(2,1)}, bf16[65,16,128]{2,1,0:T(8,12...) custom-call(s32[1]{0:T(128)} %bitcast.refs_0_, ...), custom_call_target="tpu_custom_call" | custom-call | bytes 4194304 | tf_op jit(solution)/shard_map/pallas_call | solution.py:145
  5.7 3.0 %collective-permute-start = (bf16[65,16,128]{2,1,0:T(8,128)(2,1)}, bf16[65,16,128]{2,1,0:T(8,128)(2,1)S(1)}, u32[]{:S(2)}, u32[]{:S(2)}) collective-permute-start(bf16[65,16,128]{2,1,0:T(8,128)(2,1)} %get-tuple-element.29), channel_id=1, source_target_pairs={{0,4},{4,0},{8,12},{12,8},{16,20},{20,16},{24,28},{28,24},{1,5},{5... | collective-permute-start | bytes 798728 | tf_op jit(solution)/shard_map/ppermute | solution.py:461
  10.3 3.0 %collective-permute-start.3 = (bf16[65,16,128]{2,1,0:T(8,128)(2,1)}, bf16[65,16,128]{2,1,0:T(8,128)(2,1)S(1)}, u32[]{:S(2)}, u32[]{:S(2)}) collective-permute-start(bf16[65,16,128]{2,1,0:T(8,128)(2,1)} %get-tuple-element.32), channel_id=1, source_target_pairs={{0,16},{4,20},{8,24},{12,28},{16,0},{20,4},{24,8},{28,12},{1,17},{... | collective-permute-start | bytes 798728 | tf_op jit(solution)/shard_map/ppermute | solution.py:461
  15.4 3.8 %collective-permute-start.5 = (bf16[65,16,128]{2,1,0:T(8,128)(2,1)}, bf16[65,16,128]{2,1,0:T(8,128)(2,1)S(1)}, u32[]{:S(2)}, u32[]{:S(2)}) collective-permute-start(bf16[65,16,128]{2,1,0:T(8,128)(2,1)} %get-tuple-element.34), channel_id=1, source_target_pairs={{0,24},{4,28},{8,16},{12,20},{16,8},{20,12},{24,0},{28,4},{1,25},{... | collective-permute-start | bytes 798728 | tf_op jit(solution)/shard_map/ppermute | solution.py:461
  19.1 9.5 %collective-permute-done.1.refs_4_ = bf16[65,16,128]{2,1,0:T(8,128)(2,1)S(1)} collective-permute-done((bf16[65,16,128]{2,1,0:T(8,128)(2,1)}, bf16[65,16,128]{2,1,0:T(8,128)(2,1)S(1)}, u32[]{:S(2)}, u32[]{:S(2)}) %collective-permute-start.1) | collective-permute-done | bytes 266272 | tf_op jit(solution)/shard_map/ppermute | solution.py:461
  29.7 2.3 collective-permute-done.2.refs_5_
  33.8 16.8 %collective-permute-done.4.refs_7_ = bf16[65,16,128]{2,1,0:T(8,128)(2,1)S(1)} collective-permute-done((bf16[65,16,128]{2,1,0:T(8,128)(2,1)}, bf16[65,16,128]{2,1,0:T(8,128)(2,1)S(1)}, u32[]{:S(2)}, u32[]{:S(2)}) %collective-permute-start.4) | collective-permute-done | bytes 266272 | tf_op jit(solution)/shard_map/ppermute | solution.py:461
  53.0 3.4 %shard_map.112 = (bf16[64,16,128]{2,1,0:T(8,128)(2,1)}, bf16[64,16,128]{2,1,0:T(8,128)(2,1)}, bf16[64,16,128]{2,1,0:T(8,128)(2,1)}, bf16[64,16,128]{2,1,0:T(8,128)(2,1)}) custom-call(s32[128]{0:T(128)} %get-tuple-element.98.refs_0_, s32[128]{0:T(128)} %get-tuple-element.97.refs_1_, bf16[65,16,128]{2,1,0:T(8,128)(2,1)} %get-tuple-element.28.refs_2_, ...), custom_call_target="tpu_custom_call" | custom-call | bytes 3145728 | tf_op jit(solution)/shard_map/pallas_call | solution.py:145
  56.4 10.0 %collective-permute-start.9 = (bf16[64,16,128]{2,1,0:T(8,128)(2,1)}, bf16[64,16,128]{2,1,0:T(8,128)(2,1)S(1)}, u32[]{:S(2)}, u32[]{:S(2)}) collective-permute-start(bf16[64,16,128]{2,1,0:T(8,128)(2,1)} %get-tuple-element.37.refs_8_.refs_5_), channel_id=1, source_target_pairs={{0,8},{8,16},{16,24},{24,28},{28,20},{20,12},{12,4},{4,0},{1,9},{9... | collective-permute-start | bytes 786440 | tf_op jit(solution)/shard_map/ppermute | solution.py:470
  66.4 2.7 %collective-permute-start.23 = (bf16[64,16,128]{2,1,0:T(8,128)(2,1)}, bf16[64,16,128]{2,1,0:T(8,128)(2,1)}, u32[]{:S(2)}, u32[]{:S(2)}) collective-permute-start(bf16[64,16,128]{2,1,0:T(8,128)(2,1)} %get-tuple-element.42.refs_8_.refs_5_), channel_id=1, source_target_pairs={{0,8},{8,16},{16,24},{24,28},{28,20},{20,12},{12,4},{4,0},{1,9},{9... | collective-permute-start | bytes 786440 | tf_op jit(solution)/shard_map/ppermute | solution.py:470
  69.1 4.2 %collective-permute-done.9.refs_9_.refs_6_ = bf16[64,16,128]{2,1,0:T(8,128)(2,1)S(1)} collective-permute-done((bf16[64,16,128]{2,1,0:T(8,128)(2,1)}, bf16[64,16,128]{2,1,0:T(8,128)(2,1)S(1)}, u32[]{:S(2)}, u32[]{:S(2)}) %collective-permute-start.9) | collective-permute-done | bytes 262176 | tf_op jit(solution)/shard_map/ppermute | solution.py:470
  73.3 2.7 %collective-permute-start.10 = (bf16[64,16,128]{2,1,0:T(8,128)(2,1)S(1)}, bf16[64,16,128]{2,1,0:T(8,128)(2,1)}, u32[]{:S(2)}, u32[]{:S(2)}) collective-permute-start(bf16[64,16,128]{2,1,0:T(8,128)(2,1)S(1)} %collective-permute-done.9.refs_9_.refs_6_), channel_id=1, source_target_pairs={{0,8},{8,16},{16,24},{24,28},{28,20},{20,12},{12,4},{4,0},{1,9},{9... | collective-permute-start | bytes 786440 | tf_op jit(solution)/shard_map/ppermute | solution.py:470
  76.5 2.5 collective-permute-done.23.refs_9_.refs_6_
  78.9 2.7 %collective-permute-start.24 = (bf16[64,16,128]{2,1,0:T(8,128)(2,1)}, bf16[64,16,128]{2,1,0:T(8,128)(2,1)}, u32[]{:S(2)}, u32[]{:S(2)}) collective-permute-start(bf16[64,16,128]{2,1,0:T(8,128)(2,1)} %collective-permute-done.23.refs_9_.refs_6_), channel_id=1, source_target_pairs={{0,8},{8,16},{16,24},{24,28},{28,20},{20,12},{12,4},{4,0},{1,9},{9... | collective-permute-start | bytes 786440 | tf_op jit(solution)/shard_map/ppermute | solution.py:470
  84.9 2.3 collective-permute-start.11
  87.7 2.5 collective-permute-done.24.refs_10_.refs_7_
  90.1 2.7 %collective-permute-start.25 = (bf16[64,16,128]{2,1,0:T(8,128)(2,1)}, bf16[64,16,128]{2,1,0:T(8,128)(2,1)}, u32[]{:S(2)}, u32[]{:S(2)}) collective-permute-start(bf16[64,16,128]{2,1,0:T(8,128)(2,1)} %collective-permute-done.24.refs_10_.refs_7_), channel_id=1, source_target_pairs={{0,8},{8,16},{16,24},{24,28},{28,20},{20,12},{12,4},{4,0},{1,9},{9... | collective-permute-start | bytes 786440 | tf_op jit(solution)/shard_map/ppermute | solution.py:470
  93.3 2.8 %copy.40 = bf16[2,64,4096]{1,2,0:T(8,128)(2,1)} copy(bf16[2,64,4096]{2,1,0:T(8,128)(2,1)} %collective-permute-done.8) | data formatting | bytes 2097152 | tf_op jit(solution)/shard_map/ppermute | solution.py:305
  96.1 4.1 %pad_maximum_fusion = bf16[2,128,4096]{1,2,0:T(8,128)(2,1)S(1)} fusion(bf16[2,64,4096]{1,2,0:T(8,128)(2,1)} %copy.40, bf16[2,32,4096]{1,2,0:T(8,128)(2,1)} %copy.39, bf16[2,32,4096]{1,2,0:T(8,128)(2,1)S(1)} %copy.38), kind=kLoop, calls=%fused_computation | loop fusion | flops 6291456 | bytes 4194304 | tf_op jit(solution)/shard_map/concatenate | solution.py:310
  101.5 2.1 collective-permute-start.15
  105.7 5.1 %collective-permute-done.15.refs_12_.refs_9_ = bf16[64,16,128]{2,1,0:T(8,128)(2,1)S(1)} collective-permute-done((bf16[64,16,128]{2,1,0:T(8,128)(2,1)S(1)}, bf16[64,16,128]{2,1,0:T(8,128)(2,1)S(1)}, u32[]{:S(2)}, u32[]{:S(2)}) %collective-permute-start.15) | collective-permute-done | bytes 262176 | tf_op jit(solution)/shard_map/ppermute | solution.py:470
  110.8 2.1 collective-permute-start.16
  112.9 3.6 %collective-permute-done.26.refs_12_.refs_9_ = bf16[64,16,128]{2,1,0:T(8,128)(2,1)} collective-permute-done((bf16[64,16,128]{2,1,0:T(8,128)(2,1)}, bf16[64,16,128]{2,1,0:T(8,128)(2,1)}, u32[]{:S(2)}, u32[]{:S(2)}) %collective-permute-start.26) | collective-permute-done | bytes 262176 | tf_op jit(solution)/shard_map/ppermute | solution.py:470
  116.6 2.1 collective-permute-start.27
  118.6 3.5 %collective-permute-done.16.refs_13_.refs_10_ = bf16[64,16,128]{2,1,0:T(8,128)(2,1)} collective-permute-done((bf16[64,16,128]{2,1,0:T(8,128)(2,1)S(1)}, bf16[64,16,128]{2,1,0:T(8,128)(2,1)}, u32[]{:S(2)}, u32[]{:S(2)}) %collective-permute-start.16) | collective-permute-done | bytes 262176 | tf_op jit(solution)/shard_map/ppermute | solution.py:470
  122.2 2.1 collective-permute-start.17
  125.7 2.1 collective-permute-done.27.refs_13_.refs_10_
  127.8 2.1 collective-permute-start.28
  129.9 3.5 %collective-permute-done.17.refs_14_.refs_11_ = bf16[64,16,128]{2,1,0:T(8,128)(2,1)} collective-permute-done((bf16[64,16,128]{2,1,0:T(8,128)(2,1)}, bf16[64,16,128]{2,1,0:T(8,128)(2,1)}, u32[]{:S(2)}, u32[]{:S(2)}) %collective-permute-start.17) | collective-permute-done | bytes 262176 | tf_op jit(solution)/shard_map/ppermute | solution.py:470
  133.4 2.1 collective-permute-start.18
  139.0 2.1 collective-permute-start.29
  141.1 3.5 %collective-permute-done.18.refs_15_.refs_12_ = bf16[64,16,128]{2,1,0:T(8,128)(2,1)} collective-permute-done((bf16[64,16,128]{2,1,0:T(8,128)(2,1)}, bf16[64,16,128]{2,1,0:T(8,128)(2,1)}, u32[]{:S(2)}, u32[]{:S(2)}) %collective-permute-start.18) | collective-permute-done | bytes 262176 | tf_op jit(solution)/shard_map/ppermute | solution.py:470
  144.7 2.1 collective-permute-done.22.refs_23_.refs_20_
  146.7 12.1 %shard_map.113 = (bf16[32,128,128]{2,1,0:T(8,128)(2,1)}, f32[32,128,128]{2,1,0:T(8,128)}, bf16[8,16,128,128]{3,2,1,0:T(8,128)(2,1)}) custom-call(s32[8]{0:T(128)} %get-tuple-element.94.refs_0_, s32[128]{0:T(128)} %get-tuple-element.105.refs_1_.refs_3_.refs_0_, s32[128]{0:T(128)} %get-tuple-element.100.refs_2_.refs_4_.refs_1_, ...), custom_call_target="tpu_custom_call" | custom-call | flops 17179869184 | bytes 13631488 | tf_op jit(solution)/shard_map/pallas_call | solution.py:145
  159.9 2.1 collective-permute-start.53
  162.8 10.0 %shard_map.114 = (bf16[32,128,128]{2,1,0:T(8,128)(2,1)}, bf16[8,16,128,128]{3,2,1,0:T(8,128)(2,1)}) custom-call(s32[8]{0:T(128)} %get-tuple-element.94.refs_0_, s32[128]{0:T(128)} %get-tuple-element.106.refs_3_.refs_1_.refs_0_, s32[128]{0:T(128)} %get-tuple-element.99.refs_4_.refs_2_.refs_1_, s32[128]{0:T(128)} %get-tuple-element.105.refs_1_.refs_3_.refs_0_, ...), custom_call_target="tpu_custom_call" | custom-call | flops 17179869184 | bytes 13631488 | tf_op jit(solution)/shard_map/pallas_call | solution.py:145
  173.8 2.1 collective-permute-start.37
  176.1 2.1 collective-permute-start.55
  178.2 3.9 %collective-permute-done.37 = bf16[16,64,128]{2,1,0:T(8,128)(2,1)S(1)} collective-permute-done((bf16[16,64,128]{2,1,0:T(8,128)(2,1)S(1)}, bf16[16,64,128]{2,1,0:T(8,128)(2,1)S(1)}, u32[]{:S(2)}, u32[]{:S(2)}) %collective-permute-start.37) | collective-permute-done | bytes 262176 | tf_op jit(solution)/shard_map/ppermute | solution.py:341
  182.1 2.7 %collective-permute-done.38 = bf16[16,64,128]{2,1,0:T(8,128)(2,1)S(1)} collective-permute-done((bf16[16,64,128]{2,1,0:T(8,128)(2,1)S(1)}, bf16[16,64,128]{2,1,0:T(8,128)(2,1)S(1)}, u32[]{:S(2)}, u32[]{:S(2)}) %collective-permute-start.38) | collective-permute-done | bytes 262176 | tf_op jit(solution)/shard_map/ppermute | solution.py:341
  188.1 6.3 %shard_map.115 = bf16[128,4096]{1,0:T(8,128)(2,1)} custom-call(s32[128]{0:T(128)} %get-tuple-element.106.refs_3_.refs_1_.refs_0_, s32[128]{0:T(128)} %get-tuple-element.99.refs_4_.refs_2_.refs_1_, s32[8]{0:T(128)} %get-tuple-element.96.refs_5_.refs_2_, s32[8]{0:T(128)} %get-tuple-element.95.refs_6_.refs_3_, bf16[32,128,128]{2,1,0:T(8,128)(2,1)} %get-tuple-element.46.refs_4_, ...), custom_call_target="tpu_custom_call" | custom-call | flops 8589934592 | bytes 6291456 | tf_op jit(solution)/shard_map/pallas_call | solution.py:145
  200.0 7.9 %shard_map.116 = bf16[128,4096]{1,0:T(8,128)(2,1)} custom-call(s32[128]{0:T(128)} %get-tuple-element.105.refs_1_.refs_3_.refs_0_, s32[128]{0:T(128)} %get-tuple-element.100.refs_2_.refs_4_.refs_1_, s32[8]{0:T(128)} %get-tuple-element.96.refs_5_.refs_2_, s32[8]{0:T(128)} %get-tuple-element.95.refs_6_.refs_3_, ...), custom_call_target="tpu_custom_call" | custom-call | flops 8589934592 | bytes 6291456 | tf_op jit(solution)/shard_map/pallas_call | solution.py:145
  217.1 3.7 %collective-permute-done.44 = bf16[16,64,128]{2,1,0:T(8,128)(2,1)S(1)} collective-permute-done((bf16[16,64,128]{2,1,0:T(8,128)(2,1)S(1)}, bf16[16,64,128]{2,1,0:T(8,128)(2,1)S(1)}, u32[]{:S(2)}, u32[]{:S(2)}) %collective-permute-start.44) | collective-permute-done | bytes 262176 | tf_op jit(solution)/shard_map/ppermute | solution.py:341
  223.3 3.1 %collective-permute-done.58 = bf16[16,64,128]{2,1,0:T(8,128)(2,1)S(1)} collective-permute-done((bf16[16,64,128]{2,1,0:T(8,128)(2,1)S(1)}, bf16[16,64,128]{2,1,0:T(8,128)(2,1)S(1)}, u32[]{:S(2)}, u32[]{:S(2)}) %collective-permute-start.58) | collective-permute-done | bytes 262176 | tf_op jit(solution)/shard_map/ppermute | solution.py:341
  229.0 3.0 %collective-permute-done.45 = bf16[16,64,128]{2,1,0:T(8,128)(2,1)S(1)} collective-permute-done((bf16[16,64,128]{2,1,0:T(8,128)(2,1)S(1)}, bf16[16,64,128]{2,1,0:T(8,128)(2,1)S(1)}, u32[]{:S(2)}, u32[]{:S(2)}) %collective-permute-start.45) | collective-permute-done | bytes 262176 | tf_op jit(solution)/shard_map/ppermute | solution.py:341
  234.6 3.0 %collective-permute-done.59 = bf16[16,64,128]{2,1,0:T(8,128)(2,1)S(1)} collective-permute-done((bf16[16,64,128]{2,1,0:T(8,128)(2,1)S(1)}, bf16[16,64,128]{2,1,0:T(8,128)(2,1)S(1)}, u32[]{:S(2)}, u32[]{:S(2)}) %collective-permute-start.59) | collective-permute-done | bytes 262176 | tf_op jit(solution)/shard_map/ppermute | solution.py:341
  245.8 3.0 %collective-permute-done.60 = bf16[16,64,128]{2,1,0:T(8,128)(2,1)S(1)} collective-permute-done((bf16[16,64,128]{2,1,0:T(8,128)(2,1)S(1)}, bf16[16,64,128]{2,1,0:T(8,128)(2,1)S(1)}, u32[]{:S(2)}, u32[]{:S(2)}) %collective-permute-start.60) | collective-permute-done | bytes 262176 | tf_op jit(solution)/shard_map/ppermute | solution.py:341
  250.4 3.7 %collective-permute-done.47 = bf16[16,64,128]{2,1,0:T(8,128)(2,1)S(1)} collective-permute-done((bf16[16,64,128]{2,1,0:T(8,128)(2,1)S(1)}, bf16[16,64,128]{2,1,0:T(8,128)(2,1)S(1)}, u32[]{:S(2)}, u32[]{:S(2)}) %collective-permute-start.47) | collective-permute-done | bytes 262176 | tf_op jit(solution)/shard_map/ppermute | solution.py:341
  (197 shorter events, 64.6 us)
Async XLA Ops:
  8.7 20.0 %collective-permute-start.1 = (bf16[65,16,128]{2,1,0:T(8,128)(2,1)}, bf16[65,16,128]{2,1,0:T(8,128)(2,1)S(1)}, u32[]{:S(2)}, u32[]{:S(2)}) collective-permute-start(bf16[65,16,128]{2,1,0:T(8,128)(2,1)} %get-tuple-element.30), channel_id=1, source_target_pairs={{0,8},{4,12},{8,0},{12,4},{16,24},{20,28},{24,16},{28,20},{1,9},{5... | collective-permute-start | bytes 798728 | tf_op jit(solution)/shard_map/ppermute | solution.py:461
  10.3 21.8 %collective-permute-start.2 = (bf16[65,16,128]{2,1,0:T(8,128)(2,1)}, bf16[65,16,128]{2,1,0:T(8,128)(2,1)S(1)}, u32[]{:S(2)}, u32[]{:S(2)}) collective-permute-start(bf16[65,16,128]{2,1,0:T(8,128)(2,1)} %get-tuple-element.31), channel_id=1, source_target_pairs={{0,12},{4,8},{8,4},{12,0},{16,28},{20,24},{24,20},{28,16},{1,13},{... | collective-permute-start | bytes 798728 | tf_op jit(solution)/shard_map/ppermute | solution.py:461
  10.3 23.5 %collective-permute-start.3 = (bf16[65,16,128]{2,1,0:T(8,128)(2,1)}, bf16[65,16,128]{2,1,0:T(8,128)(2,1)S(1)}, u32[]{:S(2)}, u32[]{:S(2)}) collective-permute-start(bf16[65,16,128]{2,1,0:T(8,128)(2,1)} %get-tuple-element.32), channel_id=1, source_target_pairs={{0,16},{4,20},{8,24},{12,28},{16,0},{20,4},{24,8},{28,12},{1,17},{... | collective-permute-start | bytes 798728 | tf_op jit(solution)/shard_map/ppermute | solution.py:461
  13.3 37.3 %collective-permute-start.4 = (bf16[65,16,128]{2,1,0:T(8,128)(2,1)}, bf16[65,16,128]{2,1,0:T(8,128)(2,1)S(1)}, u32[]{:S(2)}, u32[]{:S(2)}) collective-permute-start(bf16[65,16,128]{2,1,0:T(8,128)(2,1)} %get-tuple-element.33), channel_id=1, source_target_pairs={{0,20},{4,16},{8,28},{12,24},{16,4},{20,0},{24,12},{28,8},{1,21},{... | collective-permute-start | bytes 798728 | tf_op jit(solution)/shard_map/ppermute | solution.py:461
  15.4 35.2 %collective-permute-start.5 = (bf16[65,16,128]{2,1,0:T(8,128)(2,1)}, bf16[65,16,128]{2,1,0:T(8,128)(2,1)S(1)}, u32[]{:S(2)}, u32[]{:S(2)}) collective-permute-start(bf16[65,16,128]{2,1,0:T(8,128)(2,1)} %get-tuple-element.34), channel_id=1, source_target_pairs={{0,24},{4,28},{8,16},{12,20},{16,8},{20,12},{24,0},{28,4},{1,25},{... | collective-permute-start | bytes 798728 | tf_op jit(solution)/shard_map/ppermute | solution.py:461
  28.7 21.9 %collective-permute-start.6 = (bf16[65,16,128]{2,1,0:T(8,128)(2,1)}, bf16[65,16,128]{2,1,0:T(8,128)(2,1)S(1)}, u32[]{:S(2)}, u32[]{:S(2)}) collective-permute-start(bf16[65,16,128]{2,1,0:T(8,128)(2,1)} %get-tuple-element.35), channel_id=1, source_target_pairs={{0,28},{4,24},{8,20},{12,16},{16,12},{20,8},{24,4},{28,0},{1,29},{... | collective-permute-start | bytes 798728 | tf_op jit(solution)/shard_map/ppermute | solution.py:461
  32.1 19.0 %collective-permute-start.7 = (bf16[2,32,4096]{2,1,0:T(8,128)(2,1)S(1)}, bf16[2,32,4096]{2,1,0:T(8,128)(2,1)S(1)}, u32[]{:S(2)}, u32[]{:S(2)}) collective-permute-start(bf16[2,32,4096]{2,1,0:T(8,128)(2,1)S(1)} %pad_maximum_fusion.3), channel_id=1, source_target_pairs={{0,2},{1,3},{2,0},{3,1},{4,6},{5,7},{6,4},{7,5},{8,10},{9,11},{10,... | collective-permute-start | bytes 1572872 | tf_op jit(solution)/shard_map/ppermute | solution.py:305
  52.2 41.2 %collective-permute-start.8 = (bf16[2,64,4096]{2,1,0:T(8,128)(2,1)}, bf16[2,64,4096]{2,1,0:T(8,128)(2,1)}, u32[]{:S(2)}, u32[]{:S(2)}) collective-permute-start(bf16[2,64,4096]{2,1,0:T(8,128)(2,1)} %pad_maximum_fusion.2), channel_id=1, source_target_pairs={{0,1},{1,0},{2,3},{3,2},{4,5},{5,4},{6,7},{7,6},{8,9},{9,8},{10,11... | collective-permute-start | bytes 3145736 | tf_op jit(solution)/shard_map/ppermute | solution.py:305
  56.4 16.9 %collective-permute-start.9 = (bf16[64,16,128]{2,1,0:T(8,128)(2,1)}, bf16[64,16,128]{2,1,0:T(8,128)(2,1)S(1)}, u32[]{:S(2)}, u32[]{:S(2)}) collective-permute-start(bf16[64,16,128]{2,1,0:T(8,128)(2,1)} %get-tuple-element.37.refs_8_.refs_5_), channel_id=1, source_target_pairs={{0,8},{8,16},{16,24},{24,28},{28,20},{20,12},{12,4},{4,0},{1,9},{9... | collective-permute-start | bytes 786440 | tf_op jit(solution)/shard_map/ppermute | solution.py:470
  66.4 12.6 %collective-permute-start.23 = (bf16[64,16,128]{2,1,0:T(8,128)(2,1)}, bf16[64,16,128]{2,1,0:T(8,128)(2,1)}, u32[]{:S(2)}, u32[]{:S(2)}) collective-permute-start(bf16[64,16,128]{2,1,0:T(8,128)(2,1)} %get-tuple-element.42.refs_8_.refs_5_), channel_id=1, source_target_pairs={{0,8},{8,16},{16,24},{24,28},{28,20},{20,12},{12,4},{4,0},{1,9},{9... | collective-permute-start | bytes 786440 | tf_op jit(solution)/shard_map/ppermute | solution.py:470
  69.1 13.0 %collective-permute-start.30 = (bf16[64,16,128]{2,1,0:T(8,128)(2,1)}, bf16[64,16,128]{2,1,0:T(8,128)(2,1)}, u32[]{:S(2)}, u32[]{:S(2)}) collective-permute-start(bf16[64,16,128]{2,1,0:T(8,128)(2,1)} %get-tuple-element.43.refs_16_.refs_13_), channel_id=1, source_target_pairs={{8,0},{16,8},{24,16},{28,24},{20,28},{12,20},{4,12},{0,4},{9,1},{1... | collective-permute-start | bytes 786440 | tf_op jit(solution)/shard_map/ppermute | solution.py:470
  73.3 11.6 %collective-permute-start.10 = (bf16[64,16,128]{2,1,0:T(8,128)(2,1)S(1)}, bf16[64,16,128]{2,1,0:T(8,128)(2,1)}, u32[]{:S(2)}, u32[]{:S(2)}) collective-permute-start(bf16[64,16,128]{2,1,0:T(8,128)(2,1)S(1)} %collective-permute-done.9.refs_9_.refs_6_), channel_id=1, source_target_pairs={{0,8},{8,16},{16,24},{24,28},{28,20},{20,12},{12,4},{4,0},{1,9},{9... | collective-permute-start | bytes 786440 | tf_op jit(solution)/shard_map/ppermute | solution.py:470
  76.5 11.2 %collective-permute-start.13 = (bf16[64,16,128]{2,1,0:T(8,128)(2,1)}, bf16[64,16,128]{2,1,0:T(8,128)(2,1)}, u32[]{:S(2)}, u32[]{:S(2)}) collective-permute-start(bf16[64,16,128]{2,1,0:T(8,128)(2,1)} %collective-permute-done.12.refs_17_.refs_14_), channel_id=1, source_target_pairs={{8,0},{16,8},{24,16},{28,24},{20,28},{12,20},{4,12},{0,4},{9,1},{1... | collective-permute-start | bytes 786440 | tf_op jit(solution)/shard_map/ppermute | solution.py:470
  78.9 11.2 %collective-permute-start.24 = (bf16[64,16,128]{2,1,0:T(8,128)(2,1)}, bf16[64,16,128]{2,1,0:T(8,128)(2,1)}, u32[]{:S(2)}, u32[]{:S(2)}) collective-permute-start(bf16[64,16,128]{2,1,0:T(8,128)(2,1)} %collective-permute-done.23.refs_9_.refs_6_), channel_id=1, source_target_pairs={{0,8},{8,16},{16,24},{24,28},{28,20},{20,12},{12,4},{4,0},{1,9},{9... | collective-permute-start | bytes 786440 | tf_op jit(solution)/shard_map/ppermute | solution.py:470
  82.1 11.2 %collective-permute-start.31 = (bf16[64,16,128]{2,1,0:T(8,128)(2,1)}, bf16[64,16,128]{2,1,0:T(8,128)(2,1)}, u32[]{:S(2)}, u32[]{:S(2)}) collective-permute-start(bf16[64,16,128]{2,1,0:T(8,128)(2,1)} %collective-permute-done.30.refs_17_.refs_14_), channel_id=1, source_target_pairs={{8,0},{16,8},{24,16},{28,24},{20,28},{12,20},{4,12},{0,4},{9,1},{1... | collective-permute-start | bytes 786440 | tf_op jit(solution)/shard_map/ppermute | solution.py:470
  84.9 16.7 %collective-permute-start.11 = (bf16[64,16,128]{2,1,0:T(8,128)(2,1)}, bf16[64,16,128]{2,1,0:T(8,128)(2,1)S(1)}, u32[]{:S(2)}, u32[]{:S(2)}) collective-permute-start(bf16[64,16,128]{2,1,0:T(8,128)(2,1)} %collective-permute-done.10.refs_10_.refs_7_), channel_id=1, source_target_pairs={{0,8},{8,16},{16,24},{24,28},{28,20},{20,12},{12,4},{4,0},{1,9},{9... | collective-permute-start | bytes 786440 | tf_op jit(solution)/shard_map/ppermute | solution.py:470
  87.7 13.8 %collective-permute-start.14 = (bf16[64,16,128]{2,1,0:T(8,128)(2,1)}, bf16[64,16,128]{2,1,0:T(8,128)(2,1)S(1)}, u32[]{:S(2)}, u32[]{:S(2)}) collective-permute-start(bf16[64,16,128]{2,1,0:T(8,128)(2,1)} %collective-permute-done.13.refs_18_.refs_15_), channel_id=1, source_target_pairs={{8,0},{16,8},{24,16},{28,24},{20,28},{12,20},{4,12},{0,4},{9,1},{1... | collective-permute-start | bytes 786440 | tf_op jit(solution)/shard_map/ppermute | solution.py:470
  90.1 13.5 %collective-permute-start.25 = (bf16[64,16,128]{2,1,0:T(8,128)(2,1)}, bf16[64,16,128]{2,1,0:T(8,128)(2,1)}, u32[]{:S(2)}, u32[]{:S(2)}) collective-permute-start(bf16[64,16,128]{2,1,0:T(8,128)(2,1)} %collective-permute-done.24.refs_10_.refs_7_), channel_id=1, source_target_pairs={{0,8},{8,16},{16,24},{24,28},{28,20},{20,12},{12,4},{4,0},{1,9},{9... | collective-permute-start | bytes 786440 | tf_op jit(solution)/shard_map/ppermute | solution.py:470
  93.3 12.4 %collective-permute-start.32 = (bf16[64,16,128]{2,1,0:T(8,128)(2,1)}, bf16[64,16,128]{2,1,0:T(8,128)(2,1)}, u32[]{:S(2)}, u32[]{:S(2)}) collective-permute-start(bf16[64,16,128]{2,1,0:T(8,128)(2,1)} %collective-permute-done.31.refs_18_.refs_15_), channel_id=1, source_target_pairs={{8,0},{16,8},{24,16},{28,24},{20,28},{12,20},{4,12},{0,4},{9,1},{1... | collective-permute-start | bytes 786440 | tf_op jit(solution)/shard_map/ppermute | solution.py:470
  103.7 12.9 %collective-permute-start.26 = (bf16[64,16,128]{2,1,0:T(8,128)(2,1)}, bf16[64,16,128]{2,1,0:T(8,128)(2,1)}, u32[]{:S(2)}, u32[]{:S(2)}) collective-permute-start(bf16[64,16,128]{2,1,0:T(8,128)(2,1)} %collective-permute-done.25.refs_11_.refs_8_), channel_id=1, source_target_pairs={{0,8},{8,16},{16,24},{24,28},{28,20},{20,12},{12,4},{4,0},{1,9},{9... | collective-permute-start | bytes 786440 | tf_op jit(solution)/shard_map/ppermute | solution.py:470
  105.7 12.9 %collective-permute-start.33 = (bf16[64,16,128]{2,1,0:T(8,128)(2,1)}, bf16[64,16,128]{2,1,0:T(8,128)(2,1)}, u32[]{:S(2)}, u32[]{:S(2)}) collective-permute-start(bf16[64,16,128]{2,1,0:T(8,128)(2,1)} %collective-permute-done.32.refs_19_.refs_16_), channel_id=1, source_target_pairs={{8,0},{16,8},{24,16},{28,24},{20,28},{12,20},{4,12},{0,4},{9,1},{1... | collective-permute-start | bytes 786440 | tf_op jit(solution)/shard_map/ppermute | solution.py:470
  110.8 11.3 %collective-permute-start.16 = (bf16[64,16,128]{2,1,0:T(8,128)(2,1)S(1)}, bf16[64,16,128]{2,1,0:T(8,128)(2,1)}, u32[]{:S(2)}, u32[]{:S(2)}) collective-permute-start(bf16[64,16,128]{2,1,0:T(8,128)(2,1)S(1)} %collective-permute-done.15.refs_12_.refs_9_), channel_id=1, source_target_pairs={{0,8},{8,16},{16,24},{24,28},{28,20},{20,12},{12,4},{4,0},{1,9},{9... | collective-permute-start | bytes 786440 | tf_op jit(solution)/shard_map/ppermute | solution.py:470
  112.9 11.3 %collective-permute-start.20 = (bf16[64,16,128]{2,1,0:T(8,128)(2,1)S(1)}, bf16[64,16,128]{2,1,0:T(8,128)(2,1)}, u32[]{:S(2)}, u32[]{:S(2)}) collective-permute-start(bf16[64,16,128]{2,1,0:T(8,128)(2,1)S(1)} %collective-permute-done.19.refs_20_.refs_17_), channel_id=1, source_target_pairs={{8,0},{16,8},{24,16},{28,24},{20,28},{12,20},{4,12},{0,4},{9,1},{1... | collective-permute-start | bytes 786440 | tf_op jit(solution)/shard_map/ppermute | solution.py:470
  116.6 11.2 %collective-permute-start.27 = (bf16[64,16,128]{2,1,0:T(8,128)(2,1)}, bf16[64,16,128]{2,1,0:T(8,128)(2,1)}, u32[]{:S(2)}, u32[]{:S(2)}) collective-permute-start(bf16[64,16,128]{2,1,0:T(8,128)(2,1)} %collective-permute-done.26.refs_12_.refs_9_), channel_id=1, source_target_pairs={{0,8},{8,16},{16,24},{24,28},{28,20},{20,12},{12,4},{4,0},{1,9},{9... | collective-permute-start | bytes 786440 | tf_op jit(solution)/shard_map/ppermute | solution.py:470
  118.6 11.2 %collective-permute-start.34 = (bf16[64,16,128]{2,1,0:T(8,128)(2,1)}, bf16[64,16,128]{2,1,0:T(8,128)(2,1)}, u32[]{:S(2)}, u32[]{:S(2)}) collective-permute-start(bf16[64,16,128]{2,1,0:T(8,128)(2,1)} %collective-permute-done.33.refs_20_.refs_17_), channel_id=1, source_target_pairs={{8,0},{16,8},{24,16},{28,24},{20,28},{12,20},{4,12},{0,4},{9,1},{1... | collective-permute-start | bytes 786440 | tf_op jit(solution)/shard_map/ppermute | solution.py:470
  122.2 11.2 %collective-permute-start.17 = (bf16[64,16,128]{2,1,0:T(8,128)(2,1)}, bf16[64,16,128]{2,1,0:T(8,128)(2,1)}, u32[]{:S(2)}, u32[]{:S(2)}) collective-permute-start(bf16[64,16,128]{2,1,0:T(8,128)(2,1)} %collective-permute-done.16.refs_13_.refs_10_), channel_id=1, source_target_pairs={{0,8},{8,16},{16,24},{24,28},{28,20},{20,12},{12,4},{4,0},{1,9},{9... | collective-permute-start | bytes 786440 | tf_op jit(solution)/shard_map/ppermute | solution.py:470
  124.2 11.2 %collective-permute-start.21 = (bf16[64,16,128]{2,1,0:T(8,128)(2,1)}, bf16[64,16,128]{2,1,0:T(8,128)(2,1)}, u32[]{:S(2)}, u32[]{:S(2)}) collective-permute-start(bf16[64,16,128]{2,1,0:T(8,128)(2,1)} %collective-permute-done.20.refs_21_.refs_18_), channel_id=1, source_target_pairs={{8,0},{16,8},{24,16},{28,24},{20,28},{12,20},{4,12},{0,4},{9,1},{1... | collective-permute-start | bytes 786440 | tf_op jit(solution)/shard_map/ppermute | solution.py:470
  127.8 11.2 %collective-permute-start.28 = (bf16[64,16,128]{2,1,0:T(8,128)(2,1)}, bf16[64,16,128]{2,1,0:T(8,128)(2,1)}, u32[]{:S(2)}, u32[]{:S(2)}) collective-permute-start(bf16[64,16,128]{2,1,0:T(8,128)(2,1)} %collective-permute-done.27.refs_13_.refs_10_), channel_id=1, source_target_pairs={{0,8},{8,16},{16,24},{24,28},{28,20},{20,12},{12,4},{4,0},{1,9},{9... | collective-permute-start | bytes 786440 | tf_op jit(solution)/shard_map/ppermute | solution.py:470
  129.9 11.2 %collective-permute-start.35 = (bf16[64,16,128]{2,1,0:T(8,128)(2,1)}, bf16[64,16,128]{2,1,0:T(8,128)(2,1)}, u32[]{:S(2)}, u32[]{:S(2)}) collective-permute-start(bf16[64,16,128]{2,1,0:T(8,128)(2,1)} %collective-permute-done.34.refs_21_.refs_18_), channel_id=1, source_target_pairs={{8,0},{16,8},{24,16},{28,24},{20,28},{12,20},{4,12},{0,4},{9,1},{1... | collective-permute-start | bytes 786440 | tf_op jit(solution)/shard_map/ppermute | solution.py:470
  133.4 11.2 %collective-permute-start.18 = (bf16[64,16,128]{2,1,0:T(8,128)(2,1)}, bf16[64,16,128]{2,1,0:T(8,128)(2,1)}, u32[]{:S(2)}, u32[]{:S(2)}) collective-permute-start(bf16[64,16,128]{2,1,0:T(8,128)(2,1)} %collective-permute-done.17.refs_14_.refs_11_), channel_id=1, source_target_pairs={{0,8},{8,16},{16,24},{24,28},{28,20},{20,12},{12,4},{4,0},{1,9},{9... | collective-permute-start | bytes 786440 | tf_op jit(solution)/shard_map/ppermute | solution.py:470
  135.5 11.2 %collective-permute-start.22 = (bf16[64,16,128]{2,1,0:T(8,128)(2,1)}, bf16[64,16,128]{2,1,0:T(8,128)(2,1)}, u32[]{:S(2)}, u32[]{:S(2)}) collective-permute-start(bf16[64,16,128]{2,1,0:T(8,128)(2,1)} %collective-permute-done.21.refs_22_.refs_19_), channel_id=1, source_target_pairs={{8,0},{16,8},{24,16},{28,24},{20,28},{12,20},{4,12},{0,4},{9,1},{1... | collective-permute-start | bytes 786440 | tf_op jit(solution)/shard_map/ppermute | solution.py:470
  139.0 22.9 %collective-permute-start.29 = (bf16[64,16,128]{2,1,0:T(8,128)(2,1)}, bf16[64,16,128]{2,1,0:T(8,128)(2,1)S(1)}, u32[]{:S(2)}, u32[]{:S(2)}) collective-permute-start(bf16[64,16,128]{2,1,0:T(8,128)(2,1)} %collective-permute-done.28.refs_14_.refs_11_), channel_id=1, source_target_pairs={{0,8},{8,16},{16,24},{24,28},{28,20},{20,12},{12,4},{4,0},{1,9},{9... | collective-permute-start | bytes 786440 | tf_op jit(solution)/shard_map/ppermute | solution.py:470
  141.1 20.9 %collective-permute-start.36 = (bf16[64,16,128]{2,1,0:T(8,128)(2,1)}, bf16[64,16,128]{2,1,0:T(8,128)(2,1)S(1)}, u32[]{:S(2)}, u32[]{:S(2)}) collective-permute-start(bf16[64,16,128]{2,1,0:T(8,128)(2,1)} %collective-permute-done.35.refs_22_.refs_19_), channel_id=1, source_target_pairs={{8,0},{16,8},{24,16},{28,24},{20,28},{12,20},{4,12},{0,4},{9,1},{1... | collective-permute-start | bytes 786440 | tf_op jit(solution)/shard_map/ppermute | solution.py:470
  159.9 16.0 %collective-permute-start.53 = (bf16[16,64,128]{2,1,0:T(8,128)(2,1)S(1)}, bf16[16,64,128]{2,1,0:T(8,128)(2,1)S(1)}, u32[]{:S(2)}, u32[]{:S(2)}) collective-permute-start(bf16[16,64,128]{2,1,0:T(8,128)(2,1)S(1)} %get-tuple-element.69), channel_id=1, source_target_pairs={{0,8},{8,16},{16,24},{24,28},{28,20},{20,12},{12,4},{4,0},{1,9},{9... | collective-permute-start | bytes 786440 | tf_op jit(solution)/shard_map/ppermute | solution.py:341
  162.0 14.0 %collective-permute-start.54 = (bf16[16,64,128]{2,1,0:T(8,128)(2,1)S(1)}, bf16[16,64,128]{2,1,0:T(8,128)(2,1)S(1)}, u32[]{:S(2)}, u32[]{:S(2)}) collective-permute-start(bf16[16,64,128]{2,1,0:T(8,128)(2,1)S(1)} %get-tuple-element.68), channel_id=1, source_target_pairs={{8,0},{16,8},{24,16},{28,24},{20,28},{12,20},{4,12},{0,4},{9,1},{1... | collective-permute-start | bytes 786440 | tf_op jit(solution)/shard_map/ppermute | solution.py:341
  176.1 18.3 %collective-permute-start.55 = (bf16[16,64,128]{2,1,0:T(8,128)(2,1)S(1)}, bf16[16,64,128]{2,1,0:T(8,128)(2,1)S(1)}, u32[]{:S(2)}, u32[]{:S(2)}) collective-permute-start(bf16[16,64,128]{2,1,0:T(8,128)(2,1)S(1)} %get-tuple-element.66), channel_id=1, source_target_pairs={{0,8},{8,16},{16,24},{24,28},{28,20},{20,12},{12,4},{4,0},{1,9},{9... | collective-permute-start | bytes 786440 | tf_op jit(solution)/shard_map/ppermute | solution.py:341
  178.2 16.2 %collective-permute-start.61 = (bf16[16,64,128]{2,1,0:T(8,128)(2,1)S(1)}, bf16[16,64,128]{2,1,0:T(8,128)(2,1)S(1)}, u32[]{:S(2)}, u32[]{:S(2)}) collective-permute-start(bf16[16,64,128]{2,1,0:T(8,128)(2,1)S(1)} %get-tuple-element.67), channel_id=1, source_target_pairs={{8,0},{16,8},{24,16},{28,24},{20,28},{12,20},{4,12},{0,4},{9,1},{1... | collective-permute-start | bytes 786440 | tf_op jit(solution)/shard_map/ppermute | solution.py:341
  194.6 13.3 %collective-permute-start.56 = (bf16[16,64,128]{2,1,0:T(8,128)(2,1)S(1)}, bf16[16,64,128]{2,1,0:T(8,128)(2,1)S(1)}, u32[]{:S(2)}, u32[]{:S(2)}) collective-permute-start(bf16[16,64,128]{2,1,0:T(8,128)(2,1)S(1)} %get-tuple-element.64), channel_id=1, source_target_pairs={{0,8},{8,16},{16,24},{24,28},{28,20},{20,12},{12,4},{4,0},{1,9},{9... | collective-permute-start | bytes 786440 | tf_op jit(solution)/shard_map/ppermute | solution.py:341
  194.7 13.2 %collective-permute-start.62 = (bf16[16,64,128]{2,1,0:T(8,128)(2,1)S(1)}, bf16[16,64,128]{2,1,0:T(8,128)(2,1)S(1)}, u32[]{:S(2)}, u32[]{:S(2)}) collective-permute-start(bf16[16,64,128]{2,1,0:T(8,128)(2,1)S(1)} %get-tuple-element.65), channel_id=1, source_target_pairs={{8,0},{16,8},{24,16},{28,24},{20,28},{12,20},{4,12},{0,4},{9,1},{1... | collective-permute-start | bytes 786440 | tf_op jit(solution)/shard_map/ppermute | solution.py:341
  197.9 13.5 %collective-permute-start.43 = (bf16[16,64,128]{2,1,0:T(8,128)(2,1)S(1)}, bf16[16,64,128]{2,1,0:T(8,128)(2,1)S(1)}, u32[]{:S(2)}, u32[]{:S(2)}) collective-permute-start(bf16[16,64,128]{2,1,0:T(8,128)(2,1)S(1)} %get-tuple-element.81), channel_id=1, source_target_pairs={{0,8},{8,16},{16,24},{24,28},{28,20},{20,12},{12,4},{4,0},{1,9},{9... | collective-permute-start | bytes 786440 | tf_op jit(solution)/shard_map/ppermute | solution.py:341
  198.0 13.4 %collective-permute-start.48 = (bf16[16,64,128]{2,1,0:T(8,128)(2,1)S(1)}, bf16[16,64,128]{2,1,0:T(8,128)(2,1)S(1)}, u32[]{:S(2)}, u32[]{:S(2)}) collective-permute-start(bf16[16,64,128]{2,1,0:T(8,128)(2,1)S(1)} %get-tuple-element.80), channel_id=1, source_target_pairs={{8,0},{16,8},{24,16},{28,24},{20,28},{12,20},{4,12},{0,4},{9,1},{1... | collective-permute-start | bytes 786440 | tf_op jit(solution)/shard_map/ppermute | solution.py:341
  211.3 28.9 %collective-permute-start.41 = (bf16[2,64,4096]{2,1,0:T(8,128)(2,1)S(1)}, bf16[2,64,4096]{2,1,0:T(8,128)(2,1)S(1)}, u32[]{:S(2)}, u32[]{:S(2)}) collective-permute-start(bf16[2,64,4096]{2,1,0:T(8,128)(2,1)S(1)} %pad_maximum_fusion.1), channel_id=1, source_target_pairs={{0,1},{1,0},{2,3},{3,2},{4,5},{5,4},{6,7},{7,6},{8,9},{9,8},{10,11... | collective-permute-start | bytes 3145736 | tf_op jit(solution)/shard_map/ppermute | solution.py:305
  215.0 11.4 %collective-permute-start.58 = (bf16[16,64,128]{2,1,0:T(8,128)(2,1)S(1)}, bf16[16,64,128]{2,1,0:T(8,128)(2,1)S(1)}, u32[]{:S(2)}, u32[]{:S(2)}) collective-permute-start(bf16[16,64,128]{2,1,0:T(8,128)(2,1)S(1)} %get-tuple-element.60), channel_id=1, source_target_pairs={{0,8},{8,16},{16,24},{24,28},{28,20},{20,12},{12,4},{4,0},{1,9},{9... | collective-permute-start | bytes 786440 | tf_op jit(solution)/shard_map/ppermute | solution.py:341
  215.9 10.8 %collective-permute-start.64 = (bf16[16,64,128]{2,1,0:T(8,128)(2,1)S(1)}, bf16[16,64,128]{2,1,0:T(8,128)(2,1)S(1)}, u32[]{:S(2)}, u32[]{:S(2)}) collective-permute-start(bf16[16,64,128]{2,1,0:T(8,128)(2,1)S(1)} %get-tuple-element.61), channel_id=1, source_target_pairs={{8,0},{16,8},{24,16},{28,24},{20,28},{12,20},{4,12},{0,4},{9,1},{1... | collective-permute-start | bytes 786440 | tf_op jit(solution)/shard_map/ppermute | solution.py:341
  221.3 10.8 %collective-permute-start.45 = (bf16[16,64,128]{2,1,0:T(8,128)(2,1)S(1)}, bf16[16,64,128]{2,1,0:T(8,128)(2,1)S(1)}, u32[]{:S(2)}, u32[]{:S(2)}) collective-permute-start(bf16[16,64,128]{2,1,0:T(8,128)(2,1)S(1)} %get-tuple-element.76), channel_id=1, source_target_pairs={{0,8},{8,16},{16,24},{24,28},{28,20},{20,12},{12,4},{4,0},{1,9},{9... | collective-permute-start | bytes 786440 | tf_op jit(solution)/shard_map/ppermute | solution.py:341
  226.9 10.7 %collective-permute-start.59 = (bf16[16,64,128]{2,1,0:T(8,128)(2,1)S(1)}, bf16[16,64,128]{2,1,0:T(8,128)(2,1)S(1)}, u32[]{:S(2)}, u32[]{:S(2)}) collective-permute-start(bf16[16,64,128]{2,1,0:T(8,128)(2,1)S(1)} %get-tuple-element.58), channel_id=1, source_target_pairs={{0,8},{8,16},{16,24},{24,28},{28,20},{20,12},{12,4},{4,0},{1,9},{9... | collective-permute-start | bytes 786440 | tf_op jit(solution)/shard_map/ppermute | solution.py:341
  238.1 10.7 %collective-permute-start.60 = (bf16[16,64,128]{2,1,0:T(8,128)(2,1)S(1)}, bf16[16,64,128]{2,1,0:T(8,128)(2,1)S(1)}, u32[]{:S(2)}, u32[]{:S(2)}) collective-permute-start(bf16[16,64,128]{2,1,0:T(8,128)(2,1)S(1)} %get-tuple-element.56), channel_id=1, source_target_pairs={{0,8},{8,16},{16,24},{24,28},{28,20},{20,12},{12,4},{4,0},{1,9},{9... | collective-permute-start | bytes 786440 | tf_op jit(solution)/shard_map/ppermute | solution.py:341
  240.5 14.9 %collective-permute-start.42 = (bf16[2,32,4096]{2,1,0:T(8,128)(2,1)S(1)}, bf16[2,32,4096]{2,1,0:T(8,128)(2,1)S(1)}, u32[]{:S(2)}, u32[]{:S(2)}) collective-permute-start(bf16[2,32,4096]{2,1,0:T(8,128)(2,1)S(1)} %slice.243), channel_id=1, source_target_pairs={{0,2},{1,3},{2,0},{3,1},{4,6},{5,7},{6,4},{7,5},{8,10},{9,11},{10,... | collective-permute-start | bytes 1572872 | tf_op jit(solution)/shard_map/ppermute | solution.py:305
  (39 other events, 504.3 us)

commit v5 on v4

--- a/solution.py
+++ b/solution.py
@@ -42,10 +42,6 @@
     return lax.dot_general(a, b, (((ca,), (cb,)), ((), ())), preferred_element_type=jnp.float32)
 
 
-def unroll_of(count):
-    return math.gcd(count, 8)
-
-
 class Whole:
     sides = 1
 
@@ -58,15 +54,14 @@
 
 
 class Parts:
-    def __init__(self, arrays, slots):
-        self.arrays, self.tables, self.slots = list(arrays), [], slots
-        first = arrays[0]
-        self.held = pltpu.VMEM((len(arrays) * slots, *first.shape[1:]), first.dtype)
+    def __init__(self, arrays, first, slots):
+        self.arrays, self.tables, self.first, self.slots = list(arrays), [], first, slots
+        self.held = pltpu.VMEM((len(arrays) * slots, *arrays[0].shape[1:]), arrays[0].dtype)
 
     def copies(self, tables, refs, held, sems):
         slots = self.slots
         return [
-            pltpu.make_async_copy(ref.at[pl.ds(0, slots)], held.at[pl.ds(i * slots, slots)], sems.at[i])
+            pltpu.make_async_copy(ref.at[pl.ds(self.first, slots)], held.at[pl.ds(i * slots, slots)], sems.at[i])
             for i, ref in enumerate(refs)
         ]
 
@@ -159,47 +154,46 @@
     )(*small, *tables, *arrays)
 
 
-def split_blocks(me, up, down, note, devices):
+def split_blocks(me, up, down, codes, group_blocks, devices):
     slots = up.shape[0]
     piece = BLK // devices
 
-    def kernel(need, send, me_ref, up_ref, down_ref, note_ref, *outs):
-        need(0, 1, 2)
+    def kernel(need, send, me_ref, codes_ref, up_ref, down_ref, *refs):
+        *outs, note = refs
+        need(0)
+        code = codes_ref[...]
+        live = code >= 0
+        known = jnp.where(live, code, 0)
+        note[...] = jnp.zeros_like(note)
+        note[0:2, 0:slots] = lax.div(known, jnp.full_like(known, group_blocks)).astype(jnp.float32)
+        note[2:4, 0:slots] = jnp.where(live, lax.rem(known, jnp.full_like(known, group_blocks)), -1).astype(jnp.float32)
+        need(1, 2)
         for step, out in enumerate(outs):
             start = pl.multiple_of((me_ref[0] ^ step) * piece, piece)
             out[:slots] = up_ref[:, pl.ds(start, piece), :]
             out[slots : 2 * slots] = down_ref[:, pl.ds(start, piece), :]
-            out[2 * slots] = note_ref[...]
+            out[2 * slots] = note[...].astype(jnp.bfloat16)
             send(step)
 
     out = [shape((2 * slots + 1, piece, BLK), up.dtype)] * devices
-    return run(kernel, [me], [Whole(up), Whole(down), Whole(note)], out, nbytes=8 * up.size)
-
-
-def pack_pieces(pick, parts, slots, live):
+    items = [Whole(codes), Whole(up), Whole(down)]
+    return run(kernel, [me], items, out, [pltpu.VMEM((piece, BLK), jnp.float32)], nbytes=8 * up.size)
+
+
+def pack_pieces(pick, parts, first, slots, live):
     piece = parts[0].shape[1]
     half = live // 2
-    unroll = unroll_of(half)
-
-    def kernel(need, send, up_pick, down_pick, held, *outs):
+
+    def kernel(need, send, pick_ref, held, *outs):
         need(0)
-        for which, picked in enumerate((up_pick, down_pick)):
-            ahead, behind = outs[2 * which : 2 * which + 2]
-
-            def body(i, carry, picked=picked, ahead=ahead, behind=behind):
-                for u in range(unroll):
-                    k = i * unroll + u
-                    ahead[k] = held[picked[k]]
-                    behind[k] = held[picked[half + k]]
-                return carry
-
-            lax.fori_loop(0, half // unroll, body, 0)
-            send(2 * which)
-            send(2 * which + 1)
-
-    out = [shape((half, piece, BLK), parts[0].dtype)] * 4
-    items = [Parts(parts, 2 * slots)]
-    return run(kernel, [pick[0], pick[1]], items, out, nbytes=6 * len(parts) * slots * piece * BLK)
+        for side, out in enumerate(outs):
+            for k in range(half):
+                out[k] = held[pick_ref[side * half + k]]
+            send(side)
+
+    out = [shape((half, piece, BLK), parts[0].dtype)] * 2
+    nbytes = 3 * len(parts) * slots * piece * BLK
+    return tuple(run(kernel, [pick], [Parts(parts, first, slots)], out, nbytes=nbytes))
 
 
 def lanes(ref, block):
@@ -256,7 +250,7 @@
         )
         return carry
 
-    lax.fori_loop(0, acc.shape[0], body, 0)
+    lax.fori_loop(0, acc.shape[0], body, 0, unroll=4)
     send(0)
     send(1)
     need(2)
@@ -273,7 +267,7 @@
         grad[c] = (acc[c] * slope[c]).astype(jnp.bfloat16)
         return carry
 
-    lax.fori_loop(0, acc.shape[0], body, 0)
+    lax.fori_loop(0, acc.shape[0], body, 0, unroll=4)
     send(0)
     need(3)
     up_terms(owner, up_rows, up_cols, tok_turned, grad, out, lambda q: send(1, q))
@@ -445,34 +439,23 @@
         kernel = functools.partial(width_kernel, contract, weights.sides)
         return run(kernel, [rows, cols], [Whole(x), weights], outs, [model_acc], flops, nbytes)[0]
 
-    is_live = codes >= 0
-    row_codes = jnp.where(is_live, codes // group_blocks, 0)
-    col_codes = jnp.where(is_live, codes % group_blocks, -1)
-
     if BLK % (PACK * devices) == 0 and slots <= BLK:
         here = me.reshape(1).astype(jnp.int32)
-        piece = BLK // devices
-
-        note = jnp.concatenate([row_codes, col_codes]).reshape(4, slots).astype(jnp.bfloat16)
-        note = jnp.pad(note, ((0, piece - 4), (0, BLK - slots)))
-        messages = split_blocks(here, up_slots, down_slots, note, devices)
+        messages = split_blocks(here, up_slots, down_slots, codes.reshape(2, slots), group_blocks, devices)
         parts = [messages[0]] * devices
         for step in range(1, devices):
             parts[step] = lax.ppermute(messages[step], "dp", [(i, i ^ step) for i in range(devices)])
         notes = jnp.stack([part[2 * slots, :4, :slots] for part in parts], axis=1).astype(jnp.int32)
         pick, rows, cols = tables(notes[:2], notes[2:], index ^ me)
-        place_of = (pick // slots) * (2 * slots) + pick % slots
-        pick = place_of + jnp.array([[0], [slots]], jnp.int32)
-
         tok, cot = gather_rows(tie(jnp.stack([tokens, cotangent]), parts[1]))
 
         def onward(pair):
             return lax.ppermute(pair[0], "dp", ahead), lax.ppermute(pair[1], "dp", behind)
 
-        packed = pack_pieces(pick, parts, slots, live)
         tok_turned = tok.T
 
-        up_ring, down_ring = [tuple(packed[:2])], [tuple(packed[2:])]
+        up_ring = [pack_pieces(pick[0], parts, 0, slots, live)]
+        down_ring = [pack_pieces(pick[1], parts, slots, slots, live)]
         for s in range(1, devices):
             up_ring.append(onward(tie(up_ring[-1], tok_turned) if s == devices // 2 else up_ring[-1]))
             down_ring.append(onward(down_ring[-1]))
@@ -482,6 +465,9 @@
         def everywhere(x, axis):
             return lax.all_gather(x, "dp", axis=axis, tiled=True)
 
+        is_live = codes >= 0
+        row_codes = jnp.where(is_live, codes // group_blocks, 0)
+        col_codes = jnp.where(is_live, codes % group_blocks, -1)
         pick, rows, cols = tables(everywhere(row_codes, 1), everywhere(col_codes, 1), index)
         tok, cot = gather_rows(jnp.stack([tokens, cotangent]))
         tok_turned = tok.T

time: 257 us -> 254 us (0.988)
  waiting for transfers between devices: 93.8 us -> 90.8 us
    ppermute x14, waiting for transfers between devices: 30.7 us -> 27.7 us  [onward(): lax.ppermute(pair[0], 'dp', ahead)]
    pallas_call x6 -> x7, Pallas kernels: 42.6 us -> 43.2 us  [run(): pl.pallas_call(body, out_shape=list(outs), in_specs=[SMEM_SPEC] * (len(sm...]
  transfers between devices with their start and end apart: 67 -> 67, of which waited for: 35 -> 35; matrix products, arithmetic and copies ran while one was open for 11% -> 11% of each run, Pallas kernels for 15% -> 16%
where the time goes in v5:
time: 254 us; the launch traced here: 253 us
  waiting for transfers between devices  90.8 us (36%)
  starting transfers between devices  85.7 us (34%)
  Pallas kernels  43.2 us (17%)
  local copies, waits for them, and re-layouts  16.8 us (7%)
  other arithmetic  15.5 us (6%)
    pallas_call x7, Pallas kernels, run(): pl.pallas_call(body, out_shape=list(outs), in_specs=[SMEM_SPEC] * (len(sm...  43.2 us
    ppermute x14, starting transfers between devices, onward(): lax.ppermute(pair[0], 'dp', ahead)  39.6 us
    ppermute x7, waiting for transfers between devices, shards(): lax.ppermute(messages[step], 'dp', [(i, i ^ step) for i in range(devices)])  28.6 us
    ppermute x14, waiting for transfers between devices, onward(): lax.ppermute(pair[0], 'dp', ahead)  27.7 us
    ppermute x14, waiting for transfers between devices, send(): lax.ppermute(a, 'dp', self.ahead)  25.4 us
    ppermute x14, starting transfers between devices, send(): lax.ppermute(b, 'dp', self.behind)  16.5 us
    ppermute x7, starting transfers between devices, shards(): lax.ppermute(messages[step], 'dp', [(i, i ^ step) for i in range(devices)])  13.7 us
    ppermute x14, starting transfers between devices, send(): lax.ppermute(a, 'dp', self.ahead)  12.6 us
  transfers between devices with their start and end apart: 67, of which 35 were waited for; matrix products, arithmetic and copies ran while one was open for 11% of the time, Pallas kernels for 16%

profile of v5, /device:TPU:0, one launch (start us, length us, event | category | flops | bytes accessed | tf_op | source)
XLA Modules:
  0.0 253.2 jit_solution(16570746405999223043)
XLA Ops:
  1.9 3.0 %shard_map.102 = (bf16[65,16,128]{2,1,0:T(8,128)(2,1)}, bf16[65,16,128]{2,1,0:T(8,128)(2,1)}, bf16[65,16,128]{2,1,0:T(8,128)(2,1)}, bf16[65,16,128]{2,1,0:T(8,12...) custom-call(s32[1]{0:T(128)} %bitcast.refs_0_, ...), custom_call_target="tpu_custom_call" | custom-call | bytes 4194304 | tf_op jit(solution)/shard_map/pallas_call | solution.py:140
  5.0 3.0 %collective-permute-start = (bf16[65,16,128]{2,1,0:T(8,128)(2,1)}, bf16[65,16,128]{2,1,0:T(8,128)(2,1)S(1)}, u32[]{:S(2)}, u32[]{:S(2)}) collective-permute-start(bf16[65,16,128]{2,1,0:T(8,128)(2,1)} %get-tuple-element.29), channel_id=1, source_target_pairs={{0,4},{4,0},{8,12},{12,8},{16,20},{20,16},{24,28},{28,24},{1,5},{5... | collective-permute-start | bytes 798728 | tf_op jit(solution)/shard_map/ppermute | solution.py:447
  9.5 3.0 %collective-permute-start.3 = (bf16[65,16,128]{2,1,0:T(8,128)(2,1)}, bf16[65,16,128]{2,1,0:T(8,128)(2,1)S(1)}, u32[]{:S(2)}, u32[]{:S(2)}) collective-permute-start(bf16[65,16,128]{2,1,0:T(8,128)(2,1)} %get-tuple-element.32), channel_id=1, source_target_pairs={{0,16},{4,20},{8,24},{12,28},{16,0},{20,4},{24,8},{28,12},{1,17},{... | collective-permute-start | bytes 798728 | tf_op jit(solution)/shard_map/ppermute | solution.py:447
  14.6 3.8 %collective-permute-start.5 = (bf16[65,16,128]{2,1,0:T(8,128)(2,1)}, bf16[65,16,128]{2,1,0:T(8,128)(2,1)S(1)}, u32[]{:S(2)}, u32[]{:S(2)}) collective-permute-start(bf16[65,16,128]{2,1,0:T(8,128)(2,1)} %get-tuple-element.34), channel_id=1, source_target_pairs={{0,24},{4,28},{8,16},{12,20},{16,8},{20,12},{24,0},{28,4},{1,25},{... | collective-permute-start | bytes 798728 | tf_op jit(solution)/shard_map/ppermute | solution.py:447
  18.4 9.5 %collective-permute-done.1.refs_3_ = bf16[65,16,128]{2,1,0:T(8,128)(2,1)S(1)} collective-permute-done((bf16[65,16,128]{2,1,0:T(8,128)(2,1)}, bf16[65,16,128]{2,1,0:T(8,128)(2,1)S(1)}, u32[]{:S(2)}, u32[]{:S(2)}) %collective-permute-start.1) | collective-permute-done | bytes 266272 | tf_op jit(solution)/shard_map/ppermute | solution.py:447
  29.0 2.3 collective-permute-done.2.refs_4_
  33.1 16.8 %collective-permute-done.4.refs_6_ = bf16[65,16,128]{2,1,0:T(8,128)(2,1)S(1)} collective-permute-done((bf16[65,16,128]{2,1,0:T(8,128)(2,1)}, bf16[65,16,128]{2,1,0:T(8,128)(2,1)S(1)}, u32[]{:S(2)}, u32[]{:S(2)}) %collective-permute-start.4) | collective-permute-done | bytes 266272 | tf_op jit(solution)/shard_map/ppermute | solution.py:447
  52.2 2.9 %shard_map.103 = (bf16[64,16,128]{2,1,0:T(8,128)(2,1)}, bf16[64,16,128]{2,1,0:T(8,128)(2,1)}) custom-call(s32[128]{0:T(128)} %get-tuple-element.97.refs_0_, bf16[65,16,128]{2,1,0:T(8,128)(2,1)} %get-tuple-element.28.refs_1_, bf16[65,16,128]{2,1,0:T(8,128)(2,1)} %copy-done.4, bf16[65,16,128]{2,1,0:T(8,128)(2,1)} %copy-done.5, bf16[65,16,128]{2,1,0:T(8,128)(2,1)} %copy-done.6, ...), custom_call_target="tpu_custom_call" | custom-call | bytes 1572864 | tf_op jit(solution)/shard_map/pallas_call | solution.py:140
  55.1 9.9 %collective-permute-start.9 = (bf16[64,16,128]{2,1,0:T(8,128)(2,1)}, bf16[64,16,128]{2,1,0:T(8,128)(2,1)S(1)}, u32[]{:S(2)}, u32[]{:S(2)}) collective-permute-start(bf16[64,16,128]{2,1,0:T(8,128)(2,1)} %get-tuple-element.37.refs_8_.refs_5_), channel_id=1, source_target_pairs={{0,8},{8,16},{16,24},{24,28},{28,20},{20,12},{12,4},{4,0},{1,9},{9... | collective-permute-start | bytes 786440 | tf_op jit(solution)/shard_map/ppermute | solution.py:453
  65.0 2.9 %shard_map.105 = (bf16[64,16,128]{2,1,0:T(8,128)(2,1)}, bf16[64,16,128]{2,1,0:T(8,128)(2,1)}) custom-call(s32[128]{0:T(128)} %get-tuple-element.98.refs_0_, bf16[65,16,128]{2,1,0:T(8,128)(2,1)} %get-tuple-element.28.refs_1_, bf16[65,16,128]{2,1,0:T(8,128)(2,1)} %copy-done.4, bf16[65,16,128]{2,1,0:T(8,128)(2,1)} %copy-done.5, bf16[65,16,128]{2,1,0:T(8,128)(2,1)} %copy-done.6, ...), custom_call_target="tpu_custom_call" | custom-call | bytes 1572864 | tf_op jit(solution)/shard_map/pallas_call | solution.py:140
  67.9 2.8 %collective-permute-start.23 = (bf16[64,16,128]{2,1,0:T(8,128)(2,1)}, bf16[64,16,128]{2,1,0:T(8,128)(2,1)}, u32[]{:S(2)}, u32[]{:S(2)}) collective-permute-start(bf16[64,16,128]{2,1,0:T(8,128)(2,1)} %get-tuple-element.42.refs_8_.refs_5_), channel_id=1, source_target_pairs={{0,8},{8,16},{16,24},{24,28},{28,20},{20,12},{12,4},{4,0},{1,9},{9... | collective-permute-start | bytes 786440 | tf_op jit(solution)/shard_map/ppermute | solution.py:453
  71.7 2.9 %collective-permute-start.10 = (bf16[64,16,128]{2,1,0:T(8,128)(2,1)S(1)}, bf16[64,16,128]{2,1,0:T(8,128)(2,1)}, u32[]{:S(2)}, u32[]{:S(2)}) collective-permute-start(bf16[64,16,128]{2,1,0:T(8,128)(2,1)S(1)} %collective-permute-done.9.refs_9_.refs_6_), channel_id=1, source_target_pairs={{0,8},{8,16},{16,24},{24,28},{28,20},{20,12},{12,4},{4,0},{1,9},{9... | collective-permute-start | bytes 786440 | tf_op jit(solution)/shard_map/ppermute | solution.py:453
  75.1 2.5 %collective-permute-done.23.refs_9_.refs_6_ = bf16[64,16,128]{2,1,0:T(8,128)(2,1)} collective-permute-done((bf16[64,16,128]{2,1,0:T(8,128)(2,1)}, bf16[64,16,128]{2,1,0:T(8,128)(2,1)}, u32[]{:S(2)}, u32[]{:S(2)}) %collective-permute-start.23) | collective-permute-done | bytes 262176 | tf_op jit(solution)/shard_map/ppermute | solution.py:453
  77.7 2.6 %collective-permute-start.24 = (bf16[64,16,128]{2,1,0:T(8,128)(2,1)}, bf16[64,16,128]{2,1,0:T(8,128)(2,1)}, u32[]{:S(2)}, u32[]{:S(2)}) collective-permute-start(bf16[64,16,128]{2,1,0:T(8,128)(2,1)} %collective-permute-done.23.refs_9_.refs_6_), channel_id=1, source_target_pairs={{0,8},{8,16},{16,24},{24,28},{28,20},{20,12},{12,4},{4,0},{1,9},{9... | collective-permute-start | bytes 786440 | tf_op jit(solution)/shard_map/ppermute | solution.py:453
  83.5 2.3 collective-permute-start.11
  86.4 2.5 %collective-permute-done.24.refs_10_.refs_7_ = bf16[64,16,128]{2,1,0:T(8,128)(2,1)} collective-permute-done((bf16[64,16,128]{2,1,0:T(8,128)(2,1)}, bf16[64,16,128]{2,1,0:T(8,128)(2,1)}, u32[]{:S(2)}, u32[]{:S(2)}) %collective-permute-start.24) | collective-permute-done | bytes 262176 | tf_op jit(solution)/shard_map/ppermute | solution.py:453
  88.9 2.6 %collective-permute-start.25 = (bf16[64,16,128]{2,1,0:T(8,128)(2,1)}, bf16[64,16,128]{2,1,0:T(8,128)(2,1)}, u32[]{:S(2)}, u32[]{:S(2)}) collective-permute-start(bf16[64,16,128]{2,1,0:T(8,128)(2,1)} %collective-permute-done.24.refs_10_.refs_7_), channel_id=1, source_target_pairs={{0,8},{8,16},{16,24},{24,28},{28,20},{20,12},{12,4},{4,0},{1,9},{9... | collective-permute-start | bytes 786440 | tf_op jit(solution)/shard_map/ppermute | solution.py:453
  92.0 2.8 %copy.39 = bf16[2,64,4096]{1,2,0:T(8,128)(2,1)} copy(bf16[2,64,4096]{2,1,0:T(8,128)(2,1)} %collective-permute-done.8) | data formatting | bytes 2097152 | tf_op jit(solution)/shard_map/ppermute | solution.py:299
  94.8 4.1 %pad_maximum_fusion = bf16[2,128,4096]{1,2,0:T(8,128)(2,1)S(1)} fusion(bf16[2,64,4096]{1,2,0:T(8,128)(2,1)} %copy.39, bf16[2,32,4096]{1,2,0:T(8,128)(2,1)} %copy.38, bf16[2,32,4096]{1,2,0:T(8,128)(2,1)S(1)} %copy.37), kind=kLoop, calls=%fused_computation | loop fusion | flops 6291456 | bytes 4194304 | tf_op jit(solution)/shard_map/concatenate | solution.py:304
  100.2 2.1 collective-permute-start.15
  104.4 5.1 %collective-permute-done.15.refs_12_.refs_9_ = bf16[64,16,128]{2,1,0:T(8,128)(2,1)S(1)} collective-permute-done((bf16[64,16,128]{2,1,0:T(8,128)(2,1)S(1)}, bf16[64,16,128]{2,1,0:T(8,128)(2,1)S(1)}, u32[]{:S(2)}, u32[]{:S(2)}) %collective-permute-start.15) | collective-permute-done | bytes 262176 | tf_op jit(solution)/shard_map/ppermute | solution.py:453
  109.5 2.1 collective-permute-start.16
  111.6 3.6 %collective-permute-done.26.refs_12_.refs_9_ = bf16[64,16,128]{2,1,0:T(8,128)(2,1)} collective-permute-done((bf16[64,16,128]{2,1,0:T(8,128)(2,1)}, bf16[64,16,128]{2,1,0:T(8,128)(2,1)}, u32[]{:S(2)}, u32[]{:S(2)}) %collective-permute-start.26) | collective-permute-done | bytes 262176 | tf_op jit(solution)/shard_map/ppermute | solution.py:453
  115.2 2.1 collective-permute-start.27
  117.3 3.5 %collective-permute-done.16.refs_13_.refs_10_ = bf16[64,16,128]{2,1,0:T(8,128)(2,1)} collective-permute-done((bf16[64,16,128]{2,1,0:T(8,128)(2,1)S(1)}, bf16[64,16,128]{2,1,0:T(8,128)(2,1)}, u32[]{:S(2)}, u32[]{:S(2)}) %collective-permute-start.16) | collective-permute-done | bytes 262176 | tf_op jit(solution)/shard_map/ppermute | solution.py:453
  120.8 2.1 collective-permute-start.17
  124.3 2.1 collective-permute-done.27.refs_13_.refs_10_
  126.5 2.1 collective-permute-start.28
  128.5 3.5 %collective-permute-done.17.refs_14_.refs_11_ = bf16[64,16,128]{2,1,0:T(8,128)(2,1)} collective-permute-done((bf16[64,16,128]{2,1,0:T(8,128)(2,1)}, bf16[64,16,128]{2,1,0:T(8,128)(2,1)}, u32[]{:S(2)}, u32[]{:S(2)}) %collective-permute-start.17) | collective-permute-done | bytes 262176 | tf_op jit(solution)/shard_map/ppermute | solution.py:453
  132.1 2.1 collective-permute-start.18
  137.7 2.1 collective-permute-start.29
  139.8 3.5 %collective-permute-done.18.refs_15_.refs_12_ = bf16[64,16,128]{2,1,0:T(8,128)(2,1)} collective-permute-done((bf16[64,16,128]{2,1,0:T(8,128)(2,1)}, bf16[64,16,128]{2,1,0:T(8,128)(2,1)}, u32[]{:S(2)}, u32[]{:S(2)}) %collective-permute-start.18) | collective-permute-done | bytes 262176 | tf_op jit(solution)/shard_map/ppermute | solution.py:453
  143.3 2.1 collective-permute-done.22.refs_23_.refs_20_
  145.4 10.3 %shard_map.104 = (bf16[32,128,128]{2,1,0:T(8,128)(2,1)}, f32[32,128,128]{2,1,0:T(8,128)}, bf16[8,16,128,128]{3,2,1,0:T(8,128)(2,1)}) custom-call(s32[8]{0:T(128)} %get-tuple-element.94.refs_0_, s32[128]{0:T(128)} %get-tuple-element.103.refs_1_.refs_3_.refs_0_, s32[128]{0:T(128)} %get-tuple-element.100.refs_2_.refs_4_.refs_1_, ...), custom_call_target="tpu_custom_call" | custom-call | flops 17179869184 | bytes 13631488 | tf_op jit(solution)/shard_map/pallas_call | solution.py:140
  156.8 2.1 collective-permute-start.53
  159.7 9.8 %shard_map.106 = (bf16[32,128,128]{2,1,0:T(8,128)(2,1)}, bf16[8,16,128,128]{3,2,1,0:T(8,128)(2,1)}) custom-call(s32[8]{0:T(128)} %get-tuple-element.94.refs_0_, s32[128]{0:T(128)} %get-tuple-element.104.refs_3_.refs_1_.refs_0_, s32[128]{0:T(128)} %get-tuple-element.99.refs_4_.refs_2_.refs_1_, s32[128]{0:T(128)} %get-tuple-element.103.refs_1_.refs_3_.refs_0_, ...), custom_call_target="tpu_custom_call" | custom-call | flops 17179869184 | bytes 13631488 | tf_op jit(solution)/shard_map/pallas_call | solution.py:140
  170.6 2.1 collective-permute-start.37
  172.9 2.1 collective-permute-start.55
  175.0 3.9 %collective-permute-done.37 = bf16[16,64,128]{2,1,0:T(8,128)(2,1)S(1)} collective-permute-done((bf16[16,64,128]{2,1,0:T(8,128)(2,1)S(1)}, bf16[16,64,128]{2,1,0:T(8,128)(2,1)S(1)}, u32[]{:S(2)}, u32[]{:S(2)}) %collective-permute-start.37) | collective-permute-done | bytes 262176 | tf_op jit(solution)/shard_map/ppermute | solution.py:335
  178.9 2.7 %collective-permute-done.38 = bf16[16,64,128]{2,1,0:T(8,128)(2,1)S(1)} collective-permute-done((bf16[16,64,128]{2,1,0:T(8,128)(2,1)S(1)}, bf16[16,64,128]{2,1,0:T(8,128)(2,1)S(1)}, u32[]{:S(2)}, u32[]{:S(2)}) %collective-permute-start.38) | collective-permute-done | bytes 262176 | tf_op jit(solution)/shard_map/ppermute | solution.py:335
  184.9 6.3 %shard_map.107 = bf16[128,4096]{1,0:T(8,128)(2,1)} custom-call(s32[128]{0:T(128)} %get-tuple-element.104.refs_3_.refs_1_.refs_0_, s32[128]{0:T(128)} %get-tuple-element.99.refs_4_.refs_2_.refs_1_, s32[8]{0:T(128)} %get-tuple-element.96.refs_5_.refs_2_, s32[8]{0:T(128)} %get-tuple-element.95.refs_6_.refs_3_, bf16[32,128,128]{2,1,0:T(8,128)(2,1)} %get-tuple-element.46.refs_4_, ...), custom_call_target="tpu_custom_call" | custom-call | flops 8589934592 | bytes 6291456 | tf_op jit(solution)/shard_map/pallas_call | solution.py:140
  196.8 7.9 %shard_map.108 = bf16[128,4096]{1,0:T(8,128)(2,1)} custom-call(s32[128]{0:T(128)} %get-tuple-element.103.refs_1_.refs_3_.refs_0_, s32[128]{0:T(128)} %get-tuple-element.100.refs_2_.refs_4_.refs_1_, s32[8]{0:T(128)} %get-tuple-element.96.refs_5_.refs_2_, s32[8]{0:T(128)} %get-tuple-element.95.refs_6_.refs_3_, ...), custom_call_target="tpu_custom_call" | custom-call | flops 8589934592 | bytes 6291456 | tf_op jit(solution)/shard_map/pallas_call | solution.py:140
  213.9 3.7 %collective-permute-done.44 = bf16[16,64,128]{2,1,0:T(8,128)(2,1)S(1)} collective-permute-done((bf16[16,64,128]{2,1,0:T(8,128)(2,1)S(1)}, bf16[16,64,128]{2,1,0:T(8,128)(2,1)S(1)}, u32[]{:S(2)}, u32[]{:S(2)}) %collective-permute-start.44) | collective-permute-done | bytes 262176 | tf_op jit(solution)/shard_map/ppermute | solution.py:335
  220.1 3.0 %collective-permute-done.58 = bf16[16,64,128]{2,1,0:T(8,128)(2,1)S(1)} collective-permute-done((bf16[16,64,128]{2,1,0:T(8,128)(2,1)S(1)}, bf16[16,64,128]{2,1,0:T(8,128)(2,1)S(1)}, u32[]{:S(2)}, u32[]{:S(2)}) %collective-permute-start.58) | collective-permute-done | bytes 262176 | tf_op jit(solution)/shard_map/ppermute | solution.py:335
  225.8 3.0 %collective-permute-done.45 = bf16[16,64,128]{2,1,0:T(8,128)(2,1)S(1)} collective-permute-done((bf16[16,64,128]{2,1,0:T(8,128)(2,1)S(1)}, bf16[16,64,128]{2,1,0:T(8,128)(2,1)S(1)}, u32[]{:S(2)}, u32[]{:S(2)}) %collective-permute-start.45) | collective-permute-done | bytes 262176 | tf_op jit(solution)/shard_map/ppermute | solution.py:335
  231.4 3.0 %collective-permute-done.59 = bf16[16,64,128]{2,1,0:T(8,128)(2,1)S(1)} collective-permute-done((bf16[16,64,128]{2,1,0:T(8,128)(2,1)S(1)}, bf16[16,64,128]{2,1,0:T(8,128)(2,1)S(1)}, u32[]{:S(2)}, u32[]{:S(2)}) %collective-permute-start.59) | collective-permute-done | bytes 262176 | tf_op jit(solution)/shard_map/ppermute | solution.py:335
  242.6 3.0 %collective-permute-done.60 = bf16[16,64,128]{2,1,0:T(8,128)(2,1)S(1)} collective-permute-done((bf16[16,64,128]{2,1,0:T(8,128)(2,1)S(1)}, bf16[16,64,128]{2,1,0:T(8,128)(2,1)S(1)}, u32[]{:S(2)}, u32[]{:S(2)}) %collective-permute-start.60) | collective-permute-done | bytes 262176 | tf_op jit(solution)/shard_map/ppermute | solution.py:335
  247.2 3.7 %collective-permute-done.47 = bf16[16,64,128]{2,1,0:T(8,128)(2,1)S(1)} collective-permute-done((bf16[16,64,128]{2,1,0:T(8,128)(2,1)S(1)}, bf16[16,64,128]{2,1,0:T(8,128)(2,1)S(1)}, u32[]{:S(2)}, u32[]{:S(2)}) %collective-permute-start.47) | collective-permute-done | bytes 262176 | tf_op jit(solution)/shard_map/ppermute | solution.py:335
  (191 shorter events, 64.9 us)
Async XLA Ops:
  8.0 20.0 %collective-permute-start.1 = (bf16[65,16,128]{2,1,0:T(8,128)(2,1)}, bf16[65,16,128]{2,1,0:T(8,128)(2,1)S(1)}, u32[]{:S(2)}, u32[]{:S(2)}) collective-permute-start(bf16[65,16,128]{2,1,0:T(8,128)(2,1)} %get-tuple-element.30), channel_id=1, source_target_pairs={{0,8},{4,12},{8,0},{12,4},{16,24},{20,28},{24,16},{28,20},{1,9},{5... | collective-permute-start | bytes 798728 | tf_op jit(solution)/shard_map/ppermute | solution.py:447
  9.5 21.8 %collective-permute-start.2 = (bf16[65,16,128]{2,1,0:T(8,128)(2,1)}, bf16[65,16,128]{2,1,0:T(8,128)(2,1)S(1)}, u32[]{:S(2)}, u32[]{:S(2)}) collective-permute-start(bf16[65,16,128]{2,1,0:T(8,128)(2,1)} %get-tuple-element.31), channel_id=1, source_target_pairs={{0,12},{4,8},{8,4},{12,0},{16,28},{20,24},{24,20},{28,16},{1,13},{... | collective-permute-start | bytes 798728 | tf_op jit(solution)/shard_map/ppermute | solution.py:447
  9.5 23.5 %collective-permute-start.3 = (bf16[65,16,128]{2,1,0:T(8,128)(2,1)}, bf16[65,16,128]{2,1,0:T(8,128)(2,1)S(1)}, u32[]{:S(2)}, u32[]{:S(2)}) collective-permute-start(bf16[65,16,128]{2,1,0:T(8,128)(2,1)} %get-tuple-element.32), channel_id=1, source_target_pairs={{0,16},{4,20},{8,24},{12,28},{16,0},{20,4},{24,8},{28,12},{1,17},{... | collective-permute-start | bytes 798728 | tf_op jit(solution)/shard_map/ppermute | solution.py:447
  12.5 37.3 %collective-permute-start.4 = (bf16[65,16,128]{2,1,0:T(8,128)(2,1)}, bf16[65,16,128]{2,1,0:T(8,128)(2,1)S(1)}, u32[]{:S(2)}, u32[]{:S(2)}) collective-permute-start(bf16[65,16,128]{2,1,0:T(8,128)(2,1)} %get-tuple-element.33), channel_id=1, source_target_pairs={{0,20},{4,16},{8,28},{12,24},{16,4},{20,0},{24,12},{28,8},{1,21},{... | collective-permute-start | bytes 798728 | tf_op jit(solution)/shard_map/ppermute | solution.py:447
  14.6 35.2 %collective-permute-start.5 = (bf16[65,16,128]{2,1,0:T(8,128)(2,1)}, bf16[65,16,128]{2,1,0:T(8,128)(2,1)S(1)}, u32[]{:S(2)}, u32[]{:S(2)}) collective-permute-start(bf16[65,16,128]{2,1,0:T(8,128)(2,1)} %get-tuple-element.34), channel_id=1, source_target_pairs={{0,24},{4,28},{8,16},{12,20},{16,8},{20,12},{24,0},{28,4},{1,25},{... | collective-permute-start | bytes 798728 | tf_op jit(solution)/shard_map/ppermute | solution.py:447
  27.9 22.0 %collective-permute-start.6 = (bf16[65,16,128]{2,1,0:T(8,128)(2,1)}, bf16[65,16,128]{2,1,0:T(8,128)(2,1)S(1)}, u32[]{:S(2)}, u32[]{:S(2)}) collective-permute-start(bf16[65,16,128]{2,1,0:T(8,128)(2,1)} %get-tuple-element.35), channel_id=1, source_target_pairs={{0,28},{4,24},{8,20},{12,16},{16,12},{20,8},{24,4},{28,0},{1,29},{... | collective-permute-start | bytes 798728 | tf_op jit(solution)/shard_map/ppermute | solution.py:447
  31.3 18.6 %collective-permute-start.7 = (bf16[2,32,4096]{2,1,0:T(8,128)(2,1)S(1)}, bf16[2,32,4096]{2,1,0:T(8,128)(2,1)S(1)}, u32[]{:S(2)}, u32[]{:S(2)}) collective-permute-start(bf16[2,32,4096]{2,1,0:T(8,128)(2,1)S(1)} %pad_maximum_fusion.3), channel_id=1, source_target_pairs={{0,2},{1,3},{2,0},{3,1},{4,6},{5,7},{6,4},{7,5},{8,10},{9,11},{10,... | collective-permute-start | bytes 1572872 | tf_op jit(solution)/shard_map/ppermute | solution.py:299
  51.1 40.9 %collective-permute-start.8 = (bf16[2,64,4096]{2,1,0:T(8,128)(2,1)}, bf16[2,64,4096]{2,1,0:T(8,128)(2,1)}, u32[]{:S(2)}, u32[]{:S(2)}) collective-permute-start(bf16[2,64,4096]{2,1,0:T(8,128)(2,1)} %pad_maximum_fusion.2), channel_id=1, source_target_pairs={{0,1},{1,0},{2,3},{3,2},{4,5},{5,4},{6,7},{7,6},{8,9},{9,8},{10,11... | collective-permute-start | bytes 3145736 | tf_op jit(solution)/shard_map/ppermute | solution.py:299
  55.1 16.6 %collective-permute-start.9 = (bf16[64,16,128]{2,1,0:T(8,128)(2,1)}, bf16[64,16,128]{2,1,0:T(8,128)(2,1)S(1)}, u32[]{:S(2)}, u32[]{:S(2)}) collective-permute-start(bf16[64,16,128]{2,1,0:T(8,128)(2,1)} %get-tuple-element.37.refs_8_.refs_5_), channel_id=1, source_target_pairs={{0,8},{8,16},{16,24},{24,28},{28,20},{20,12},{12,4},{4,0},{1,9},{9... | collective-permute-start | bytes 786440 | tf_op jit(solution)/shard_map/ppermute | solution.py:453
  71.7 11.8 %collective-permute-start.10 = (bf16[64,16,128]{2,1,0:T(8,128)(2,1)S(1)}, bf16[64,16,128]{2,1,0:T(8,128)(2,1)}, u32[]{:S(2)}, u32[]{:S(2)}) collective-permute-start(bf16[64,16,128]{2,1,0:T(8,128)(2,1)S(1)} %collective-permute-done.9.refs_9_.refs_6_), channel_id=1, source_target_pairs={{0,8},{8,16},{16,24},{24,28},{28,20},{20,12},{12,4},{4,0},{1,9},{9... | collective-permute-start | bytes 786440 | tf_op jit(solution)/shard_map/ppermute | solution.py:453
  75.1 11.2 %collective-permute-start.13 = (bf16[64,16,128]{2,1,0:T(8,128)(2,1)}, bf16[64,16,128]{2,1,0:T(8,128)(2,1)}, u32[]{:S(2)}, u32[]{:S(2)}) collective-permute-start(bf16[64,16,128]{2,1,0:T(8,128)(2,1)} %collective-permute-done.12.refs_17_.refs_14_), channel_id=1, source_target_pairs={{8,0},{16,8},{24,16},{28,24},{20,28},{12,20},{4,12},{0,4},{9,1},{1... | collective-permute-start | bytes 786440 | tf_op jit(solution)/shard_map/ppermute | solution.py:453
  77.7 11.2 %collective-permute-start.24 = (bf16[64,16,128]{2,1,0:T(8,128)(2,1)}, bf16[64,16,128]{2,1,0:T(8,128)(2,1)}, u32[]{:S(2)}, u32[]{:S(2)}) collective-permute-start(bf16[64,16,128]{2,1,0:T(8,128)(2,1)} %collective-permute-done.23.refs_9_.refs_6_), channel_id=1, source_target_pairs={{0,8},{8,16},{16,24},{24,28},{28,20},{20,12},{12,4},{4,0},{1,9},{9... | collective-permute-start | bytes 786440 | tf_op jit(solution)/shard_map/ppermute | solution.py:453
  80.7 11.2 %collective-permute-start.31 = (bf16[64,16,128]{2,1,0:T(8,128)(2,1)}, bf16[64,16,128]{2,1,0:T(8,128)(2,1)}, u32[]{:S(2)}, u32[]{:S(2)}) collective-permute-start(bf16[64,16,128]{2,1,0:T(8,128)(2,1)} %collective-permute-done.30.refs_17_.refs_14_), channel_id=1, source_target_pairs={{8,0},{16,8},{24,16},{28,24},{20,28},{12,20},{4,12},{0,4},{9,1},{1... | collective-permute-start | bytes 786440 | tf_op jit(solution)/shard_map/ppermute | solution.py:453
  83.5 16.7 %collective-permute-start.11 = (bf16[64,16,128]{2,1,0:T(8,128)(2,1)}, bf16[64,16,128]{2,1,0:T(8,128)(2,1)S(1)}, u32[]{:S(2)}, u32[]{:S(2)}) collective-permute-start(bf16[64,16,128]{2,1,0:T(8,128)(2,1)} %collective-permute-done.10.refs_10_.refs_7_), channel_id=1, source_target_pairs={{0,8},{8,16},{16,24},{24,28},{28,20},{20,12},{12,4},{4,0},{1,9},{9... | collective-permute-start | bytes 786440 | tf_op jit(solution)/shard_map/ppermute | solution.py:453
  86.4 13.8 %collective-permute-start.14 = (bf16[64,16,128]{2,1,0:T(8,128)(2,1)}, bf16[64,16,128]{2,1,0:T(8,128)(2,1)S(1)}, u32[]{:S(2)}, u32[]{:S(2)}) collective-permute-start(bf16[64,16,128]{2,1,0:T(8,128)(2,1)} %collective-permute-done.13.refs_18_.refs_15_), channel_id=1, source_target_pairs={{8,0},{16,8},{24,16},{28,24},{20,28},{12,20},{4,12},{0,4},{9,1},{1... | collective-permute-start | bytes 786440 | tf_op jit(solution)/shard_map/ppermute | solution.py:453
  88.9 13.4 %collective-permute-start.25 = (bf16[64,16,128]{2,1,0:T(8,128)(2,1)}, bf16[64,16,128]{2,1,0:T(8,128)(2,1)}, u32[]{:S(2)}, u32[]{:S(2)}) collective-permute-start(bf16[64,16,128]{2,1,0:T(8,128)(2,1)} %collective-permute-done.24.refs_10_.refs_7_), channel_id=1, source_target_pairs={{0,8},{8,16},{16,24},{24,28},{28,20},{20,12},{12,4},{4,0},{1,9},{9... | collective-permute-start | bytes 786440 | tf_op jit(solution)/shard_map/ppermute | solution.py:453
  92.0 12.4 %collective-permute-start.32 = (bf16[64,16,128]{2,1,0:T(8,128)(2,1)}, bf16[64,16,128]{2,1,0:T(8,128)(2,1)}, u32[]{:S(2)}, u32[]{:S(2)}) collective-permute-start(bf16[64,16,128]{2,1,0:T(8,128)(2,1)} %collective-permute-done.31.refs_18_.refs_15_), channel_id=1, source_target_pairs={{8,0},{16,8},{24,16},{28,24},{20,28},{12,20},{4,12},{0,4},{9,1},{1... | collective-permute-start | bytes 786440 | tf_op jit(solution)/shard_map/ppermute | solution.py:453
  102.3 12.9 %collective-permute-start.26 = (bf16[64,16,128]{2,1,0:T(8,128)(2,1)}, bf16[64,16,128]{2,1,0:T(8,128)(2,1)}, u32[]{:S(2)}, u32[]{:S(2)}) collective-permute-start(bf16[64,16,128]{2,1,0:T(8,128)(2,1)} %collective-permute-done.25.refs_11_.refs_8_), channel_id=1, source_target_pairs={{0,8},{8,16},{16,24},{24,28},{28,20},{20,12},{12,4},{4,0},{1,9},{9... | collective-permute-start | bytes 786440 | tf_op jit(solution)/shard_map/ppermute | solution.py:453
  104.4 12.9 %collective-permute-start.33 = (bf16[64,16,128]{2,1,0:T(8,128)(2,1)}, bf16[64,16,128]{2,1,0:T(8,128)(2,1)}, u32[]{:S(2)}, u32[]{:S(2)}) collective-permute-start(bf16[64,16,128]{2,1,0:T(8,128)(2,1)} %collective-permute-done.32.refs_19_.refs_16_), channel_id=1, source_target_pairs={{8,0},{16,8},{24,16},{28,24},{20,28},{12,20},{4,12},{0,4},{9,1},{1... | collective-permute-start | bytes 786440 | tf_op jit(solution)/shard_map/ppermute | solution.py:453
  109.5 11.3 %collective-permute-start.16 = (bf16[64,16,128]{2,1,0:T(8,128)(2,1)S(1)}, bf16[64,16,128]{2,1,0:T(8,128)(2,1)}, u32[]{:S(2)}, u32[]{:S(2)}) collective-permute-start(bf16[64,16,128]{2,1,0:T(8,128)(2,1)S(1)} %collective-permute-done.15.refs_12_.refs_9_), channel_id=1, source_target_pairs={{0,8},{8,16},{16,24},{24,28},{28,20},{20,12},{12,4},{4,0},{1,9},{9... | collective-permute-start | bytes 786440 | tf_op jit(solution)/shard_map/ppermute | solution.py:453
  111.6 11.3 %collective-permute-start.20 = (bf16[64,16,128]{2,1,0:T(8,128)(2,1)S(1)}, bf16[64,16,128]{2,1,0:T(8,128)(2,1)}, u32[]{:S(2)}, u32[]{:S(2)}) collective-permute-start(bf16[64,16,128]{2,1,0:T(8,128)(2,1)S(1)} %collective-permute-done.19.refs_20_.refs_17_), channel_id=1, source_target_pairs={{8,0},{16,8},{24,16},{28,24},{20,28},{12,20},{4,12},{0,4},{9,1},{1... | collective-permute-start | bytes 786440 | tf_op jit(solution)/shard_map/ppermute | solution.py:453
  115.2 11.2 %collective-permute-start.27 = (bf16[64,16,128]{2,1,0:T(8,128)(2,1)}, bf16[64,16,128]{2,1,0:T(8,128)(2,1)}, u32[]{:S(2)}, u32[]{:S(2)}) collective-permute-start(bf16[64,16,128]{2,1,0:T(8,128)(2,1)} %collective-permute-done.26.refs_12_.refs_9_), channel_id=1, source_target_pairs={{0,8},{8,16},{16,24},{24,28},{28,20},{20,12},{12,4},{4,0},{1,9},{9... | collective-permute-start | bytes 786440 | tf_op jit(solution)/shard_map/ppermute | solution.py:453
  117.3 11.2 %collective-permute-start.34 = (bf16[64,16,128]{2,1,0:T(8,128)(2,1)}, bf16[64,16,128]{2,1,0:T(8,128)(2,1)}, u32[]{:S(2)}, u32[]{:S(2)}) collective-permute-start(bf16[64,16,128]{2,1,0:T(8,128)(2,1)} %collective-permute-done.33.refs_20_.refs_17_), channel_id=1, source_target_pairs={{8,0},{16,8},{24,16},{28,24},{20,28},{12,20},{4,12},{0,4},{9,1},{1... | collective-permute-start | bytes 786440 | tf_op jit(solution)/shard_map/ppermute | solution.py:453
  120.8 11.2 %collective-permute-start.17 = (bf16[64,16,128]{2,1,0:T(8,128)(2,1)}, bf16[64,16,128]{2,1,0:T(8,128)(2,1)}, u32[]{:S(2)}, u32[]{:S(2)}) collective-permute-start(bf16[64,16,128]{2,1,0:T(8,128)(2,1)} %collective-permute-done.16.refs_13_.refs_10_), channel_id=1, source_target_pairs={{0,8},{8,16},{16,24},{24,28},{28,20},{20,12},{12,4},{4,0},{1,9},{9... | collective-permute-start | bytes 786440 | tf_op jit(solution)/shard_map/ppermute | solution.py:453
  122.9 11.2 %collective-permute-start.21 = (bf16[64,16,128]{2,1,0:T(8,128)(2,1)}, bf16[64,16,128]{2,1,0:T(8,128)(2,1)}, u32[]{:S(2)}, u32[]{:S(2)}) collective-permute-start(bf16[64,16,128]{2,1,0:T(8,128)(2,1)} %collective-permute-done.20.refs_21_.refs_18_), channel_id=1, source_target_pairs={{8,0},{16,8},{24,16},{28,24},{20,28},{12,20},{4,12},{0,4},{9,1},{1... | collective-permute-start | bytes 786440 | tf_op jit(solution)/shard_map/ppermute | solution.py:453
  126.5 11.2 %collective-permute-start.28 = (bf16[64,16,128]{2,1,0:T(8,128)(2,1)}, bf16[64,16,128]{2,1,0:T(8,128)(2,1)}, u32[]{:S(2)}, u32[]{:S(2)}) collective-permute-start(bf16[64,16,128]{2,1,0:T(8,128)(2,1)} %collective-permute-done.27.refs_13_.refs_10_), channel_id=1, source_target_pairs={{0,8},{8,16},{16,24},{24,28},{28,20},{20,12},{12,4},{4,0},{1,9},{9... | collective-permute-start | bytes 786440 | tf_op jit(solution)/shard_map/ppermute | solution.py:453
  128.5 11.2 %collective-permute-start.35 = (bf16[64,16,128]{2,1,0:T(8,128)(2,1)}, bf16[64,16,128]{2,1,0:T(8,128)(2,1)}, u32[]{:S(2)}, u32[]{:S(2)}) collective-permute-start(bf16[64,16,128]{2,1,0:T(8,128)(2,1)} %collective-permute-done.34.refs_21_.refs_18_), channel_id=1, source_target_pairs={{8,0},{16,8},{24,16},{28,24},{20,28},{12,20},{4,12},{0,4},{9,1},{1... | collective-permute-start | bytes 786440 | tf_op jit(solution)/shard_map/ppermute | solution.py:453
  132.1 11.2 %collective-permute-start.18 = (bf16[64,16,128]{2,1,0:T(8,128)(2,1)}, bf16[64,16,128]{2,1,0:T(8,128)(2,1)}, u32[]{:S(2)}, u32[]{:S(2)}) collective-permute-start(bf16[64,16,128]{2,1,0:T(8,128)(2,1)} %collective-permute-done.17.refs_14_.refs_11_), channel_id=1, source_target_pairs={{0,8},{8,16},{16,24},{24,28},{28,20},{20,12},{12,4},{4,0},{1,9},{9... | collective-permute-start | bytes 786440 | tf_op jit(solution)/shard_map/ppermute | solution.py:453
  134.2 11.2 %collective-permute-start.22 = (bf16[64,16,128]{2,1,0:T(8,128)(2,1)}, bf16[64,16,128]{2,1,0:T(8,128)(2,1)}, u32[]{:S(2)}, u32[]{:S(2)}) collective-permute-start(bf16[64,16,128]{2,1,0:T(8,128)(2,1)} %collective-permute-done.21.refs_22_.refs_19_), channel_id=1, source_target_pairs={{8,0},{16,8},{24,16},{28,24},{20,28},{12,20},{4,12},{0,4},{9,1},{1... | collective-permute-start | bytes 786440 | tf_op jit(solution)/shard_map/ppermute | solution.py:453
  137.7 21.2 %collective-permute-start.29 = (bf16[64,16,128]{2,1,0:T(8,128)(2,1)}, bf16[64,16,128]{2,1,0:T(8,128)(2,1)S(1)}, u32[]{:S(2)}, u32[]{:S(2)}) collective-permute-start(bf16[64,16,128]{2,1,0:T(8,128)(2,1)} %collective-permute-done.28.refs_14_.refs_11_), channel_id=1, source_target_pairs={{0,8},{8,16},{16,24},{24,28},{28,20},{20,12},{12,4},{4,0},{1,9},{9... | collective-permute-start | bytes 786440 | tf_op jit(solution)/shard_map/ppermute | solution.py:453
  139.8 19.1 %collective-permute-start.36 = (bf16[64,16,128]{2,1,0:T(8,128)(2,1)}, bf16[64,16,128]{2,1,0:T(8,128)(2,1)S(1)}, u32[]{:S(2)}, u32[]{:S(2)}) collective-permute-start(bf16[64,16,128]{2,1,0:T(8,128)(2,1)} %collective-permute-done.35.refs_22_.refs_19_), channel_id=1, source_target_pairs={{8,0},{16,8},{24,16},{28,24},{20,28},{12,20},{4,12},{0,4},{9,1},{1... | collective-permute-start | bytes 786440 | tf_op jit(solution)/shard_map/ppermute | solution.py:453
  156.8 15.9 %collective-permute-start.53 = (bf16[16,64,128]{2,1,0:T(8,128)(2,1)S(1)}, bf16[16,64,128]{2,1,0:T(8,128)(2,1)S(1)}, u32[]{:S(2)}, u32[]{:S(2)}) collective-permute-start(bf16[16,64,128]{2,1,0:T(8,128)(2,1)S(1)} %get-tuple-element.69), channel_id=1, source_target_pairs={{0,8},{8,16},{16,24},{24,28},{28,20},{20,12},{12,4},{4,0},{1,9},{9... | collective-permute-start | bytes 786440 | tf_op jit(solution)/shard_map/ppermute | solution.py:335
  158.9 13.8 %collective-permute-start.54 = (bf16[16,64,128]{2,1,0:T(8,128)(2,1)S(1)}, bf16[16,64,128]{2,1,0:T(8,128)(2,1)S(1)}, u32[]{:S(2)}, u32[]{:S(2)}) collective-permute-start(bf16[16,64,128]{2,1,0:T(8,128)(2,1)S(1)} %get-tuple-element.68), channel_id=1, source_target_pairs={{8,0},{16,8},{24,16},{28,24},{20,28},{12,20},{4,12},{0,4},{9,1},{1... | collective-permute-start | bytes 786440 | tf_op jit(solution)/shard_map/ppermute | solution.py:335
  172.9 18.3 %collective-permute-start.55 = (bf16[16,64,128]{2,1,0:T(8,128)(2,1)S(1)}, bf16[16,64,128]{2,1,0:T(8,128)(2,1)S(1)}, u32[]{:S(2)}, u32[]{:S(2)}) collective-permute-start(bf16[16,64,128]{2,1,0:T(8,128)(2,1)S(1)} %get-tuple-element.66), channel_id=1, source_target_pairs={{0,8},{8,16},{16,24},{24,28},{28,20},{20,12},{12,4},{4,0},{1,9},{9... | collective-permute-start | bytes 786440 | tf_op jit(solution)/shard_map/ppermute | solution.py:335
  175.0 16.2 %collective-permute-start.61 = (bf16[16,64,128]{2,1,0:T(8,128)(2,1)S(1)}, bf16[16,64,128]{2,1,0:T(8,128)(2,1)S(1)}, u32[]{:S(2)}, u32[]{:S(2)}) collective-permute-start(bf16[16,64,128]{2,1,0:T(8,128)(2,1)S(1)} %get-tuple-element.67), channel_id=1, source_target_pairs={{8,0},{16,8},{24,16},{28,24},{20,28},{12,20},{4,12},{0,4},{9,1},{1... | collective-permute-start | bytes 786440 | tf_op jit(solution)/shard_map/ppermute | solution.py:335
  182.8 10.7 %collective-permute-start.39 = (bf16[16,64,128]{2,1,0:T(8,128)(2,1)S(1)}, bf16[16,64,128]{2,1,0:T(8,128)(2,1)S(1)}, u32[]{:S(2)}, u32[]{:S(2)}) collective-permute-start(bf16[16,64,128]{2,1,0:T(8,128)(2,1)S(1)} %get-tuple-element.83), channel_id=1, source_target_pairs={{0,8},{8,16},{16,24},{24,28},{28,20},{20,12},{12,4},{4,0},{1,9},{9... | collective-permute-start | bytes 786440 | tf_op jit(solution)/shard_map/ppermute | solution.py:335
  191.4 13.3 %collective-permute-start.56 = (bf16[16,64,128]{2,1,0:T(8,128)(2,1)S(1)}, bf16[16,64,128]{2,1,0:T(8,128)(2,1)S(1)}, u32[]{:S(2)}, u32[]{:S(2)}) collective-permute-start(bf16[16,64,128]{2,1,0:T(8,128)(2,1)S(1)} %get-tuple-element.64), channel_id=1, source_target_pairs={{0,8},{8,16},{16,24},{24,28},{28,20},{20,12},{12,4},{4,0},{1,9},{9... | collective-permute-start | bytes 786440 | tf_op jit(solution)/shard_map/ppermute | solution.py:335
  191.5 13.2 %collective-permute-start.62 = (bf16[16,64,128]{2,1,0:T(8,128)(2,1)S(1)}, bf16[16,64,128]{2,1,0:T(8,128)(2,1)S(1)}, u32[]{:S(2)}, u32[]{:S(2)}) collective-permute-start(bf16[16,64,128]{2,1,0:T(8,128)(2,1)S(1)} %get-tuple-element.65), channel_id=1, source_target_pairs={{8,0},{16,8},{24,16},{28,24},{20,28},{12,20},{4,12},{0,4},{9,1},{1... | collective-permute-start | bytes 786440 | tf_op jit(solution)/shard_map/ppermute | solution.py:335
  194.7 13.5 %collective-permute-start.43 = (bf16[16,64,128]{2,1,0:T(8,128)(2,1)S(1)}, bf16[16,64,128]{2,1,0:T(8,128)(2,1)S(1)}, u32[]{:S(2)}, u32[]{:S(2)}) collective-permute-start(bf16[16,64,128]{2,1,0:T(8,128)(2,1)S(1)} %get-tuple-element.81), channel_id=1, source_target_pairs={{0,8},{8,16},{16,24},{24,28},{28,20},{20,12},{12,4},{4,0},{1,9},{9... | collective-permute-start | bytes 786440 | tf_op jit(solution)/shard_map/ppermute | solution.py:335
  194.8 13.4 %collective-permute-start.48 = (bf16[16,64,128]{2,1,0:T(8,128)(2,1)S(1)}, bf16[16,64,128]{2,1,0:T(8,128)(2,1)S(1)}, u32[]{:S(2)}, u32[]{:S(2)}) collective-permute-start(bf16[16,64,128]{2,1,0:T(8,128)(2,1)S(1)} %get-tuple-element.80), channel_id=1, source_target_pairs={{8,0},{16,8},{24,16},{28,24},{20,28},{12,20},{4,12},{0,4},{9,1},{1... | collective-permute-start | bytes 786440 | tf_op jit(solution)/shard_map/ppermute | solution.py:335
  208.1 28.9 %collective-permute-start.41 = (bf16[2,64,4096]{2,1,0:T(8,128)(2,1)S(1)}, bf16[2,64,4096]{2,1,0:T(8,128)(2,1)S(1)}, u32[]{:S(2)}, u32[]{:S(2)}) collective-permute-start(bf16[2,64,4096]{2,1,0:T(8,128)(2,1)S(1)} %pad_maximum_fusion.1), channel_id=1, source_target_pairs={{0,1},{1,0},{2,3},{3,2},{4,5},{5,4},{6,7},{7,6},{8,9},{9,8},{10,11... | collective-permute-start | bytes 3145736 | tf_op jit(solution)/shard_map/ppermute | solution.py:299
  211.8 11.4 %collective-permute-start.58 = (bf16[16,64,128]{2,1,0:T(8,128)(2,1)S(1)}, bf16[16,64,128]{2,1,0:T(8,128)(2,1)S(1)}, u32[]{:S(2)}, u32[]{:S(2)}) collective-permute-start(bf16[16,64,128]{2,1,0:T(8,128)(2,1)S(1)} %get-tuple-element.60), channel_id=1, source_target_pairs={{0,8},{8,16},{16,24},{24,28},{28,20},{20,12},{12,4},{4,0},{1,9},{9... | collective-permute-start | bytes 786440 | tf_op jit(solution)/shard_map/ppermute | solution.py:335
  212.7 10.8 %collective-permute-start.64 = (bf16[16,64,128]{2,1,0:T(8,128)(2,1)S(1)}, bf16[16,64,128]{2,1,0:T(8,128)(2,1)S(1)}, u32[]{:S(2)}, u32[]{:S(2)}) collective-permute-start(bf16[16,64,128]{2,1,0:T(8,128)(2,1)S(1)} %get-tuple-element.61), channel_id=1, source_target_pairs={{8,0},{16,8},{24,16},{28,24},{20,28},{12,20},{4,12},{0,4},{9,1},{1... | collective-permute-start | bytes 786440 | tf_op jit(solution)/shard_map/ppermute | solution.py:335
  218.0 10.7 %collective-permute-start.45 = (bf16[16,64,128]{2,1,0:T(8,128)(2,1)S(1)}, bf16[16,64,128]{2,1,0:T(8,128)(2,1)S(1)}, u32[]{:S(2)}, u32[]{:S(2)}) collective-permute-start(bf16[16,64,128]{2,1,0:T(8,128)(2,1)S(1)} %get-tuple-element.76), channel_id=1, source_target_pairs={{0,8},{8,16},{16,24},{24,28},{28,20},{20,12},{12,4},{4,0},{1,9},{9... | collective-permute-start | bytes 786440 | tf_op jit(solution)/shard_map/ppermute | solution.py:335
  223.7 10.7 %collective-permute-start.59 = (bf16[16,64,128]{2,1,0:T(8,128)(2,1)S(1)}, bf16[16,64,128]{2,1,0:T(8,128)(2,1)S(1)}, u32[]{:S(2)}, u32[]{:S(2)}) collective-permute-start(bf16[16,64,128]{2,1,0:T(8,128)(2,1)S(1)} %get-tuple-element.58), channel_id=1, source_target_pairs={{0,8},{8,16},{16,24},{24,28},{28,20},{20,12},{12,4},{4,0},{1,9},{9... | collective-permute-start | bytes 786440 | tf_op jit(solution)/shard_map/ppermute | solution.py:335
  229.3 10.7 %collective-permute-start.46 = (bf16[16,64,128]{2,1,0:T(8,128)(2,1)S(1)}, bf16[16,64,128]{2,1,0:T(8,128)(2,1)S(1)}, u32[]{:S(2)}, u32[]{:S(2)}) collective-permute-start(bf16[16,64,128]{2,1,0:T(8,128)(2,1)S(1)} %get-tuple-element.74), channel_id=1, source_target_pairs={{0,8},{8,16},{16,24},{24,28},{28,20},{20,12},{12,4},{4,0},{1,9},{9... | collective-permute-start | bytes 786440 | tf_op jit(solution)/shard_map/ppermute | solution.py:335
  234.9 10.7 %collective-permute-start.60 = (bf16[16,64,128]{2,1,0:T(8,128)(2,1)S(1)}, bf16[16,64,128]{2,1,0:T(8,128)(2,1)S(1)}, u32[]{:S(2)}, u32[]{:S(2)}) collective-permute-start(bf16[16,64,128]{2,1,0:T(8,128)(2,1)S(1)} %get-tuple-element.56), channel_id=1, source_target_pairs={{0,8},{8,16},{16,24},{24,28},{28,20},{20,12},{12,4},{4,0},{1,9},{9... | collective-permute-start | bytes 786440 | tf_op jit(solution)/shard_map/ppermute | solution.py:335
  237.3 14.9 %collective-permute-start.42 = (bf16[2,32,4096]{2,1,0:T(8,128)(2,1)S(1)}, bf16[2,32,4096]{2,1,0:T(8,128)(2,1)S(1)}, u32[]{:S(2)}, u32[]{:S(2)}) collective-permute-start(bf16[2,32,4096]{2,1,0:T(8,128)(2,1)S(1)} %slice.243), channel_id=1, source_target_pairs={{0,2},{1,3},{2,0},{3,1},{4,6},{5,7},{6,4},{7,5},{8,10},{9,11},{10,... | collective-permute-start | bytes 1572872 | tf_op jit(solution)/shard_map/ppermute | solution.py:299
  (39 other events, 501.2 us)

commit v6 on v5

--- a/solution.py
+++ b/solution.py
@@ -11,7 +11,7 @@
 FF = 16384
 BLK = 128
 PACK = 16
-WEIGHT = 16
+WEIGHT = 20
 VMEM_LIMIT = 56 << 20
 
 gelu_root = 0.7978845608028654
@@ -111,7 +111,10 @@
             for item, t, x, held, sems in zip(items, table_refs, array_refs, held_refs, in_sems, strict=True)
         ]
         for copies in fetches:
-            for copy in copies:
+            for copy in copies[: len(copies) // 2 or 1]:
+                copy.start()
+        for copies in fetches:
+            for copy in copies[len(copies) // 2 or 1 :]:
                 copy.start()
 
         def need(*which, part=(0, 1)):
@@ -250,7 +253,7 @@
         )
         return carry
 
-    lax.fori_loop(0, acc.shape[0], body, 0, unroll=4)
+    lax.fori_loop(0, acc.shape[0], body, 0, unroll=8)
     send(0)
     send(1)
     need(2)
@@ -267,7 +270,7 @@
         grad[c] = (acc[c] * slope[c]).astype(jnp.bfloat16)
         return carry
 
-    lax.fori_loop(0, acc.shape[0], body, 0, unroll=4)
+    lax.fori_loop(0, acc.shape[0], body, 0, unroll=8)
     send(0)
     need(3)
     up_terms(owner, up_rows, up_cols, tok_turned, grad, out, lambda q: send(1, q))

time: 254 us -> 253 us (level)
  no operation moved by 1% of the time
where the time goes in v6:
time: 253 us
  waiting for transfers between devices  90.8 us (36%)
  starting transfers between devices  85.7 us (34%)
  Pallas kernels  42.9 us (17%)
  local copies, waits for them, and re-layouts  16.8 us (7%)
  other arithmetic  15.5 us (6%)
    pallas_call x7, Pallas kernels, run(): pl.pallas_call(body, out_shape=list(outs), in_specs=[SMEM_SPEC] * (len(sm...  42.9 us
    ppermute x14, starting transfers between devices, onward(): lax.ppermute(pair[0], 'dp', ahead)  39.6 us
    ppermute x7, waiting for transfers between devices, shards(): lax.ppermute(messages[step], 'dp', [(i, i ^ step) for i in range(devices)])  28.7 us
    ppermute x14, waiting for transfers between devices, onward(): lax.ppermute(pair[0], 'dp', ahead)  27.7 us
    ppermute x14, waiting for transfers between devices, send(): lax.ppermute(a, 'dp', self.ahead)  25.4 us
    ppermute x14, starting transfers between devices, send(): lax.ppermute(b, 'dp', self.behind)  16.2 us
    ppermute x7, starting transfers between devices, shards(): lax.ppermute(messages[step], 'dp', [(i, i ^ step) for i in range(devices)])  13.7 us
    ppermute x14, starting transfers between devices, send(): lax.ppermute(a, 'dp', self.ahead)  12.9 us
  transfers between devices with their start and end apart: 67, of which 35 were waited for; matrix products, arithmetic and copies ran while one was open for 11% of the time, Pallas kernels for 16%

profile of v6, /device:TPU:0, one launch (start us, length us, event | category | flops | bytes accessed | tf_op | source)
XLA Modules:
  0.0 252.8 jit_solution(3596913965618490041)
XLA Ops:
  1.9 3.0 %shard_map.102 = (bf16[65,16,128]{2,1,0:T(8,128)(2,1)}, bf16[65,16,128]{2,1,0:T(8,128)(2,1)}, bf16[65,16,128]{2,1,0:T(8,128)(2,1)}, bf16[65,16,128]{2,1,0:T(8,12...) custom-call(s32[1]{0:T(128)} %bitcast.refs_0_, ...), custom_call_target="tpu_custom_call" | custom-call | bytes 4194304 | tf_op jit(solution)/shard_map/pallas_call | solution.py:143
  5.0 3.0 %collective-permute-start = (bf16[65,16,128]{2,1,0:T(8,128)(2,1)}, bf16[65,16,128]{2,1,0:T(8,128)(2,1)S(1)}, u32[]{:S(2)}, u32[]{:S(2)}) collective-permute-start(bf16[65,16,128]{2,1,0:T(8,128)(2,1)} %get-tuple-element.29), channel_id=1, source_target_pairs={{0,4},{4,0},{8,12},{12,8},{16,20},{20,16},{24,28},{28,24},{1,5},{5... | collective-permute-start | bytes 798728 | tf_op jit(solution)/shard_map/ppermute | solution.py:450
  9.5 3.0 %collective-permute-start.3 = (bf16[65,16,128]{2,1,0:T(8,128)(2,1)}, bf16[65,16,128]{2,1,0:T(8,128)(2,1)S(1)}, u32[]{:S(2)}, u32[]{:S(2)}) collective-permute-start(bf16[65,16,128]{2,1,0:T(8,128)(2,1)} %get-tuple-element.32), channel_id=1, source_target_pairs={{0,16},{4,20},{8,24},{12,28},{16,0},{20,4},{24,8},{28,12},{1,17},{... | collective-permute-start | bytes 798728 | tf_op jit(solution)/shard_map/ppermute | solution.py:450
  14.6 3.8 %collective-permute-start.5 = (bf16[65,16,128]{2,1,0:T(8,128)(2,1)}, bf16[65,16,128]{2,1,0:T(8,128)(2,1)S(1)}, u32[]{:S(2)}, u32[]{:S(2)}) collective-permute-start(bf16[65,16,128]{2,1,0:T(8,128)(2,1)} %get-tuple-element.34), channel_id=1, source_target_pairs={{0,24},{4,28},{8,16},{12,20},{16,8},{20,12},{24,0},{28,4},{1,25},{... | collective-permute-start | bytes 798728 | tf_op jit(solution)/shard_map/ppermute | solution.py:450
  18.4 9.5 %collective-permute-done.1.refs_3_ = bf16[65,16,128]{2,1,0:T(8,128)(2,1)S(1)} collective-permute-done((bf16[65,16,128]{2,1,0:T(8,128)(2,1)}, bf16[65,16,128]{2,1,0:T(8,128)(2,1)S(1)}, u32[]{:S(2)}, u32[]{:S(2)}) %collective-permute-start.1) | collective-permute-done | bytes 266272 | tf_op jit(solution)/shard_map/ppermute | solution.py:450
  29.0 2.3 collective-permute-done.2.refs_4_
  33.1 16.8 %collective-permute-done.4.refs_6_ = bf16[65,16,128]{2,1,0:T(8,128)(2,1)S(1)} collective-permute-done((bf16[65,16,128]{2,1,0:T(8,128)(2,1)}, bf16[65,16,128]{2,1,0:T(8,128)(2,1)S(1)}, u32[]{:S(2)}, u32[]{:S(2)}) %collective-permute-start.4) | collective-permute-done | bytes 266272 | tf_op jit(solution)/shard_map/ppermute | solution.py:450
  52.2 2.9 %shard_map.103 = (bf16[64,16,128]{2,1,0:T(8,128)(2,1)}, bf16[64,16,128]{2,1,0:T(8,128)(2,1)}) custom-call(s32[128]{0:T(128)} %get-tuple-element.97.refs_0_, bf16[65,16,128]{2,1,0:T(8,128)(2,1)} %get-tuple-element.28.refs_1_, bf16[65,16,128]{2,1,0:T(8,128)(2,1)} %copy-done.4, bf16[65,16,128]{2,1,0:T(8,128)(2,1)} %copy-done.5, bf16[65,16,128]{2,1,0:T(8,128)(2,1)} %copy-done.6, ...), custom_call_target="tpu_custom_call" | custom-call | bytes 1572864 | tf_op jit(solution)/shard_map/pallas_call | solution.py:143
  55.1 9.9 %collective-permute-start.9 = (bf16[64,16,128]{2,1,0:T(8,128)(2,1)}, bf16[64,16,128]{2,1,0:T(8,128)(2,1)S(1)}, u32[]{:S(2)}, u32[]{:S(2)}) collective-permute-start(bf16[64,16,128]{2,1,0:T(8,128)(2,1)} %get-tuple-element.37.refs_8_.refs_5_), channel_id=1, source_target_pairs={{0,8},{8,16},{16,24},{24,28},{28,20},{20,12},{12,4},{4,0},{1,9},{9... | collective-permute-start | bytes 786440 | tf_op jit(solution)/shard_map/ppermute | solution.py:456
  65.0 2.9 %shard_map.105 = (bf16[64,16,128]{2,1,0:T(8,128)(2,1)}, bf16[64,16,128]{2,1,0:T(8,128)(2,1)}) custom-call(s32[128]{0:T(128)} %get-tuple-element.98.refs_0_, bf16[65,16,128]{2,1,0:T(8,128)(2,1)} %get-tuple-element.28.refs_1_, bf16[65,16,128]{2,1,0:T(8,128)(2,1)} %copy-done.4, bf16[65,16,128]{2,1,0:T(8,128)(2,1)} %copy-done.5, bf16[65,16,128]{2,1,0:T(8,128)(2,1)} %copy-done.6, ...), custom_call_target="tpu_custom_call" | custom-call | bytes 1572864 | tf_op jit(solution)/shard_map/pallas_call | solution.py:143
  67.9 2.8 %collective-permute-start.23 = (bf16[64,16,128]{2,1,0:T(8,128)(2,1)}, bf16[64,16,128]{2,1,0:T(8,128)(2,1)}, u32[]{:S(2)}, u32[]{:S(2)}) collective-permute-start(bf16[64,16,128]{2,1,0:T(8,128)(2,1)} %get-tuple-element.42.refs_8_.refs_5_), channel_id=1, source_target_pairs={{0,8},{8,16},{16,24},{24,28},{28,20},{20,12},{12,4},{4,0},{1,9},{9... | collective-permute-start | bytes 786440 | tf_op jit(solution)/shard_map/ppermute | solution.py:456
  71.7 2.9 %collective-permute-start.10 = (bf16[64,16,128]{2,1,0:T(8,128)(2,1)S(1)}, bf16[64,16,128]{2,1,0:T(8,128)(2,1)}, u32[]{:S(2)}, u32[]{:S(2)}) collective-permute-start(bf16[64,16,128]{2,1,0:T(8,128)(2,1)S(1)} %collective-permute-done.9.refs_9_.refs_6_), channel_id=1, source_target_pairs={{0,8},{8,16},{16,24},{24,28},{28,20},{20,12},{12,4},{4,0},{1,9},{9... | collective-permute-start | bytes 786440 | tf_op jit(solution)/shard_map/ppermute | solution.py:456
  75.1 2.5 %collective-permute-done.23.refs_9_.refs_6_ = bf16[64,16,128]{2,1,0:T(8,128)(2,1)} collective-permute-done((bf16[64,16,128]{2,1,0:T(8,128)(2,1)}, bf16[64,16,128]{2,1,0:T(8,128)(2,1)}, u32[]{:S(2)}, u32[]{:S(2)}) %collective-permute-start.23) | collective-permute-done | bytes 262176 | tf_op jit(solution)/shard_map/ppermute | solution.py:456
  77.7 2.6 %collective-permute-start.24 = (bf16[64,16,128]{2,1,0:T(8,128)(2,1)}, bf16[64,16,128]{2,1,0:T(8,128)(2,1)}, u32[]{:S(2)}, u32[]{:S(2)}) collective-permute-start(bf16[64,16,128]{2,1,0:T(8,128)(2,1)} %collective-permute-done.23.refs_9_.refs_6_), channel_id=1, source_target_pairs={{0,8},{8,16},{16,24},{24,28},{28,20},{20,12},{12,4},{4,0},{1,9},{9... | collective-permute-start | bytes 786440 | tf_op jit(solution)/shard_map/ppermute | solution.py:456
  83.5 2.3 collective-permute-start.11
  86.4 2.5 %collective-permute-done.24.refs_10_.refs_7_ = bf16[64,16,128]{2,1,0:T(8,128)(2,1)} collective-permute-done((bf16[64,16,128]{2,1,0:T(8,128)(2,1)}, bf16[64,16,128]{2,1,0:T(8,128)(2,1)}, u32[]{:S(2)}, u32[]{:S(2)}) %collective-permute-start.24) | collective-permute-done | bytes 262176 | tf_op jit(solution)/shard_map/ppermute | solution.py:456
  88.9 2.6 %collective-permute-start.25 = (bf16[64,16,128]{2,1,0:T(8,128)(2,1)}, bf16[64,16,128]{2,1,0:T(8,128)(2,1)}, u32[]{:S(2)}, u32[]{:S(2)}) collective-permute-start(bf16[64,16,128]{2,1,0:T(8,128)(2,1)} %collective-permute-done.24.refs_10_.refs_7_), channel_id=1, source_target_pairs={{0,8},{8,16},{16,24},{24,28},{28,20},{20,12},{12,4},{4,0},{1,9},{9... | collective-permute-start | bytes 786440 | tf_op jit(solution)/shard_map/ppermute | solution.py:456
  92.0 2.8 %copy.39 = bf16[2,64,4096]{1,2,0:T(8,128)(2,1)} copy(bf16[2,64,4096]{2,1,0:T(8,128)(2,1)} %collective-permute-done.8) | data formatting | bytes 2097152 | tf_op jit(solution)/shard_map/ppermute | solution.py:302
  94.8 4.1 %pad_maximum_fusion = bf16[2,128,4096]{1,2,0:T(8,128)(2,1)S(1)} fusion(bf16[2,64,4096]{1,2,0:T(8,128)(2,1)} %copy.39, bf16[2,32,4096]{1,2,0:T(8,128)(2,1)} %copy.38, bf16[2,32,4096]{1,2,0:T(8,128)(2,1)S(1)} %copy.37), kind=kLoop, calls=%fused_computation | loop fusion | flops 6291456 | bytes 4194304 | tf_op jit(solution)/shard_map/concatenate | solution.py:307
  100.2 2.1 collective-permute-start.15
  104.4 5.1 %collective-permute-done.15.refs_12_.refs_9_ = bf16[64,16,128]{2,1,0:T(8,128)(2,1)S(1)} collective-permute-done((bf16[64,16,128]{2,1,0:T(8,128)(2,1)S(1)}, bf16[64,16,128]{2,1,0:T(8,128)(2,1)S(1)}, u32[]{:S(2)}, u32[]{:S(2)}) %collective-permute-start.15) | collective-permute-done | bytes 262176 | tf_op jit(solution)/shard_map/ppermute | solution.py:456
  109.5 2.1 collective-permute-start.16
  111.6 3.6 %collective-permute-done.26.refs_12_.refs_9_ = bf16[64,16,128]{2,1,0:T(8,128)(2,1)} collective-permute-done((bf16[64,16,128]{2,1,0:T(8,128)(2,1)}, bf16[64,16,128]{2,1,0:T(8,128)(2,1)}, u32[]{:S(2)}, u32[]{:S(2)}) %collective-permute-start.26) | collective-permute-done | bytes 262176 | tf_op jit(solution)/shard_map/ppermute | solution.py:456
  115.2 2.1 collective-permute-start.27
  117.3 3.5 %collective-permute-done.16.refs_13_.refs_10_ = bf16[64,16,128]{2,1,0:T(8,128)(2,1)} collective-permute-done((bf16[64,16,128]{2,1,0:T(8,128)(2,1)S(1)}, bf16[64,16,128]{2,1,0:T(8,128)(2,1)}, u32[]{:S(2)}, u32[]{:S(2)}) %collective-permute-start.16) | collective-permute-done | bytes 262176 | tf_op jit(solution)/shard_map/ppermute | solution.py:456
  120.8 2.1 collective-permute-start.17
  124.3 2.1 collective-permute-done.27.refs_13_.refs_10_
  126.5 2.1 collective-permute-start.28
  128.5 3.5 %collective-permute-done.17.refs_14_.refs_11_ = bf16[64,16,128]{2,1,0:T(8,128)(2,1)} collective-permute-done((bf16[64,16,128]{2,1,0:T(8,128)(2,1)}, bf16[64,16,128]{2,1,0:T(8,128)(2,1)}, u32[]{:S(2)}, u32[]{:S(2)}) %collective-permute-start.17) | collective-permute-done | bytes 262176 | tf_op jit(solution)/shard_map/ppermute | solution.py:456
  132.1 2.1 collective-permute-start.18
  137.7 2.1 collective-permute-start.29
  139.8 3.5 %collective-permute-done.18.refs_15_.refs_12_ = bf16[64,16,128]{2,1,0:T(8,128)(2,1)} collective-permute-done((bf16[64,16,128]{2,1,0:T(8,128)(2,1)}, bf16[64,16,128]{2,1,0:T(8,128)(2,1)}, u32[]{:S(2)}, u32[]{:S(2)}) %collective-permute-start.18) | collective-permute-done | bytes 262176 | tf_op jit(solution)/shard_map/ppermute | solution.py:456
  143.3 2.1 collective-permute-done.22.refs_23_.refs_20_
  145.4 10.0 %shard_map.104 = (bf16[32,128,128]{2,1,0:T(8,128)(2,1)}, f32[32,128,128]{2,1,0:T(8,128)}, bf16[8,16,128,128]{3,2,1,0:T(8,128)(2,1)}) custom-call(s32[8]{0:T(128)} %get-tuple-element.94.refs_0_, s32[128]{0:T(128)} %get-tuple-element.103.refs_1_.refs_3_.refs_0_, s32[128]{0:T(128)} %get-tuple-element.100.refs_2_.refs_4_.refs_1_, ...), custom_call_target="tpu_custom_call" | custom-call | flops 21474836480 | bytes 13631488 | tf_op jit(solution)/shard_map/pallas_call | solution.py:143
  156.5 2.1 collective-permute-start.53
  159.4 9.8 %shard_map.106 = (bf16[32,128,128]{2,1,0:T(8,128)(2,1)}, bf16[8,16,128,128]{3,2,1,0:T(8,128)(2,1)}) custom-call(s32[8]{0:T(128)} %get-tuple-element.94.refs_0_, s32[128]{0:T(128)} %get-tuple-element.104.refs_3_.refs_1_.refs_0_, s32[128]{0:T(128)} %get-tuple-element.99.refs_4_.refs_2_.refs_1_, s32[128]{0:T(128)} %get-tuple-element.103.refs_1_.refs_3_.refs_0_, ...), custom_call_target="tpu_custom_call" | custom-call | flops 21474836480 | bytes 13631488 | tf_op jit(solution)/shard_map/pallas_call | solution.py:143
  170.3 2.1 collective-permute-start.37
  172.6 2.1 collective-permute-start.55
  174.7 3.9 %collective-permute-done.37 = bf16[16,64,128]{2,1,0:T(8,128)(2,1)S(1)} collective-permute-done((bf16[16,64,128]{2,1,0:T(8,128)(2,1)S(1)}, bf16[16,64,128]{2,1,0:T(8,128)(2,1)S(1)}, u32[]{:S(2)}, u32[]{:S(2)}) %collective-permute-start.37) | collective-permute-done | bytes 262176 | tf_op jit(solution)/shard_map/ppermute | solution.py:338
  178.6 2.7 %collective-permute-done.38 = bf16[16,64,128]{2,1,0:T(8,128)(2,1)S(1)} collective-permute-done((bf16[16,64,128]{2,1,0:T(8,128)(2,1)S(1)}, bf16[16,64,128]{2,1,0:T(8,128)(2,1)S(1)}, u32[]{:S(2)}, u32[]{:S(2)}) %collective-permute-start.38) | collective-permute-done | bytes 262176 | tf_op jit(solution)/shard_map/ppermute | solution.py:338
  184.6 6.3 %shard_map.107 = bf16[128,4096]{1,0:T(8,128)(2,1)} custom-call(s32[128]{0:T(128)} %get-tuple-element.104.refs_3_.refs_1_.refs_0_, s32[128]{0:T(128)} %get-tuple-element.99.refs_4_.refs_2_.refs_1_, s32[8]{0:T(128)} %get-tuple-element.96.refs_5_.refs_2_, s32[8]{0:T(128)} %get-tuple-element.95.refs_6_.refs_3_, bf16[32,128,128]{2,1,0:T(8,128)(2,1)} %get-tuple-element.46.refs_4_, ...), custom_call_target="tpu_custom_call" | custom-call | flops 10737418240 | bytes 6291456 | tf_op jit(solution)/shard_map/pallas_call | solution.py:143
  196.5 7.9 %shard_map.108 = bf16[128,4096]{1,0:T(8,128)(2,1)} custom-call(s32[128]{0:T(128)} %get-tuple-element.103.refs_1_.refs_3_.refs_0_, s32[128]{0:T(128)} %get-tuple-element.100.refs_2_.refs_4_.refs_1_, s32[8]{0:T(128)} %get-tuple-element.96.refs_5_.refs_2_, s32[8]{0:T(128)} %get-tuple-element.95.refs_6_.refs_3_, ...), custom_call_target="tpu_custom_call" | custom-call | flops 10737418240 | bytes 6291456 | tf_op jit(solution)/shard_map/pallas_call | solution.py:143
  213.5 3.7 %collective-permute-done.44 = bf16[16,64,128]{2,1,0:T(8,128)(2,1)S(1)} collective-permute-done((bf16[16,64,128]{2,1,0:T(8,128)(2,1)S(1)}, bf16[16,64,128]{2,1,0:T(8,128)(2,1)S(1)}, u32[]{:S(2)}, u32[]{:S(2)}) %collective-permute-start.44) | collective-permute-done | bytes 262176 | tf_op jit(solution)/shard_map/ppermute | solution.py:338
  219.8 3.0 %collective-permute-done.58 = bf16[16,64,128]{2,1,0:T(8,128)(2,1)S(1)} collective-permute-done((bf16[16,64,128]{2,1,0:T(8,128)(2,1)S(1)}, bf16[16,64,128]{2,1,0:T(8,128)(2,1)S(1)}, u32[]{:S(2)}, u32[]{:S(2)}) %collective-permute-start.58) | collective-permute-done | bytes 262176 | tf_op jit(solution)/shard_map/ppermute | solution.py:338
  225.4 3.0 %collective-permute-done.45 = bf16[16,64,128]{2,1,0:T(8,128)(2,1)S(1)} collective-permute-done((bf16[16,64,128]{2,1,0:T(8,128)(2,1)S(1)}, bf16[16,64,128]{2,1,0:T(8,128)(2,1)S(1)}, u32[]{:S(2)}, u32[]{:S(2)}) %collective-permute-start.45) | collective-permute-done | bytes 262176 | tf_op jit(solution)/shard_map/ppermute | solution.py:338
  231.0 3.0 %collective-permute-done.59 = bf16[16,64,128]{2,1,0:T(8,128)(2,1)S(1)} collective-permute-done((bf16[16,64,128]{2,1,0:T(8,128)(2,1)S(1)}, bf16[16,64,128]{2,1,0:T(8,128)(2,1)S(1)}, u32[]{:S(2)}, u32[]{:S(2)}) %collective-permute-start.59) | collective-permute-done | bytes 262176 | tf_op jit(solution)/shard_map/ppermute | solution.py:338
  242.3 3.0 %collective-permute-done.60 = bf16[16,64,128]{2,1,0:T(8,128)(2,1)S(1)} collective-permute-done((bf16[16,64,128]{2,1,0:T(8,128)(2,1)S(1)}, bf16[16,64,128]{2,1,0:T(8,128)(2,1)S(1)}, u32[]{:S(2)}, u32[]{:S(2)}) %collective-permute-start.60) | collective-permute-done | bytes 262176 | tf_op jit(solution)/shard_map/ppermute | solution.py:338
  246.9 3.7 %collective-permute-done.47 = bf16[16,64,128]{2,1,0:T(8,128)(2,1)S(1)} collective-permute-done((bf16[16,64,128]{2,1,0:T(8,128)(2,1)S(1)}, bf16[16,64,128]{2,1,0:T(8,128)(2,1)S(1)}, u32[]{:S(2)}, u32[]{:S(2)}) %collective-permute-start.47) | collective-permute-done | bytes 262176 | tf_op jit(solution)/shard_map/ppermute | solution.py:338
  (191 shorter events, 64.9 us)
Async XLA Ops:
  8.0 20.0 %collective-permute-start.1 = (bf16[65,16,128]{2,1,0:T(8,128)(2,1)}, bf16[65,16,128]{2,1,0:T(8,128)(2,1)S(1)}, u32[]{:S(2)}, u32[]{:S(2)}) collective-permute-start(bf16[65,16,128]{2,1,0:T(8,128)(2,1)} %get-tuple-element.30), channel_id=1, source_target_pairs={{0,8},{4,12},{8,0},{12,4},{16,24},{20,28},{24,16},{28,20},{1,9},{5... | collective-permute-start | bytes 798728 | tf_op jit(solution)/shard_map/ppermute | solution.py:450
  9.5 21.8 %collective-permute-start.2 = (bf16[65,16,128]{2,1,0:T(8,128)(2,1)}, bf16[65,16,128]{2,1,0:T(8,128)(2,1)S(1)}, u32[]{:S(2)}, u32[]{:S(2)}) collective-permute-start(bf16[65,16,128]{2,1,0:T(8,128)(2,1)} %get-tuple-element.31), channel_id=1, source_target_pairs={{0,12},{4,8},{8,4},{12,0},{16,28},{20,24},{24,20},{28,16},{1,13},{... | collective-permute-start | bytes 798728 | tf_op jit(solution)/shard_map/ppermute | solution.py:450
  9.5 23.5 %collective-permute-start.3 = (bf16[65,16,128]{2,1,0:T(8,128)(2,1)}, bf16[65,16,128]{2,1,0:T(8,128)(2,1)S(1)}, u32[]{:S(2)}, u32[]{:S(2)}) collective-permute-start(bf16[65,16,128]{2,1,0:T(8,128)(2,1)} %get-tuple-element.32), channel_id=1, source_target_pairs={{0,16},{4,20},{8,24},{12,28},{16,0},{20,4},{24,8},{28,12},{1,17},{... | collective-permute-start | bytes 798728 | tf_op jit(solution)/shard_map/ppermute | solution.py:450
  12.5 37.3 %collective-permute-start.4 = (bf16[65,16,128]{2,1,0:T(8,128)(2,1)}, bf16[65,16,128]{2,1,0:T(8,128)(2,1)S(1)}, u32[]{:S(2)}, u32[]{:S(2)}) collective-permute-start(bf16[65,16,128]{2,1,0:T(8,128)(2,1)} %get-tuple-element.33), channel_id=1, source_target_pairs={{0,20},{4,16},{8,28},{12,24},{16,4},{20,0},{24,12},{28,8},{1,21},{... | collective-permute-start | bytes 798728 | tf_op jit(solution)/shard_map/ppermute | solution.py:450
  14.6 35.2 %collective-permute-start.5 = (bf16[65,16,128]{2,1,0:T(8,128)(2,1)}, bf16[65,16,128]{2,1,0:T(8,128)(2,1)S(1)}, u32[]{:S(2)}, u32[]{:S(2)}) collective-permute-start(bf16[65,16,128]{2,1,0:T(8,128)(2,1)} %get-tuple-element.34), channel_id=1, source_target_pairs={{0,24},{4,28},{8,16},{12,20},{16,8},{20,12},{24,0},{28,4},{1,25},{... | collective-permute-start | bytes 798728 | tf_op jit(solution)/shard_map/ppermute | solution.py:450
  27.9 22.0 %collective-permute-start.6 = (bf16[65,16,128]{2,1,0:T(8,128)(2,1)}, bf16[65,16,128]{2,1,0:T(8,128)(2,1)S(1)}, u32[]{:S(2)}, u32[]{:S(2)}) collective-permute-start(bf16[65,16,128]{2,1,0:T(8,128)(2,1)} %get-tuple-element.35), channel_id=1, source_target_pairs={{0,28},{4,24},{8,20},{12,16},{16,12},{20,8},{24,4},{28,0},{1,29},{... | collective-permute-start | bytes 798728 | tf_op jit(solution)/shard_map/ppermute | solution.py:450
  31.3 18.6 %collective-permute-start.7 = (bf16[2,32,4096]{2,1,0:T(8,128)(2,1)S(1)}, bf16[2,32,4096]{2,1,0:T(8,128)(2,1)S(1)}, u32[]{:S(2)}, u32[]{:S(2)}) collective-permute-start(bf16[2,32,4096]{2,1,0:T(8,128)(2,1)S(1)} %pad_maximum_fusion.3), channel_id=1, source_target_pairs={{0,2},{1,3},{2,0},{3,1},{4,6},{5,7},{6,4},{7,5},{8,10},{9,11},{10,... | collective-permute-start | bytes 1572872 | tf_op jit(solution)/shard_map/ppermute | solution.py:302
  51.1 40.9 %collective-permute-start.8 = (bf16[2,64,4096]{2,1,0:T(8,128)(2,1)}, bf16[2,64,4096]{2,1,0:T(8,128)(2,1)}, u32[]{:S(2)}, u32[]{:S(2)}) collective-permute-start(bf16[2,64,4096]{2,1,0:T(8,128)(2,1)} %pad_maximum_fusion.2), channel_id=1, source_target_pairs={{0,1},{1,0},{2,3},{3,2},{4,5},{5,4},{6,7},{7,6},{8,9},{9,8},{10,11... | collective-permute-start | bytes 3145736 | tf_op jit(solution)/shard_map/ppermute | solution.py:302
  55.1 16.6 %collective-permute-start.9 = (bf16[64,16,128]{2,1,0:T(8,128)(2,1)}, bf16[64,16,128]{2,1,0:T(8,128)(2,1)S(1)}, u32[]{:S(2)}, u32[]{:S(2)}) collective-permute-start(bf16[64,16,128]{2,1,0:T(8,128)(2,1)} %get-tuple-element.37.refs_8_.refs_5_), channel_id=1, source_target_pairs={{0,8},{8,16},{16,24},{24,28},{28,20},{20,12},{12,4},{4,0},{1,9},{9... | collective-permute-start | bytes 786440 | tf_op jit(solution)/shard_map/ppermute | solution.py:456
  71.7 11.8 %collective-permute-start.10 = (bf16[64,16,128]{2,1,0:T(8,128)(2,1)S(1)}, bf16[64,16,128]{2,1,0:T(8,128)(2,1)}, u32[]{:S(2)}, u32[]{:S(2)}) collective-permute-start(bf16[64,16,128]{2,1,0:T(8,128)(2,1)S(1)} %collective-permute-done.9.refs_9_.refs_6_), channel_id=1, source_target_pairs={{0,8},{8,16},{16,24},{24,28},{28,20},{20,12},{12,4},{4,0},{1,9},{9... | collective-permute-start | bytes 786440 | tf_op jit(solution)/shard_map/ppermute | solution.py:456
  75.1 11.2 %collective-permute-start.13 = (bf16[64,16,128]{2,1,0:T(8,128)(2,1)}, bf16[64,16,128]{2,1,0:T(8,128)(2,1)}, u32[]{:S(2)}, u32[]{:S(2)}) collective-permute-start(bf16[64,16,128]{2,1,0:T(8,128)(2,1)} %collective-permute-done.12.refs_17_.refs_14_), channel_id=1, source_target_pairs={{8,0},{16,8},{24,16},{28,24},{20,28},{12,20},{4,12},{0,4},{9,1},{1... | collective-permute-start | bytes 786440 | tf_op jit(solution)/shard_map/ppermute | solution.py:456
  77.7 11.2 %collective-permute-start.24 = (bf16[64,16,128]{2,1,0:T(8,128)(2,1)}, bf16[64,16,128]{2,1,0:T(8,128)(2,1)}, u32[]{:S(2)}, u32[]{:S(2)}) collective-permute-start(bf16[64,16,128]{2,1,0:T(8,128)(2,1)} %collective-permute-done.23.refs_9_.refs_6_), channel_id=1, source_target_pairs={{0,8},{8,16},{16,24},{24,28},{28,20},{20,12},{12,4},{4,0},{1,9},{9... | collective-permute-start | bytes 786440 | tf_op jit(solution)/shard_map/ppermute | solution.py:456
  80.7 11.2 %collective-permute-start.31 = (bf16[64,16,128]{2,1,0:T(8,128)(2,1)}, bf16[64,16,128]{2,1,0:T(8,128)(2,1)}, u32[]{:S(2)}, u32[]{:S(2)}) collective-permute-start(bf16[64,16,128]{2,1,0:T(8,128)(2,1)} %collective-permute-done.30.refs_17_.refs_14_), channel_id=1, source_target_pairs={{8,0},{16,8},{24,16},{28,24},{20,28},{12,20},{4,12},{0,4},{9,1},{1... | collective-permute-start | bytes 786440 | tf_op jit(solution)/shard_map/ppermute | solution.py:456
  83.5 16.7 %collective-permute-start.11 = (bf16[64,16,128]{2,1,0:T(8,128)(2,1)}, bf16[64,16,128]{2,1,0:T(8,128)(2,1)S(1)}, u32[]{:S(2)}, u32[]{:S(2)}) collective-permute-start(bf16[64,16,128]{2,1,0:T(8,128)(2,1)} %collective-permute-done.10.refs_10_.refs_7_), channel_id=1, source_target_pairs={{0,8},{8,16},{16,24},{24,28},{28,20},{20,12},{12,4},{4,0},{1,9},{9... | collective-permute-start | bytes 786440 | tf_op jit(solution)/shard_map/ppermute | solution.py:456
  86.4 13.8 %collective-permute-start.14 = (bf16[64,16,128]{2,1,0:T(8,128)(2,1)}, bf16[64,16,128]{2,1,0:T(8,128)(2,1)S(1)}, u32[]{:S(2)}, u32[]{:S(2)}) collective-permute-start(bf16[64,16,128]{2,1,0:T(8,128)(2,1)} %collective-permute-done.13.refs_18_.refs_15_), channel_id=1, source_target_pairs={{8,0},{16,8},{24,16},{28,24},{20,28},{12,20},{4,12},{0,4},{9,1},{1... | collective-permute-start | bytes 786440 | tf_op jit(solution)/shard_map/ppermute | solution.py:456
  88.9 13.4 %collective-permute-start.25 = (bf16[64,16,128]{2,1,0:T(8,128)(2,1)}, bf16[64,16,128]{2,1,0:T(8,128)(2,1)}, u32[]{:S(2)}, u32[]{:S(2)}) collective-permute-start(bf16[64,16,128]{2,1,0:T(8,128)(2,1)} %collective-permute-done.24.refs_10_.refs_7_), channel_id=1, source_target_pairs={{0,8},{8,16},{16,24},{24,28},{28,20},{20,12},{12,4},{4,0},{1,9},{9... | collective-permute-start | bytes 786440 | tf_op jit(solution)/shard_map/ppermute | solution.py:456
  92.0 12.4 %collective-permute-start.32 = (bf16[64,16,128]{2,1,0:T(8,128)(2,1)}, bf16[64,16,128]{2,1,0:T(8,128)(2,1)}, u32[]{:S(2)}, u32[]{:S(2)}) collective-permute-start(bf16[64,16,128]{2,1,0:T(8,128)(2,1)} %collective-permute-done.31.refs_18_.refs_15_), channel_id=1, source_target_pairs={{8,0},{16,8},{24,16},{28,24},{20,28},{12,20},{4,12},{0,4},{9,1},{1... | collective-permute-start | bytes 786440 | tf_op jit(solution)/shard_map/ppermute | solution.py:456
  102.3 12.9 %collective-permute-start.26 = (bf16[64,16,128]{2,1,0:T(8,128)(2,1)}, bf16[64,16,128]{2,1,0:T(8,128)(2,1)}, u32[]{:S(2)}, u32[]{:S(2)}) collective-permute-start(bf16[64,16,128]{2,1,0:T(8,128)(2,1)} %collective-permute-done.25.refs_11_.refs_8_), channel_id=1, source_target_pairs={{0,8},{8,16},{16,24},{24,28},{28,20},{20,12},{12,4},{4,0},{1,9},{9... | collective-permute-start | bytes 786440 | tf_op jit(solution)/shard_map/ppermute | solution.py:456
  104.4 12.9 %collective-permute-start.33 = (bf16[64,16,128]{2,1,0:T(8,128)(2,1)}, bf16[64,16,128]{2,1,0:T(8,128)(2,1)}, u32[]{:S(2)}, u32[]{:S(2)}) collective-permute-start(bf16[64,16,128]{2,1,0:T(8,128)(2,1)} %collective-permute-done.32.refs_19_.refs_16_), channel_id=1, source_target_pairs={{8,0},{16,8},{24,16},{28,24},{20,28},{12,20},{4,12},{0,4},{9,1},{1... | collective-permute-start | bytes 786440 | tf_op jit(solution)/shard_map/ppermute | solution.py:456
  109.5 11.3 %collective-permute-start.16 = (bf16[64,16,128]{2,1,0:T(8,128)(2,1)S(1)}, bf16[64,16,128]{2,1,0:T(8,128)(2,1)}, u32[]{:S(2)}, u32[]{:S(2)}) collective-permute-start(bf16[64,16,128]{2,1,0:T(8,128)(2,1)S(1)} %collective-permute-done.15.refs_12_.refs_9_), channel_id=1, source_target_pairs={{0,8},{8,16},{16,24},{24,28},{28,20},{20,12},{12,4},{4,0},{1,9},{9... | collective-permute-start | bytes 786440 | tf_op jit(solution)/shard_map/ppermute | solution.py:456
  111.6 11.3 %collective-permute-start.20 = (bf16[64,16,128]{2,1,0:T(8,128)(2,1)S(1)}, bf16[64,16,128]{2,1,0:T(8,128)(2,1)}, u32[]{:S(2)}, u32[]{:S(2)}) collective-permute-start(bf16[64,16,128]{2,1,0:T(8,128)(2,1)S(1)} %collective-permute-done.19.refs_20_.refs_17_), channel_id=1, source_target_pairs={{8,0},{16,8},{24,16},{28,24},{20,28},{12,20},{4,12},{0,4},{9,1},{1... | collective-permute-start | bytes 786440 | tf_op jit(solution)/shard_map/ppermute | solution.py:456
  115.2 11.2 %collective-permute-start.27 = (bf16[64,16,128]{2,1,0:T(8,128)(2,1)}, bf16[64,16,128]{2,1,0:T(8,128)(2,1)}, u32[]{:S(2)}, u32[]{:S(2)}) collective-permute-start(bf16[64,16,128]{2,1,0:T(8,128)(2,1)} %collective-permute-done.26.refs_12_.refs_9_), channel_id=1, source_target_pairs={{0,8},{8,16},{16,24},{24,28},{28,20},{20,12},{12,4},{4,0},{1,9},{9... | collective-permute-start | bytes 786440 | tf_op jit(solution)/shard_map/ppermute | solution.py:456
  117.3 11.2 %collective-permute-start.34 = (bf16[64,16,128]{2,1,0:T(8,128)(2,1)}, bf16[64,16,128]{2,1,0:T(8,128)(2,1)}, u32[]{:S(2)}, u32[]{:S(2)}) collective-permute-start(bf16[64,16,128]{2,1,0:T(8,128)(2,1)} %collective-permute-done.33.refs_20_.refs_17_), channel_id=1, source_target_pairs={{8,0},{16,8},{24,16},{28,24},{20,28},{12,20},{4,12},{0,4},{9,1},{1... | collective-permute-start | bytes 786440 | tf_op jit(solution)/shard_map/ppermute | solution.py:456
  120.8 11.2 %collective-permute-start.17 = (bf16[64,16,128]{2,1,0:T(8,128)(2,1)}, bf16[64,16,128]{2,1,0:T(8,128)(2,1)}, u32[]{:S(2)}, u32[]{:S(2)}) collective-permute-start(bf16[64,16,128]{2,1,0:T(8,128)(2,1)} %collective-permute-done.16.refs_13_.refs_10_), channel_id=1, source_target_pairs={{0,8},{8,16},{16,24},{24,28},{28,20},{20,12},{12,4},{4,0},{1,9},{9... | collective-permute-start | bytes 786440 | tf_op jit(solution)/shard_map/ppermute | solution.py:456
  122.9 11.2 %collective-permute-start.21 = (bf16[64,16,128]{2,1,0:T(8,128)(2,1)}, bf16[64,16,128]{2,1,0:T(8,128)(2,1)}, u32[]{:S(2)}, u32[]{:S(2)}) collective-permute-start(bf16[64,16,128]{2,1,0:T(8,128)(2,1)} %collective-permute-done.20.refs_21_.refs_18_), channel_id=1, source_target_pairs={{8,0},{16,8},{24,16},{28,24},{20,28},{12,20},{4,12},{0,4},{9,1},{1... | collective-permute-start | bytes 786440 | tf_op jit(solution)/shard_map/ppermute | solution.py:456
  126.5 11.2 %collective-permute-start.28 = (bf16[64,16,128]{2,1,0:T(8,128)(2,1)}, bf16[64,16,128]{2,1,0:T(8,128)(2,1)}, u32[]{:S(2)}, u32[]{:S(2)}) collective-permute-start(bf16[64,16,128]{2,1,0:T(8,128)(2,1)} %collective-permute-done.27.refs_13_.refs_10_), channel_id=1, source_target_pairs={{0,8},{8,16},{16,24},{24,28},{28,20},{20,12},{12,4},{4,0},{1,9},{9... | collective-permute-start | bytes 786440 | tf_op jit(solution)/shard_map/ppermute | solution.py:456
  128.5 11.2 %collective-permute-start.35 = (bf16[64,16,128]{2,1,0:T(8,128)(2,1)}, bf16[64,16,128]{2,1,0:T(8,128)(2,1)}, u32[]{:S(2)}, u32[]{:S(2)}) collective-permute-start(bf16[64,16,128]{2,1,0:T(8,128)(2,1)} %collective-permute-done.34.refs_21_.refs_18_), channel_id=1, source_target_pairs={{8,0},{16,8},{24,16},{28,24},{20,28},{12,20},{4,12},{0,4},{9,1},{1... | collective-permute-start | bytes 786440 | tf_op jit(solution)/shard_map/ppermute | solution.py:456
  132.1 11.2 %collective-permute-start.18 = (bf16[64,16,128]{2,1,0:T(8,128)(2,1)}, bf16[64,16,128]{2,1,0:T(8,128)(2,1)}, u32[]{:S(2)}, u32[]{:S(2)}) collective-permute-start(bf16[64,16,128]{2,1,0:T(8,128)(2,1)} %collective-permute-done.17.refs_14_.refs_11_), channel_id=1, source_target_pairs={{0,8},{8,16},{16,24},{24,28},{28,20},{20,12},{12,4},{4,0},{1,9},{9... | collective-permute-start | bytes 786440 | tf_op jit(solution)/shard_map/ppermute | solution.py:456
  134.2 11.2 %collective-permute-start.22 = (bf16[64,16,128]{2,1,0:T(8,128)(2,1)}, bf16[64,16,128]{2,1,0:T(8,128)(2,1)}, u32[]{:S(2)}, u32[]{:S(2)}) collective-permute-start(bf16[64,16,128]{2,1,0:T(8,128)(2,1)} %collective-permute-done.21.refs_22_.refs_19_), channel_id=1, source_target_pairs={{8,0},{16,8},{24,16},{28,24},{20,28},{12,20},{4,12},{0,4},{9,1},{1... | collective-permute-start | bytes 786440 | tf_op jit(solution)/shard_map/ppermute | solution.py:456
  137.7 20.9 %collective-permute-start.29 = (bf16[64,16,128]{2,1,0:T(8,128)(2,1)}, bf16[64,16,128]{2,1,0:T(8,128)(2,1)S(1)}, u32[]{:S(2)}, u32[]{:S(2)}) collective-permute-start(bf16[64,16,128]{2,1,0:T(8,128)(2,1)} %collective-permute-done.28.refs_14_.refs_11_), channel_id=1, source_target_pairs={{0,8},{8,16},{16,24},{24,28},{28,20},{20,12},{12,4},{4,0},{1,9},{9... | collective-permute-start | bytes 786440 | tf_op jit(solution)/shard_map/ppermute | solution.py:456
  139.8 18.8 %collective-permute-start.36 = (bf16[64,16,128]{2,1,0:T(8,128)(2,1)}, bf16[64,16,128]{2,1,0:T(8,128)(2,1)S(1)}, u32[]{:S(2)}, u32[]{:S(2)}) collective-permute-start(bf16[64,16,128]{2,1,0:T(8,128)(2,1)} %collective-permute-done.35.refs_22_.refs_19_), channel_id=1, source_target_pairs={{8,0},{16,8},{24,16},{28,24},{20,28},{12,20},{4,12},{0,4},{9,1},{1... | collective-permute-start | bytes 786440 | tf_op jit(solution)/shard_map/ppermute | solution.py:456
  156.5 15.9 %collective-permute-start.53 = (bf16[16,64,128]{2,1,0:T(8,128)(2,1)S(1)}, bf16[16,64,128]{2,1,0:T(8,128)(2,1)S(1)}, u32[]{:S(2)}, u32[]{:S(2)}) collective-permute-start(bf16[16,64,128]{2,1,0:T(8,128)(2,1)S(1)} %get-tuple-element.69), channel_id=1, source_target_pairs={{0,8},{8,16},{16,24},{24,28},{28,20},{20,12},{12,4},{4,0},{1,9},{9... | collective-permute-start | bytes 786440 | tf_op jit(solution)/shard_map/ppermute | solution.py:338
  158.6 13.8 %collective-permute-start.54 = (bf16[16,64,128]{2,1,0:T(8,128)(2,1)S(1)}, bf16[16,64,128]{2,1,0:T(8,128)(2,1)S(1)}, u32[]{:S(2)}, u32[]{:S(2)}) collective-permute-start(bf16[16,64,128]{2,1,0:T(8,128)(2,1)S(1)} %get-tuple-element.68), channel_id=1, source_target_pairs={{8,0},{16,8},{24,16},{28,24},{20,28},{12,20},{4,12},{0,4},{9,1},{1... | collective-permute-start | bytes 786440 | tf_op jit(solution)/shard_map/ppermute | solution.py:338
  172.6 18.3 %collective-permute-start.55 = (bf16[16,64,128]{2,1,0:T(8,128)(2,1)S(1)}, bf16[16,64,128]{2,1,0:T(8,128)(2,1)S(1)}, u32[]{:S(2)}, u32[]{:S(2)}) collective-permute-start(bf16[16,64,128]{2,1,0:T(8,128)(2,1)S(1)} %get-tuple-element.66), channel_id=1, source_target_pairs={{0,8},{8,16},{16,24},{24,28},{28,20},{20,12},{12,4},{4,0},{1,9},{9... | collective-permute-start | bytes 786440 | tf_op jit(solution)/shard_map/ppermute | solution.py:338
  174.7 16.2 %collective-permute-start.61 = (bf16[16,64,128]{2,1,0:T(8,128)(2,1)S(1)}, bf16[16,64,128]{2,1,0:T(8,128)(2,1)S(1)}, u32[]{:S(2)}, u32[]{:S(2)}) collective-permute-start(bf16[16,64,128]{2,1,0:T(8,128)(2,1)S(1)} %get-tuple-element.67), channel_id=1, source_target_pairs={{8,0},{16,8},{24,16},{28,24},{20,28},{12,20},{4,12},{0,4},{9,1},{1... | collective-permute-start | bytes 786440 | tf_op jit(solution)/shard_map/ppermute | solution.py:338
  182.5 10.7 %collective-permute-start.39 = (bf16[16,64,128]{2,1,0:T(8,128)(2,1)S(1)}, bf16[16,64,128]{2,1,0:T(8,128)(2,1)S(1)}, u32[]{:S(2)}, u32[]{:S(2)}) collective-permute-start(bf16[16,64,128]{2,1,0:T(8,128)(2,1)S(1)} %get-tuple-element.83), channel_id=1, source_target_pairs={{0,8},{8,16},{16,24},{24,28},{28,20},{20,12},{12,4},{4,0},{1,9},{9... | collective-permute-start | bytes 786440 | tf_op jit(solution)/shard_map/ppermute | solution.py:338
  191.1 13.3 %collective-permute-start.56 = (bf16[16,64,128]{2,1,0:T(8,128)(2,1)S(1)}, bf16[16,64,128]{2,1,0:T(8,128)(2,1)S(1)}, u32[]{:S(2)}, u32[]{:S(2)}) collective-permute-start(bf16[16,64,128]{2,1,0:T(8,128)(2,1)S(1)} %get-tuple-element.64), channel_id=1, source_target_pairs={{0,8},{8,16},{16,24},{24,28},{28,20},{20,12},{12,4},{4,0},{1,9},{9... | collective-permute-start | bytes 786440 | tf_op jit(solution)/shard_map/ppermute | solution.py:338
  191.2 13.2 %collective-permute-start.62 = (bf16[16,64,128]{2,1,0:T(8,128)(2,1)S(1)}, bf16[16,64,128]{2,1,0:T(8,128)(2,1)S(1)}, u32[]{:S(2)}, u32[]{:S(2)}) collective-permute-start(bf16[16,64,128]{2,1,0:T(8,128)(2,1)S(1)} %get-tuple-element.65), channel_id=1, source_target_pairs={{8,0},{16,8},{24,16},{28,24},{20,28},{12,20},{4,12},{0,4},{9,1},{1... | collective-permute-start | bytes 786440 | tf_op jit(solution)/shard_map/ppermute | solution.py:338
  194.4 13.5 %collective-permute-start.43 = (bf16[16,64,128]{2,1,0:T(8,128)(2,1)S(1)}, bf16[16,64,128]{2,1,0:T(8,128)(2,1)S(1)}, u32[]{:S(2)}, u32[]{:S(2)}) collective-permute-start(bf16[16,64,128]{2,1,0:T(8,128)(2,1)S(1)} %get-tuple-element.81), channel_id=1, source_target_pairs={{0,8},{8,16},{16,24},{24,28},{28,20},{20,12},{12,4},{4,0},{1,9},{9... | collective-permute-start | bytes 786440 | tf_op jit(solution)/shard_map/ppermute | solution.py:338
  194.5 13.4 %collective-permute-start.48 = (bf16[16,64,128]{2,1,0:T(8,128)(2,1)S(1)}, bf16[16,64,128]{2,1,0:T(8,128)(2,1)S(1)}, u32[]{:S(2)}, u32[]{:S(2)}) collective-permute-start(bf16[16,64,128]{2,1,0:T(8,128)(2,1)S(1)} %get-tuple-element.80), channel_id=1, source_target_pairs={{8,0},{16,8},{24,16},{28,24},{20,28},{12,20},{4,12},{0,4},{9,1},{1... | collective-permute-start | bytes 786440 | tf_op jit(solution)/shard_map/ppermute | solution.py:338
  207.8 28.9 %collective-permute-start.41 = (bf16[2,64,4096]{2,1,0:T(8,128)(2,1)S(1)}, bf16[2,64,4096]{2,1,0:T(8,128)(2,1)S(1)}, u32[]{:S(2)}, u32[]{:S(2)}) collective-permute-start(bf16[2,64,4096]{2,1,0:T(8,128)(2,1)S(1)} %pad_maximum_fusion.1), channel_id=1, source_target_pairs={{0,1},{1,0},{2,3},{3,2},{4,5},{5,4},{6,7},{7,6},{8,9},{9,8},{10,11... | collective-permute-start | bytes 3145736 | tf_op jit(solution)/shard_map/ppermute | solution.py:302
  211.5 11.4 %collective-permute-start.58 = (bf16[16,64,128]{2,1,0:T(8,128)(2,1)S(1)}, bf16[16,64,128]{2,1,0:T(8,128)(2,1)S(1)}, u32[]{:S(2)}, u32[]{:S(2)}) collective-permute-start(bf16[16,64,128]{2,1,0:T(8,128)(2,1)S(1)} %get-tuple-element.60), channel_id=1, source_target_pairs={{0,8},{8,16},{16,24},{24,28},{28,20},{20,12},{12,4},{4,0},{1,9},{9... | collective-permute-start | bytes 786440 | tf_op jit(solution)/shard_map/ppermute | solution.py:338
  212.5 10.7 %collective-permute-start.64 = (bf16[16,64,128]{2,1,0:T(8,128)(2,1)S(1)}, bf16[16,64,128]{2,1,0:T(8,128)(2,1)S(1)}, u32[]{:S(2)}, u32[]{:S(2)}) collective-permute-start(bf16[16,64,128]{2,1,0:T(8,128)(2,1)S(1)} %get-tuple-element.61), channel_id=1, source_target_pairs={{8,0},{16,8},{24,16},{28,24},{20,28},{12,20},{4,12},{0,4},{9,1},{1... | collective-permute-start | bytes 786440 | tf_op jit(solution)/shard_map/ppermute | solution.py:338
  217.7 10.7 %collective-permute-start.45 = (bf16[16,64,128]{2,1,0:T(8,128)(2,1)S(1)}, bf16[16,64,128]{2,1,0:T(8,128)(2,1)S(1)}, u32[]{:S(2)}, u32[]{:S(2)}) collective-permute-start(bf16[16,64,128]{2,1,0:T(8,128)(2,1)S(1)} %get-tuple-element.76), channel_id=1, source_target_pairs={{0,8},{8,16},{16,24},{24,28},{28,20},{20,12},{12,4},{4,0},{1,9},{9... | collective-permute-start | bytes 786440 | tf_op jit(solution)/shard_map/ppermute | solution.py:338
  223.4 10.7 %collective-permute-start.59 = (bf16[16,64,128]{2,1,0:T(8,128)(2,1)S(1)}, bf16[16,64,128]{2,1,0:T(8,128)(2,1)S(1)}, u32[]{:S(2)}, u32[]{:S(2)}) collective-permute-start(bf16[16,64,128]{2,1,0:T(8,128)(2,1)S(1)} %get-tuple-element.58), channel_id=1, source_target_pairs={{0,8},{8,16},{16,24},{24,28},{28,20},{20,12},{12,4},{4,0},{1,9},{9... | collective-permute-start | bytes 786440 | tf_op jit(solution)/shard_map/ppermute | solution.py:338
  229.0 10.7 %collective-permute-start.46 = (bf16[16,64,128]{2,1,0:T(8,128)(2,1)S(1)}, bf16[16,64,128]{2,1,0:T(8,128)(2,1)S(1)}, u32[]{:S(2)}, u32[]{:S(2)}) collective-permute-start(bf16[16,64,128]{2,1,0:T(8,128)(2,1)S(1)} %get-tuple-element.74), channel_id=1, source_target_pairs={{0,8},{8,16},{16,24},{24,28},{28,20},{20,12},{12,4},{4,0},{1,9},{9... | collective-permute-start | bytes 786440 | tf_op jit(solution)/shard_map/ppermute | solution.py:338
  234.6 10.7 %collective-permute-start.60 = (bf16[16,64,128]{2,1,0:T(8,128)(2,1)S(1)}, bf16[16,64,128]{2,1,0:T(8,128)(2,1)S(1)}, u32[]{:S(2)}, u32[]{:S(2)}) collective-permute-start(bf16[16,64,128]{2,1,0:T(8,128)(2,1)S(1)} %get-tuple-element.56), channel_id=1, source_target_pairs={{0,8},{8,16},{16,24},{24,28},{28,20},{20,12},{12,4},{4,0},{1,9},{9... | collective-permute-start | bytes 786440 | tf_op jit(solution)/shard_map/ppermute | solution.py:338
  237.0 14.9 %collective-permute-start.42 = (bf16[2,32,4096]{2,1,0:T(8,128)(2,1)S(1)}, bf16[2,32,4096]{2,1,0:T(8,128)(2,1)S(1)}, u32[]{:S(2)}, u32[]{:S(2)}) collective-permute-start(bf16[2,32,4096]{2,1,0:T(8,128)(2,1)S(1)} %slice.243), channel_id=1, source_target_pairs={{0,2},{1,3},{2,0},{3,1},{4,6},{5,7},{6,4},{7,5},{8,10},{9,11},{10,... | collective-permute-start | bytes 1572872 | tf_op jit(solution)/shard_map/ppermute | solution.py:302
  (39 other events, 500.7 us)
